TPU v7x, 32 devices: a whole 2x2x4 slice. The times are simulated.
32 devices in a mesh: dp: 4 (over y, x), context: 4 (over z), tensor: 2 (over core).
Axes of the slice: x: 2, y: 2, z: 4, core: 2. Of those that a mesh axis runs over, the one named last changes fastest.
Arguments:
- tokens: bfloat16 [8, 1024, 2048], P('dp', 'context'), may hold values from -6 to 6
- lengths: int32 [8], P('dp'), may hold values from 256 to 1024, as said below
- w_query: bfloat16 [2048, 2048], P(('dp', 'context'), 'tensor'), may hold values from -0.125 to 0.125
- w_key: bfloat16 [2048, 2048], P(('dp', 'context'), 'tensor'), may hold values from -0.125 to 0.125
- w_value: bfloat16 [2048, 2048], P(('dp', 'context'), 'tensor'), may hold values from -0.125 to 0.125
- w_out: bfloat16 [2048, 2048], P('tensor', ('dp', 'context')), may hold values from -1 to 1
- w_gate: bfloat16 [2048, 8192], P(('dp', 'context'), 'tensor'), may hold values from -0.125 to 0.125
- w_up: bfloat16 [2048, 8192], P(('dp', 'context'), 'tensor'), may hold values from -0.125 to 0.125
- w_down: bfloat16 [8192, 2048], P('tensor', ('dp', 'context')), may hold values from -0.0625 to 0.0625
- cotangent: bfloat16 [8, 1024, 2048], P('dp', 'context'), may hold values from -6 to 6
Outputs:
- layer_out: bfloat16 [8, 1024, 2048], P('dp', 'context')
- input_grad: float32 [8, 1024, 2048], P('dp', 'context')
- grad_query: float32 [2048, 2048], P(('dp', 'context'), 'tensor')
- grad_key: float32 [2048, 2048], P(('dp', 'context'), 'tensor')
- grad_value: float32 [2048, 2048], P(('dp', 'context'), 'tensor')
- grad_out: float32 [2048, 2048], P('tensor', ('dp', 'context'))
- grad_gate: float32 [2048, 8192], P(('dp', 'context'), 'tensor')
- grad_up: float32 [2048, 8192], P(('dp', 'context'), 'tensor')
- grad_down: float32 [8192, 2048], P('tensor', ('dp', 'context'))
Inputs may be any that keep to these rules, and one draw needn't show every extreme that they name: `lengths`: valid tokens of each slot, counted from its start; in every draw one slot is full and another holds exactly 256.
All inputs are finite; a program needn't handle non-finite values.
Results may differ from a plain program's by a relative error of at most 0.014.
Values may be sent and summed in bfloat16 or wider, within the bound.
A program may use at most 344 MiB of HBM per device.

v0:
```python
import math

import jax
import jax.numpy as jnp
from jax import lax
from jax.sharding import PartitionSpec as P

HEAD_DIM = 128


def rope_tables(positions, head_dim):
    half_dim = head_dim // 2
    inverse_freq = jnp.exp(
        -math.log(10000.0) * jnp.arange(half_dim, dtype=jnp.float32) * 2.0 / head_dim
    )
    angles = positions.astype(jnp.float32)[:, None] * inverse_freq[None, :]
    angles = jnp.concatenate([angles, angles], axis=-1)
    return (jnp.cos(angles)[:, None, :], jnp.sin(angles)[:, None, :])


def rotate(values, cosine, sine):
    half_dim = values.shape[-1] // 2
    turned = jnp.concatenate([-values[..., half_dim:], values[..., :half_dim]], axis=-1)
    return values * cosine + turned * sine


def unrotate(upstream, cosine, sine):
    half_dim = upstream.shape[-1] // 2
    scaled = upstream * sine
    turned = jnp.concatenate([scaled[..., half_dim:], -scaled[..., :half_dim]], axis=-1)
    return upstream * cosine + turned


def normalize(values):
    centered = values - jnp.mean(values, axis=-1, keepdims=True)
    inverse = lax.rsqrt(jnp.mean(centered * centered, axis=-1, keepdims=True) + 1e-05)
    return (centered * inverse, inverse)


def normalize_back(normed, inverse, upstream):
    mean_grad = jnp.mean(upstream, axis=-1, keepdims=True)
    mean_cross = jnp.mean(upstream * normed, axis=-1, keepdims=True)
    return inverse * (upstream - mean_grad - normed * mean_cross)


def split_heads(values, group_count, group_size, head_dim):
    row_count = values.shape[0]
    return jnp.moveaxis(values.reshape(row_count, group_count, group_size, head_dim), 1, 0)


def join_heads(values):
    return jnp.moveaxis(values, 0, 1).reshape(values.shape[1], -1)


def per_device(tokens, lengths, w_query, w_key, w_value, w_out, w_gate, w_up, w_down, cotangent):
    slot_count, local_rows, model_width = tokens.shape
    contexts = lax.axis_size("context")
    seq_total = local_rows * contexts
    head_dim = HEAD_DIM
    local_heads = w_query.shape[1] // head_dim
    group_size = min(local_heads, max(1, 512 // local_rows))
    group_count = local_heads // group_size
    score_scale = 1.0 / math.sqrt(head_dim)
    positions = lax.axis_index("context") * local_rows + jnp.arange(local_rows, dtype=jnp.int32)
    key_positions = jnp.arange(seq_total, dtype=jnp.int32)
    rope_cos, rope_sin = rope_tables(positions, head_dim)
    causal = key_positions[None, :] <= positions[:, None]

    def fetch_weights():
        attention_all = (
            lax.all_gather(w_query, ("dp", "context"), axis=0, tiled=True),
            lax.all_gather(w_key, ("dp", "context"), axis=0, tiled=True),
            lax.all_gather(w_value, ("dp", "context"), axis=0, tiled=True),
            lax.all_gather(w_out, ("dp", "context"), axis=1, tiled=True),
        )
        feedforward_all = (
            lax.all_gather(w_gate, ("dp", "context"), axis=0, tiled=True),
            lax.all_gather(w_up, ("dp", "context"), axis=0, tiled=True),
            lax.all_gather(w_down, ("dp", "context"), axis=1, tiled=True),
        )
        return tuple(attention_all) + tuple(feedforward_all)

    def heads_of(values):
        return split_heads(values, group_count, group_size, head_dim)

    def micro_step(slot_number, loop_state):
        out_buffer, grad_buffer, gradient_sums = loop_state
        weights_all = fetch_weights()
        query_all, key_all, value_all, out_all, gate_all, up_all, down_all = weights_all
        slot_tokens = lax.dynamic_index_in_dim(tokens, slot_number, 0, keepdims=False)
        slot_cotangent = lax.dynamic_index_in_dim(cotangent, slot_number, 0, keepdims=False)
        slot_length = lax.dynamic_index_in_dim(lengths, slot_number, 0, keepdims=False)
        valid_rows = (positions < slot_length).astype(jnp.float32)[:, None]
        allowed = causal & (key_positions < slot_length)[None, :]
        inputs_f = slot_tokens.astype(jnp.float32)
        norm_one, inverse_one = normalize(inputs_f)
        norm_one_low = norm_one.astype(jnp.bfloat16)
        query_raw = jnp.dot(norm_one_low, query_all, preferred_element_type=jnp.float32)
        key_raw = jnp.dot(norm_one_low, key_all, preferred_element_type=jnp.float32)
        value_low = jnp.dot(norm_one_low, value_all, preferred_element_type=jnp.float32).astype(
            jnp.bfloat16
        )
        query_rot = (
            rotate(query_raw.reshape(local_rows, local_heads, head_dim), rope_cos, rope_sin)
            .astype(jnp.bfloat16)
            .reshape(local_rows, -1)
        )
        key_rot = (
            rotate(key_raw.reshape(local_rows, local_heads, head_dim), rope_cos, rope_sin)
            .astype(jnp.bfloat16)
            .reshape(local_rows, -1)
        )
        keys_all, values_all = (
            lax.all_gather(key_rot, "context", axis=0, tiled=True),
            lax.all_gather(value_low, "context", axis=0, tiled=True),
        )
        query_groups = heads_of(query_rot)
        key_groups = heads_of(keys_all)
        value_groups = heads_of(values_all)

        def attend_group(operands):
            query_group, key_group, value_group = operands
            scores = (
                jnp.einsum(
                    "qhd,khd->hqk", query_group, key_group, preferred_element_type=jnp.float32
                )
                * score_scale
            )
            masked = jnp.where(allowed[None], scores, -1e30)
            row_top = jnp.max(masked, axis=-1, keepdims=True)
            exponent = jnp.where(allowed[None], jnp.exp(masked - row_top), 0.0)
            row_total = jnp.sum(exponent, axis=-1, keepdims=True)
            probabilities = (exponent / row_total).astype(jnp.bfloat16)
            attended_group = jnp.einsum(
                "hqk,khd->qhd", probabilities, value_group, preferred_element_type=jnp.float32
            )
            return (attended_group, row_top + jnp.log(row_total))

        attended_groups, log_totals = lax.map(
            attend_group, (query_groups, key_groups, value_groups)
        )
        attended_low = join_heads(attended_groups).astype(jnp.bfloat16)
        branch = lax.psum(
            jnp.dot(attended_low, out_all, preferred_element_type=jnp.float32), "tensor"
        )
        middle = inputs_f + valid_rows * branch
        norm_two, inverse_two = normalize(middle)
        norm_two_low = norm_two.astype(jnp.bfloat16)
        gate_rows = jnp.dot(norm_two_low, gate_all, preferred_element_type=jnp.float32)
        upper_rows = jnp.dot(norm_two_low, up_all, preferred_element_type=jnp.float32)
        sigmoid_gate = jax.nn.sigmoid(gate_rows)
        silu_gate = gate_rows * sigmoid_gate
        hidden = (silu_gate * upper_rows).astype(jnp.bfloat16)
        feedforward = lax.psum(
            jnp.dot(hidden, down_all, preferred_element_type=jnp.float32).astype(jnp.bfloat16),
            "tensor",
        ).astype(jnp.float32)
        layer_rows = (middle + valid_rows * feedforward).astype(jnp.bfloat16)
        out_grad = slot_cotangent.astype(jnp.float32) * valid_rows
        feedforward_grad = (valid_rows * out_grad).astype(jnp.bfloat16)
        grad_down = jnp.einsum(
            "tf,td->fd", hidden, feedforward_grad, preferred_element_type=jnp.float32
        )
        hidden_grad = jnp.einsum(
            "td,fd->tf", feedforward_grad, down_all, preferred_element_type=jnp.float32
        )
        gate_grad = (
            hidden_grad * upper_rows * sigmoid_gate * (1.0 + gate_rows * (1.0 - sigmoid_gate))
        ).astype(jnp.bfloat16)
        upper_grad = (hidden_grad * silu_gate).astype(jnp.bfloat16)
        grad_gate = jnp.einsum(
            "td,tf->df", norm_two_low, gate_grad, preferred_element_type=jnp.float32
        )
        grad_up = jnp.einsum(
            "td,tf->df", norm_two_low, upper_grad, preferred_element_type=jnp.float32
        )
        norm_two_part = jnp.einsum(
            "tf,df->td", gate_grad, gate_all, preferred_element_type=jnp.float32
        )
        norm_two_part = norm_two_part + jnp.einsum(
            "tf,df->td", upper_grad, up_all, preferred_element_type=jnp.float32
        )
        norm_two_grad = lax.psum(norm_two_part, "tensor")
        middle_grad = out_grad + normalize_back(norm_two, inverse_two, norm_two_grad)
        branch_grad = (valid_rows * middle_grad).astype(jnp.bfloat16)
        grad_out = jnp.einsum(
            "tc,td->cd", attended_low, branch_grad, preferred_element_type=jnp.float32
        )
        attended_grad = jnp.einsum(
            "td,cd->tc", branch_grad, out_all, preferred_element_type=jnp.float32
        ).astype(jnp.bfloat16)
        attended_grad_groups = heads_of(attended_grad)

        def attend_back(operands):
            query_group, key_group, value_group, attended_group_grad, log_total = operands
            scores = (
                jnp.einsum(
                    "qhd,khd->hqk", query_group, key_group, preferred_element_type=jnp.float32
                )
                * score_scale
            )
            probabilities = jnp.where(allowed[None], jnp.exp(scores - log_total), 0.0)
            prob_grad = jnp.einsum(
                "qhd,khd->hqk", attended_group_grad, value_group, preferred_element_type=jnp.float32
            )
            row_delta = jnp.sum(probabilities * prob_grad, axis=-1, keepdims=True)
            score_grad = (probabilities * (prob_grad - row_delta)).astype(jnp.bfloat16)
            query_grad = (
                jnp.einsum(
                    "hqk,khd->qhd", score_grad, key_group, preferred_element_type=jnp.float32
                )
                * score_scale
            )
            key_grad = (
                jnp.einsum(
                    "hqk,qhd->khd", score_grad, query_group, preferred_element_type=jnp.float32
                )
                * score_scale
            )
            value_grad = jnp.einsum(
                "hqk,qhd->khd",
                probabilities.astype(jnp.bfloat16),
                attended_group_grad,
                preferred_element_type=jnp.float32,
            )
            return (query_grad, key_grad, value_grad)

        query_grads, key_grads, value_grads = lax.map(
            attend_back, (query_groups, key_groups, value_groups, attended_grad_groups, log_totals)
        )
        key_sum, value_sum = (
            lax.psum_scatter(join_heads(key_grads), "context", scatter_dimension=0, tiled=True),
            lax.psum_scatter(join_heads(value_grads), "context", scatter_dimension=0, tiled=True),
        )
        query_low = (
            unrotate(
                join_heads(query_grads).reshape(local_rows, local_heads, head_dim),
                rope_cos,
                rope_sin,
            )
            .astype(jnp.bfloat16)
            .reshape(local_rows, -1)
        )
        key_low = (
            unrotate(key_sum.reshape(local_rows, local_heads, head_dim), rope_cos, rope_sin)
            .astype(jnp.bfloat16)
            .reshape(local_rows, -1)
        )
        value_grad_low = value_sum.astype(jnp.bfloat16)
        grad_query = jnp.einsum(
            "td,tc->dc", norm_one_low, query_low, preferred_element_type=jnp.float32
        )
        grad_key = jnp.einsum(
            "td,tc->dc", norm_one_low, key_low, preferred_element_type=jnp.float32
        )
        grad_value = jnp.einsum(
            "td,tc->dc", norm_one_low, value_grad_low, preferred_element_type=jnp.float32
        )
        norm_one_part = jnp.einsum(
            "tc,dc->td", query_low, query_all, preferred_element_type=jnp.float32
        )
        norm_one_part = norm_one_part + jnp.einsum(
            "tc,dc->td", key_low, key_all, preferred_element_type=jnp.float32
        )
        norm_one_part = norm_one_part + jnp.einsum(
            "tc,dc->td", value_grad_low, value_all, preferred_element_type=jnp.float32
        )
        norm_one_grad = lax.psum(norm_one_part.astype(jnp.bfloat16), "tensor").astype(jnp.float32)
        input_rows = middle_grad + normalize_back(norm_one, inverse_one, norm_one_grad)
        gradient_terms = (grad_query, grad_key, grad_value, grad_out, grad_gate, grad_up, grad_down)
        gradient_sums = jax.tree.map(jnp.add, gradient_sums, gradient_terms)
        out_buffer = lax.dynamic_update_index_in_dim(out_buffer, layer_rows, slot_number, 0)
        grad_buffer = lax.dynamic_update_index_in_dim(grad_buffer, input_rows, slot_number, 0)
        return (out_buffer, grad_buffer, gradient_sums)

    starting_sums = (
        jnp.zeros((model_width, w_query.shape[1]), jnp.float32),
        jnp.zeros((model_width, w_key.shape[1]), jnp.float32),
        jnp.zeros((model_width, w_value.shape[1]), jnp.float32),
        jnp.zeros((w_out.shape[0], model_width), jnp.float32),
        jnp.zeros((model_width, w_gate.shape[1]), jnp.float32),
        jnp.zeros((model_width, w_up.shape[1]), jnp.float32),
        jnp.zeros((w_down.shape[0], model_width), jnp.float32),
    )
    out_start = jnp.zeros(tokens.shape, jnp.bfloat16)
    grad_start = jnp.zeros(tokens.shape, jnp.float32)
    out_buffer, grad_buffer, gradient_sums = lax.fori_loop(
        0, slot_count, micro_step, (out_start, grad_start, starting_sums)
    )
    attention_part = (
        lax.psum_scatter(gradient_sums[0], ("dp", "context"), scatter_dimension=0, tiled=True),
        lax.psum_scatter(gradient_sums[1], ("dp", "context"), scatter_dimension=0, tiled=True),
        lax.psum_scatter(gradient_sums[2], ("dp", "context"), scatter_dimension=0, tiled=True),
        lax.psum_scatter(gradient_sums[3], ("dp", "context"), scatter_dimension=1, tiled=True),
    )
    feedforward_part = (
        lax.psum_scatter(gradient_sums[4], ("dp", "context"), scatter_dimension=0, tiled=True),
        lax.psum_scatter(gradient_sums[5], ("dp", "context"), scatter_dimension=0, tiled=True),
        lax.psum_scatter(gradient_sums[6], ("dp", "context"), scatter_dimension=1, tiled=True),
    )
    shards = tuple(attention_part) + tuple(feedforward_part)
    return (
        out_buffer,
        grad_buffer,
        shards[0],
        shards[1],
        shards[2],
        shards[3],
        shards[4],
        shards[5],
        shards[6],
    )


def solution(mesh):
    return jax.shard_map(
        per_device,
        mesh=mesh,
        in_specs=(
            P("dp", "context", None),
            P("dp"),
            P(("dp", "context"), "tensor"),
            P(("dp", "context"), "tensor"),
            P(("dp", "context"), "tensor"),
            P("tensor", ("dp", "context")),
            P(("dp", "context"), "tensor"),
            P(("dp", "context"), "tensor"),
            P("tensor", ("dp", "context")),
            P("dp", "context", None),
        ),
        out_specs=(
            P("dp", "context", None),
            P("dp", "context", None),
            P(("dp", "context"), "tensor"),
            P(("dp", "context"), "tensor"),
            P(("dp", "context"), "tensor"),
            P("tensor", ("dp", "context")),
            P(("dp", "context"), "tensor"),
            P(("dp", "context"), "tensor"),
            P("tensor", ("dp", "context")),
        ),
        check_vma=False,
    )
```

profile of v0, /device:TPU:0, one launch (start us, length us, event | category | flops | bytes accessed | tf_op | source)
XLA Modules:
  0.0 5626.6 jit_solution(7153314499458581981)
XLA Ops:
  10.9 2800.1 %while.101 = (s32[]{:T(128)}, bf16[2,256,2048]{2,1,0:T(8,128)(2,1)}, f32[2,256,2048]{2,1,0:T(8,128)}, f32[2048,1024]{1,0:T(8,128)}, f32[2048,1024]{1,0:T(8,128)}...) while((s32[]{:T(128)}, bf16[2,256,2048]{2,1,0:T(8,128)(2,1)}, ...), condition=%wide.region_22.23_spmd.clone.clone, body=%wide.region_0.22_spmd.clone.sunk.clone | while | flops 52632551424 | bytes 1081730560 | solution.py:287
  16.7 90.1 %all-gather.14.cloned.1.call-done = bf16[2048,1024]{0,1:T(8,128)(2,1)} async-done(((bf16[128,1024]{0,1:T(8,128)(2,1)}), bf16[2048,1024]{0,1:T(8,128)(2,1)}) %all-gather.14.cloned.1.call-update) | async-done | bytes 4194320 | tf_op jit(solution)/shard_map/while/body/eval_jaxpr/all_gather | solution.py:72
  111.5 85.0 %all-gather.16.cloned.1.call-done = bf16[2048,1024]{0,1:T(8,128)(2,1)} async-done(((bf16[128,1024]{0,1:T(8,128)(2,1)}), bf16[2048,1024]{0,1:T(8,128)(2,1)}) %all-gather.16.cloned.1.call-update) | async-done | bytes 4194320 | tf_op jit(solution)/shard_map/while/body/eval_jaxpr/all_gather | solution.py:71
  202.7 70.3 %all-gather.10.cloned.1.call-done = bf16[2048,1024]{1,0:T(8,128)(2,1)} async-done(((bf16[128,1024]{1,0:T(8,128)(2,1)}), bf16[2048,1024]{1,0:T(8,128)(2,1)}) %all-gather.10.cloned.1.call-update) | async-done | bytes 4194320 | tf_op jit(solution)/shard_map/while/body/eval_jaxpr/all_gather | solution.py:73
  280.9 39.0 all-gather.18.cloned.1.call-done
  322.9 42.8 all-gather.12.cloned.1.call-done
  390.0 65.8 %all-gather.20.cloned.1.call-done = bf16[1024,2048]{1,0:T(8,128)(2,1)} async-done(((bf16[1024,128]{1,0:T(8,128)(2,1)}), bf16[1024,2048]{1,0:T(8,128)(2,1)}) %all-gather.20.cloned.1.call-update) | async-done | bytes 4194320 | tf_op jit(solution)/shard_map/while/body/eval_jaxpr/all_gather | solution.py:74
  484.2 191.0 %all-gather.24.cloned.1.call-done = bf16[2048,4096]{1,0:T(8,128)(2,1)} async-done(((bf16[128,4096]{1,0:T(8,128)(2,1)}), bf16[2048,4096]{1,0:T(8,128)(2,1)}) %all-gather.24.cloned.1.call-update) | async-done | bytes 16777232 | tf_op jit(solution)/shard_map/while/body/eval_jaxpr/all_gather | solution.py:78
  687.9 179.4 %all-gather.22.cloned.1.call-done = bf16[2048,4096]{1,0:T(8,128)(2,1)} async-done(((bf16[128,4096]{1,0:T(8,128)(2,1)}), bf16[2048,4096]{1,0:T(8,128)(2,1)}) %all-gather.22.cloned.1.call-update) | async-done | bytes 16777232 | tf_op jit(solution)/shard_map/while/body/eval_jaxpr/all_gather | solution.py:77
  879.9 237.2 %all-gather.26.cloned.1.call-done = bf16[4096,2048]{1,0:T(8,128)(2,1)} async-done(((bf16[4096,128]{1,0:T(8,128)(2,1)}), bf16[4096,2048]{1,0:T(8,128)(2,1)}) %all-gather.26.cloned.1.call-update) | async-done | bytes 16777232 | tf_op jit(solution)/shard_map/while/body/eval_jaxpr/all_gather | solution.py:79
  1184.8 27.6 while.100
  1301.1 69.0 %reduce-scatter.26.cloned.1.call-done = f32[256,1024]{0,1:T(8,128)} async-done(((f32[1024,1024]{0,1:T(8,128)}), f32[256,1024]{0,1:T(8,128)}) %reduce-scatter.26.cloned.1.call-update) | async-done | bytes 1048592 | tf_op jit(solution)/shard_map/while/body/eval_jaxpr/reduce_scatter | solution.py:233
  1410.2 88.7 %all-gather.14.cloned.1.call-done = bf16[2048,1024]{0,1:T(8,128)(2,1)} async-done(((bf16[128,1024]{0,1:T(8,128)(2,1)}), bf16[2048,1024]{0,1:T(8,128)(2,1)}) %all-gather.14.cloned.1.call-update) | async-done | bytes 4194320 | tf_op jit(solution)/shard_map/while/body/eval_jaxpr/all_gather | solution.py:72
  1503.5 84.8 %all-gather.16.cloned.1.call-done = bf16[2048,1024]{0,1:T(8,128)(2,1)} async-done(((bf16[128,1024]{0,1:T(8,128)(2,1)}), bf16[2048,1024]{0,1:T(8,128)(2,1)}) %all-gather.16.cloned.1.call-update) | async-done | bytes 4194320 | tf_op jit(solution)/shard_map/while/body/eval_jaxpr/all_gather | solution.py:71
  1594.5 70.2 %all-gather.10.cloned.1.call-done = bf16[2048,1024]{1,0:T(8,128)(2,1)} async-done(((bf16[128,1024]{1,0:T(8,128)(2,1)}), bf16[2048,1024]{1,0:T(8,128)(2,1)}) %all-gather.10.cloned.1.call-update) | async-done | bytes 4194320 | tf_op jit(solution)/shard_map/while/body/eval_jaxpr/all_gather | solution.py:73
  1672.6 39.0 all-gather.18.cloned.1.call-done
  1714.6 43.0 all-gather.12.cloned.1.call-done
  1781.9 65.8 %all-gather.20.cloned.1.call-done = bf16[1024,2048]{1,0:T(8,128)(2,1)} async-done(((bf16[1024,128]{1,0:T(8,128)(2,1)}), bf16[1024,2048]{1,0:T(8,128)(2,1)}) %all-gather.20.cloned.1.call-update) | async-done | bytes 4194320 | tf_op jit(solution)/shard_map/while/body/eval_jaxpr/all_gather | solution.py:74
  1876.1 191.0 %all-gather.24.cloned.1.call-done = bf16[2048,4096]{1,0:T(8,128)(2,1)} async-done(((bf16[128,4096]{1,0:T(8,128)(2,1)}), bf16[2048,4096]{1,0:T(8,128)(2,1)}) %all-gather.24.cloned.1.call-update) | async-done | bytes 16777232 | tf_op jit(solution)/shard_map/while/body/eval_jaxpr/all_gather | solution.py:78
  2079.7 179.4 %all-gather.22.cloned.1.call-done = bf16[2048,4096]{1,0:T(8,128)(2,1)} async-done(((bf16[128,4096]{1,0:T(8,128)(2,1)}), bf16[2048,4096]{1,0:T(8,128)(2,1)}) %all-gather.22.cloned.1.call-update) | async-done | bytes 16777232 | tf_op jit(solution)/shard_map/while/body/eval_jaxpr/all_gather | solution.py:77
  2271.7 237.3 %all-gather.26.cloned.1.call-done = bf16[4096,2048]{1,0:T(8,128)(2,1)} async-done(((bf16[4096,128]{1,0:T(8,128)(2,1)}), bf16[4096,2048]{1,0:T(8,128)(2,1)}) %all-gather.26.cloned.1.call-update) | async-done | bytes 16777232 | tf_op jit(solution)/shard_map/while/body/eval_jaxpr/all_gather | solution.py:79
  2576.7 27.6 while.100
  2604.3 25.8 select_add_fusion.27
  2665.2 25.6 select_add_fusion.25
  2701.7 60.1 %reduce-scatter.26.cloned.1.call-done = f32[256,1024]{0,1:T(8,128)} async-done(((f32[1024,1024]{0,1:T(8,128)}), f32[256,1024]{0,1:T(8,128)}) %reduce-scatter.26.cloned.1.call-update) | async-done | bytes 1048592 | tf_op jit(solution)/shard_map/while/body/eval_jaxpr/reduce_scatter | solution.py:233
  2815.6 180.1 %reduce-scatter.10.cloned.1.call-done = f32[128,1024]{1,0:T(8,128)} async-done(((f32[2048,1024]{1,0:T(8,128)}), f32[128,1024]{1,0:T(8,128)}) %reduce-scatter.10.cloned.1.call-update) | async-done | bytes 524304 | tf_op jit(solution)/shard_map/reduce_scatter | solution.py:291
  2995.7 182.6 %reduce-scatter.12.cloned.1.call-done = f32[128,1024]{1,0:T(8,128)} async-done(((f32[2048,1024]{1,0:T(8,128)}), f32[128,1024]{1,0:T(8,128)}) %reduce-scatter.12.cloned.1.call-update) | async-done | bytes 524304 | tf_op jit(solution)/shard_map/reduce_scatter | solution.py:292
  3178.2 182.6 %reduce-scatter.14.cloned.1.call-done = f32[128,1024]{1,0:T(8,128)} async-done(((f32[2048,1024]{1,0:T(8,128)}), f32[128,1024]{1,0:T(8,128)}) %reduce-scatter.14.cloned.1.call-update) | async-done | bytes 524304 | tf_op jit(solution)/shard_map/reduce_scatter | solution.py:293
  3360.8 182.7 %reduce-scatter.16.cloned.1.call-done = f32[1024,128]{1,0:T(8,128)} async-done(((f32[1024,2048]{1,0:T(8,128)}), f32[1024,128]{1,0:T(8,128)}) %reduce-scatter.16.cloned.1.call-update) | async-done | bytes 524304 | tf_op jit(solution)/shard_map/reduce_scatter | solution.py:294
  3543.5 692.4 %reduce-scatter.22.cloned.1.call-done = f32[4096,128]{1,0:T(8,128)} async-done(((f32[4096,2048]{1,0:T(8,128)}), f32[4096,128]{1,0:T(8,128)}) %reduce-scatter.22.cloned.1.call-update) | async-done | bytes 2097168 | tf_op jit(solution)/shard_map/reduce_scatter | solution.py:299
  4235.9 691.6 %reduce-scatter.18.cloned.1.call-done = f32[128,4096]{1,0:T(8,128)} async-done(((f32[2048,4096]{1,0:T(8,128)}), f32[128,4096]{1,0:T(8,128)}) %reduce-scatter.18.cloned.1.call-update) | async-done | bytes 2097168 | tf_op jit(solution)/shard_map/reduce_scatter | solution.py:297
  4927.5 691.4 %reduce-scatter.20.cloned.1.call-done = f32[128,4096]{1,0:T(8,128)} async-done(((f32[2048,4096]{1,0:T(8,128)}), f32[128,4096]{1,0:T(8,128)}) %reduce-scatter.20.cloned.1.call-update) | async-done | bytes 2097168 | tf_op jit(solution)/shard_map/reduce_scatter | solution.py:298
  (487 shorter events, 650.6 us)
Async XLA Ops:
  12.0 184.4 %all-gather.16.cloned.1.call-start = ((), (), s32[]{:S(2)}) async-start(), calls=%async_computation.19 | async-start | bytes 4456448 | tf_op jit(solution)/shard_map/while/body/eval_jaxpr/all_gather | solution.py:71
  12.8 260.2 %all-gather.10.cloned.1.call-start = ((), (), s32[]{:S(2)}) async-start(), calls=%async_computation.16 | async-start | bytes 4456448 | tf_op jit(solution)/shard_map/while/body/eval_jaxpr/all_gather | solution.py:73
  13.5 306.4 %all-gather.18.cloned.1.call-start = ((), (), s32[]{:S(2)}) async-start(), calls=%async_computation.20 | async-start | bytes 2621440 | tf_op jit(solution)/shard_map/while/body/eval_jaxpr/all_gather | solution.py:114
  202.6 163.1 %all-gather.12.cloned.1.call-start = ((), (), s32[]{:S(2)}) async-start(), calls=%async_computation.17 | async-start | bytes 2621440 | tf_op jit(solution)/shard_map/while/body/eval_jaxpr/all_gather | solution.py:115
  277.3 178.6 %all-gather.20.cloned.1.call-start = ((), (), s32[]{:S(2)}) async-start(), calls=%async_computation.21 | async-start | bytes 4456448 | tf_op jit(solution)/shard_map/while/body/eval_jaxpr/all_gather | solution.py:74
  277.9 202.4 %all-reduce.8.cloned.1.call-start = ((), (), s32[]{:S(2)}) async-start(), calls=%async_computation.22 | async-start | bytes 4194304 | tf_op jit(solution)/shard_map/while/body/eval_jaxpr/psum | solution.py:143
  460.7 214.6 %all-gather.24.cloned.1.call-start = ((), (), s32[]{:S(2)}) async-start(), calls=%async_computation.24 | async-start | bytes 17825792 | tf_op jit(solution)/shard_map/while/body/eval_jaxpr/all_gather | solution.py:78
  461.4 405.8 %all-gather.22.cloned.1.call-start = ((), (), s32[]{:S(2)}) async-start(), calls=%async_computation.23 | async-start | bytes 17825792 | tf_op jit(solution)/shard_map/while/body/eval_jaxpr/all_gather | solution.py:77
  462.2 655.0 %all-gather.26.cloned.1.call-start = ((), (), s32[]{:S(2)}) async-start(), calls=%async_computation.25 | async-start | bytes 17825792 | tf_op jit(solution)/shard_map/while/body/eval_jaxpr/all_gather | solution.py:79
  462.7 712.7 %all-reduce.10.cloned.1.call-start = ((), (), s32[]{:S(2)}) async-start(), calls=%async_computation.26 | async-start | bytes 4194304 | tf_op jit(solution)/shard_map/while/body/eval_jaxpr/psum | solution.py:183
  1212.4 157.8 %reduce-scatter.26.cloned.1.call-start = ((), (), s32[]{:S(2)}) async-start(), calls=%async_computation.28 | async-start | bytes 5242880 | tf_op jit(solution)/shard_map/while/body/eval_jaxpr/reduce_scatter | solution.py:233
  1227.2 170.5 %all-reduce.12.cloned.1.call-start = ((), (), s32[]{:S(2)}) async-start(), calls=%async_computation.29 | async-start | bytes 4194304 | tf_op jit(solution)/shard_map/while/body/eval_jaxpr/psum | solution.py:154
  1405.8 182.5 %all-gather.16.cloned.1.call-start = ((), (), s32[]{:S(2)}) async-start(), calls=%async_computation.19 | async-start | bytes 4456448 | tf_op jit(solution)/shard_map/while/body/eval_jaxpr/all_gather | solution.py:71
  1406.4 258.3 %all-gather.10.cloned.1.call-start = ((), (), s32[]{:S(2)}) async-start(), calls=%async_computation.16 | async-start | bytes 4456448 | tf_op jit(solution)/shard_map/while/body/eval_jaxpr/all_gather | solution.py:73
  1407.0 304.6 %all-gather.18.cloned.1.call-start = ((), (), s32[]{:S(2)}) async-start(), calls=%async_computation.20 | async-start | bytes 2621440 | tf_op jit(solution)/shard_map/while/body/eval_jaxpr/all_gather | solution.py:114
  1594.5 163.1 %all-gather.12.cloned.1.call-start = ((), (), s32[]{:S(2)}) async-start(), calls=%async_computation.17 | async-start | bytes 2621440 | tf_op jit(solution)/shard_map/while/body/eval_jaxpr/all_gather | solution.py:115
  1669.0 178.7 %all-gather.20.cloned.1.call-start = ((), (), s32[]{:S(2)}) async-start(), calls=%async_computation.21 | async-start | bytes 4456448 | tf_op jit(solution)/shard_map/while/body/eval_jaxpr/all_gather | solution.py:74
  1669.6 202.6 %all-reduce.8.cloned.1.call-start = ((), (), s32[]{:S(2)}) async-start(), calls=%async_computation.22 | async-start | bytes 4194304 | tf_op jit(solution)/shard_map/while/body/eval_jaxpr/psum | solution.py:143
  1852.5 214.6 %all-gather.24.cloned.1.call-start = ((), (), s32[]{:S(2)}) async-start(), calls=%async_computation.24 | async-start | bytes 17825792 | tf_op jit(solution)/shard_map/while/body/eval_jaxpr/all_gather | solution.py:78
  1853.3 405.8 %all-gather.22.cloned.1.call-start = ((), (), s32[]{:S(2)}) async-start(), calls=%async_computation.23 | async-start | bytes 17825792 | tf_op jit(solution)/shard_map/while/body/eval_jaxpr/all_gather | solution.py:77
  1854.0 655.0 %all-gather.26.cloned.1.call-start = ((), (), s32[]{:S(2)}) async-start(), calls=%async_computation.25 | async-start | bytes 17825792 | tf_op jit(solution)/shard_map/while/body/eval_jaxpr/all_gather | solution.py:79
  1854.6 712.7 %all-reduce.10.cloned.1.call-start = ((), (), s32[]{:S(2)}) async-start(), calls=%async_computation.26 | async-start | bytes 4194304 | tf_op jit(solution)/shard_map/while/body/eval_jaxpr/psum | solution.py:183
  2547.7 143.2 %reduce-scatter.24.cloned.1.call-start = ((), (), s32[]{:S(2)}) async-start(), calls=%async_computation.27 | async-start | bytes 5242880 | tf_op jit(solution)/shard_map/while/body/eval_jaxpr/reduce_scatter | solution.py:232
  2604.3 157.6 %reduce-scatter.26.cloned.1.call-start = ((), (), s32[]{:S(2)}) async-start(), calls=%async_computation.28 | async-start | bytes 5242880 | tf_op jit(solution)/shard_map/while/body/eval_jaxpr/reduce_scatter | solution.py:233
  2630.2 172.3 %all-reduce.12.cloned.1.call-start = ((), (), s32[]{:S(2)}) async-start(), calls=%async_computation.29 | async-start | bytes 4194304 | tf_op jit(solution)/shard_map/while/body/eval_jaxpr/psum | solution.py:154
  2811.0 184.7 %reduce-scatter.10.cloned.1.call-start = ((), (), s32[]{:S(2)}) async-start(), calls=%async_computation.9 | async-start | bytes 8912896 | tf_op jit(solution)/shard_map/reduce_scatter | solution.py:291
  2811.6 366.6 %reduce-scatter.12.cloned.1.call-start = ((), (), s32[]{:S(2)}) async-start(), calls=%async_computation.10 | async-start | bytes 8912896 | tf_op jit(solution)/shard_map/reduce_scatter | solution.py:292
  2812.2 548.6 %reduce-scatter.14.cloned.1.call-start = ((), (), s32[]{:S(2)}) async-start(), calls=%async_computation.11 | async-start | bytes 8912896 | tf_op jit(solution)/shard_map/reduce_scatter | solution.py:293
  2812.8 730.8 %reduce-scatter.16.cloned.1.call-start = ((), (), s32[]{:S(2)}) async-start(), calls=%async_computation.12 | async-start | bytes 8912896 | tf_op jit(solution)/shard_map/reduce_scatter | solution.py:294
  2813.5 1422.4 %reduce-scatter.22.cloned.1.call-start = ((), (), s32[]{:S(2)}) async-start(), calls=%async_computation.15 | async-start | bytes 35651584 | tf_op jit(solution)/shard_map/reduce_scatter | solution.py:299
  2814.3 2113.2 %reduce-scatter.18.cloned.1.call-start = ((), (), s32[]{:S(2)}) async-start(), calls=%async_computation.13 | async-start | bytes 35651584 | tf_op jit(solution)/shard_map/reduce_scatter | solution.py:297
  2815.0 2803.9 %reduce-scatter.20.cloned.1.call-start = ((), (), s32[]{:S(2)}) async-start(), calls=%async_computation.14 | async-start | bytes 35651584 | tf_op jit(solution)/shard_map/reduce_scatter | solution.py:298
  (93 other events, 3666.1 us)
Sparse Core Ops, SparseCore 0:
  15.3 91.4 all-gather.13
  109.5 86.8 all-gather.15
  199.2 73.7 all-gather.9
  275.0 44.8 all-gather.17
  321.9 43.8 all-gather.11
  368.3 87.5 all-gather.19
  460.8 19.4 all-reduce.7
  483.0 192.1 all-gather.23
  678.0 189.1 all-gather.21
  869.8 247.2 all-gather.25
  1155.9 19.4 all-reduce.9
  1212.5 77.9 reduce-scatter.23
  1292.8 77.2 reduce-scatter.25
  1375.8 21.8 all-reduce.11
  1408.9 89.8 all-gather.13
  1501.4 86.8 all-gather.15
  1590.9 73.7 all-gather.9
  1666.7 44.8 all-gather.17
  1713.7 43.8 all-gather.11
  1760.1 87.5 all-gather.19
  1852.7 19.4 all-reduce.7
  1874.9 192.1 all-gather.23
  2069.9 189.1 all-gather.21
  2261.7 247.2 all-gather.25
  2547.8 19.4 all-reduce.9
  2604.4 77.9 reduce-scatter.23
  2684.5 77.2 reduce-scatter.25
  2767.5 21.8 all-reduce.11
Sparse Core Ops, SparseCore 1:
  2814.4 181.3 reduce-scatter.9
  2998.4 179.8 reduce-scatter.11
  3181.0 179.8 reduce-scatter.13
  3363.7 179.8 reduce-scatter.15
  3546.5 689.4 reduce-scatter.21
  4238.9 688.6 reduce-scatter.17
  4930.3 688.6 reduce-scatter.19
where the time goes:
time: 5630 us
  waiting for transfers between devices  5030 us (89%)
  matrix products  449 us (8%)
  local copies, waits for them, and re-layouts  66.2 us (1%)
    reduce_scatter x1, waiting for transfers between devices, per_device(): lax.psum_scatter(gradient_sums[6], ('dp', 'context'), scatter_dimension=1...  692 us
    reduce_scatter x1, waiting for transfers between devices, per_device(): lax.psum_scatter(gradient_sums[4], ('dp', 'context'), scatter_dimension=0...  692 us
    reduce_scatter x1, waiting for transfers between devices, per_device(): lax.psum_scatter(gradient_sums[5], ('dp', 'context'), scatter_dimension=0...  691 us
    all_gather x2, waiting for transfers between devices, fetch_weights(): lax.all_gather(w_down, ('dp', 'context'), axis=1, tiled=True)  475 us
    all_gather x2, waiting for transfers between devices, fetch_weights(): lax.all_gather(w_up, ('dp', 'context'), axis=0, tiled=True)  382 us
    all_gather x2, waiting for transfers between devices, fetch_weights(): lax.all_gather(w_gate, ('dp', 'context'), axis=0, tiled=True)  359 us
    reduce_scatter x1, waiting for transfers between devices, per_device(): lax.psum_scatter(gradient_sums[3], ('dp', 'context'), scatter_dimension=1...  183 us
    reduce_scatter x1, waiting for transfers between devices, per_device(): lax.psum_scatter(gradient_sums[2], ('dp', 'context'), scatter_dimension=0...  183 us
  transfers between devices with their start and end apart: 35, of which 32 were waited for; matrix products, arithmetic and copies ran while one was open for 7% of the time, Pallas kernels for 0%

commit v1 on v0

v1 whole, which is shorter than its diff:
```python
import math

import jax
import jax.numpy as jnp
from jax import lax
from jax.sharding import PartitionSpec as P

HEAD_DIM = 128
ROWS = ("context", "tensor")


def rope_tables(positions, head_dim):
    half_dim = head_dim // 2
    inverse_freq = jnp.exp(
        -math.log(10000.0) * jnp.arange(half_dim, dtype=jnp.float32) * 2.0 / head_dim
    )
    angles = positions.astype(jnp.float32)[:, None] * inverse_freq[None, :]
    angles = jnp.concatenate([angles, angles], axis=-1)
    return (jnp.cos(angles)[:, None, :], jnp.sin(angles)[:, None, :])


def rotate(values, cosine, sine):
    half_dim = values.shape[-1] // 2
    turned = jnp.concatenate([-values[..., half_dim:], values[..., :half_dim]], axis=-1)
    return values * cosine + turned * sine


def unrotate(upstream, cosine, sine):
    half_dim = upstream.shape[-1] // 2
    scaled = upstream * sine
    turned = jnp.concatenate([scaled[..., half_dim:], -scaled[..., :half_dim]], axis=-1)
    return upstream * cosine + turned


def normalize(values):
    centered = values - jnp.mean(values, axis=-1, keepdims=True)
    inverse = lax.rsqrt(jnp.mean(centered * centered, axis=-1, keepdims=True) + 1e-05)
    return (centered * inverse, inverse)


def normalize_back(normed, inverse, upstream):
    mean_grad = jnp.mean(upstream, axis=-1, keepdims=True)
    mean_cross = jnp.mean(upstream * normed, axis=-1, keepdims=True)
    return inverse * (upstream - mean_grad - normed * mean_cross)


def dot(left, right, dims):
    return lax.dot_general(left, right, (dims, ((), ())), preferred_element_type=jnp.float32)


def gather_rows(values):
    return lax.all_gather(values, ROWS, axis=1, tiled=True)


def scatter_rows(values):
    return lax.psum_scatter(values, ROWS, scatter_dimension=1, tiled=True)


def column_weight(weight):
    moved = lax.all_to_all(weight, "context", split_axis=1, concat_axis=0, tiled=True)
    return lax.all_gather(moved, "dp", axis=0, tiled=True)


def row_weight(weight):
    moved = lax.all_to_all(weight, "context", split_axis=0, concat_axis=1, tiled=True)
    return lax.all_gather(moved, "dp", axis=1, tiled=True)


def column_gradient(partial):
    summed = lax.psum_scatter(partial, "dp", scatter_dimension=0, tiled=True)
    return lax.all_to_all(summed, "context", split_axis=0, concat_axis=1, tiled=True)


def row_gradient(partial):
    summed = lax.psum_scatter(partial, "dp", scatter_dimension=1, tiled=True)
    return lax.all_to_all(summed, "context", split_axis=1, concat_axis=0, tiled=True)


def per_device(tokens, lengths, w_query, w_key, w_value, w_out, w_gate, w_up, w_down, cotangent):
    low = jnp.bfloat16
    slots, chip_rows, width = tokens.shape
    contexts, cores = lax.axis_size("context"), lax.axis_size("tensor")
    rows = chip_rows // cores
    seq = chip_rows * contexts
    total = slots * seq
    heads = w_query.shape[1] // contexts // HEAD_DIM
    scale = 1.0 / math.sqrt(HEAD_DIM)
    core = lax.axis_index("tensor")
    own_start = lax.axis_index("context") * chip_rows + core * rows
    own_positions = own_start + jnp.arange(rows, dtype=jnp.int32)
    positions = jnp.arange(seq, dtype=jnp.int32)
    rope_cos, rope_sin = rope_tables(positions, HEAD_DIM)
    allowed = (positions[None, :] <= positions[:, None])[None] & (
        positions[None, None, :] < lengths[:, None, None]
    )
    allowed = allowed[:, None]
    valid_rows = (own_positions[None, :] < lengths[:, None]).astype(jnp.float32)[..., None]

    own_tokens = lax.dynamic_slice_in_dim(tokens, core * rows, rows, 1).astype(jnp.float32)
    own_cotangent = lax.dynamic_slice_in_dim(cotangent, core * rows, rows, 1).astype(jnp.float32)

    norm_one, inverse_one = normalize(own_tokens)
    norm_one_all = gather_rows(norm_one.astype(low)).reshape(total, width)
    query_w, key_w, value_w = (column_weight(w) for w in (w_query, w_key, w_value))
    out_w = row_weight(w_out)
    gate_w, up_w = (column_weight(w) for w in (w_gate, w_up))
    down_w = row_weight(w_down)
    out_grad = own_cotangent * valid_rows
    ffn_grad_all = gather_rows((valid_rows * out_grad).astype(low)).reshape(total, width)

    def split(values):
        return values.reshape(slots, seq, heads, HEAD_DIM)

    query = rotate(split(dot(norm_one_all, query_w, ((1,), (0,)))), rope_cos, rope_sin).astype(low)
    key = rotate(split(dot(norm_one_all, key_w, ((1,), (0,)))), rope_cos, rope_sin).astype(low)
    value = split(dot(norm_one_all, value_w, ((1,), (0,))).astype(low))

    def einsum(form, left, right):
        return jnp.einsum(form, left, right, preferred_element_type=jnp.float32)

    scores = einsum("sqhd,skhd->shqk", query, key) * scale
    masked = jnp.where(allowed, scores, -1e30)
    row_top = jnp.max(masked, axis=-1, keepdims=True)
    exponent = jnp.where(allowed, jnp.exp(masked - row_top), 0.0)
    probabilities = exponent / jnp.sum(exponent, axis=-1, keepdims=True)
    attended = einsum("shqk,skhd->sqhd", probabilities.astype(low), value)
    attended = attended.reshape(total, heads * HEAD_DIM).astype(low)

    branch = dot(attended, out_w, ((1,), (0,))).astype(low).reshape(slots, seq, width)
    branch = scatter_rows(branch).astype(jnp.float32)
    middle = own_tokens + valid_rows * branch
    norm_two, inverse_two = normalize(middle)
    norm_two_all = gather_rows(norm_two.astype(low)).reshape(total, width)

    gate = dot(norm_two_all, gate_w, ((1,), (0,)))
    upper = dot(norm_two_all, up_w, ((1,), (0,)))
    sigmoid = jax.nn.sigmoid(gate)
    silu = gate * sigmoid
    hidden = (silu * upper).astype(low)
    hidden_grad = dot(ffn_grad_all, down_w, ((1,), (1,)))
    gate_grad = (hidden_grad * upper * sigmoid * (1.0 + gate * (1.0 - sigmoid))).astype(low)
    upper_grad = (hidden_grad * silu).astype(low)
    norm_two_part = dot(gate_grad, gate_w, ((1,), (1,))) + dot(upper_grad, up_w, ((1,), (1,)))
    norm_two_grad = scatter_rows(norm_two_part.astype(low).reshape(slots, seq, width)).astype(
        jnp.float32
    )
    middle_grad = out_grad + normalize_back(norm_two, inverse_two, norm_two_grad)
    branch_grad_all = gather_rows((valid_rows * middle_grad).astype(low)).reshape(total, width)

    feedforward = dot(hidden, down_w, ((1,), (0,))).astype(low).reshape(slots, seq, width)
    feedforward = scatter_rows(feedforward).astype(jnp.float32)
    layer_out = (middle + valid_rows * feedforward).astype(low)
    layer_out = lax.all_gather(layer_out, "tensor", axis=1, tiled=True)

    grad_down = row_gradient(dot(hidden, ffn_grad_all, ((0,), (0,))).astype(low))
    grad_gate = column_gradient(dot(norm_two_all, gate_grad, ((0,), (0,))).astype(low))
    grad_up = column_gradient(dot(norm_two_all, upper_grad, ((0,), (0,))).astype(low))

    attended_grad = split(dot(branch_grad_all, out_w, ((1,), (1,))).astype(low))
    grad_out = row_gradient(dot(attended, branch_grad_all, ((0,), (0,))).astype(low))
    prob_grad = einsum("sqhd,skhd->shqk", attended_grad, value)
    row_delta = jnp.sum(probabilities * prob_grad, axis=-1, keepdims=True)
    score_grad = (probabilities * (prob_grad - row_delta)).astype(low)
    query_grad = einsum("shqk,skhd->sqhd", score_grad, key) * scale
    key_grad = einsum("shqk,sqhd->skhd", score_grad, query) * scale
    value_grad = einsum("shqk,sqhd->skhd", probabilities.astype(low), attended_grad)
    query_low = unrotate(query_grad, rope_cos, rope_sin).astype(low).reshape(total, -1)
    key_low = unrotate(key_grad, rope_cos, rope_sin).astype(low).reshape(total, -1)
    value_low = value_grad.astype(low).reshape(total, -1)
    norm_one_part = (
        dot(query_low, query_w, ((1,), (1,)))
        + dot(key_low, key_w, ((1,), (1,)))
        + dot(value_low, value_w, ((1,), (1,)))
    )
    norm_one_grad = scatter_rows(norm_one_part.astype(low).reshape(slots, seq, width)).astype(
        jnp.float32
    )
    input_grad = middle_grad + normalize_back(norm_one, inverse_one, norm_one_grad)
    input_grad = lax.all_gather(input_grad, "tensor", axis=1, tiled=True)
    grad_query = column_gradient(dot(norm_one_all, query_low, ((0,), (0,))).astype(low))
    grad_key = column_gradient(dot(norm_one_all, key_low, ((0,), (0,))).astype(low))
    grad_value = column_gradient(dot(norm_one_all, value_low, ((0,), (0,))).astype(low))
    grads = (grad_query, grad_key, grad_value, grad_out, grad_gate, grad_up, grad_down)
    return (layer_out, input_grad) + tuple(g.astype(jnp.float32) for g in grads)


def solution(mesh):
    tokens = P("dp", "context", None)
    column = P(("dp", "context"), "tensor")
    row = P("tensor", ("dp", "context"))
    weights = (column, column, column, row, column, column, row)
    return jax.shard_map(
        per_device,
        mesh=mesh,
        in_specs=(tokens, P("dp")) + weights + (tokens,),
        out_specs=(tokens, tokens) + weights,
        check_vma=False,
    )
```

time: 5630 us -> 1470 us (0.26)
  waiting for transfers between devices: 5030 us -> 851 us
  blocking collectives: 0 us -> 183 us
  matrix products: 449 us -> 280 us
    reduce_scatter x11, waiting for transfers between devices: 2960 us -> 429 us  [the longest x4 257 us: scatter_rows(): return lax.psum_scatter(values, ROWS, scatter_dimension=1, tiled=True)]
    all_gather x18 -> x13, waiting for transfers between devices: 2000 us -> 408 us  [the longest x4 277 us: gather_rows(): return lax.all_gather(values, ROWS, axis=1, tiled=True)]
    dot_general x98 -> x26, matrix products: 449 us -> 266 us  [the longest x21 231 us: dot(): lax.dot_general(left, right, (dims, ((), ())), preferred_element_type=jnp...]
    all_to_all x0 -> x7, blocking collectives: none -> 183 us  [the longest x5 118 us: column_weight(): lax.all_to_all(weight, 'context', split_axis=1, concat_axis=0, tiled=True)]
    psum x6 -> x0, waiting for transfers between devices: 64.7 us -> none  [the longest x2 32.7 us: micro_step(): lax.psum(jnp.dot(attended_low, out_all, preferred_element_type=jnp.float3...]
  transfers between devices with their start and end apart: 35 -> 31, of which waited for: 32 -> 21; matrix products, arithmetic and copies ran while one was open for 7% -> 21% of each run, Pallas kernels for 0% -> 0%
where the time goes in v1:
time: 1470 us; the launch traced here: 1460 us
  waiting for transfers between devices  851 us (58%)
  matrix products  280 us (19%)
  blocking collectives  183 us (12%)
  other arithmetic  55.2 us (4%)
  local copies, waits for them, and re-layouts  47.5 us (3%)
  starting transfers between devices  31.8 us (2%)
  between operations  15.3 us (1%)
    all_gather x4, waiting for transfers between devices, gather_rows(): return lax.all_gather(values, ROWS, axis=1, tiled=True)  277 us
    reduce_scatter x4, waiting for transfers between devices, scatter_rows(): return lax.psum_scatter(values, ROWS, scatter_dimension=1, tiled=True)  257 us
    dot_general x21, matrix products, dot(): lax.dot_general(left, right, (dims, ((), ())), preferred_element_type=jnp...  231 us
    reduce_scatter x5, waiting for transfers between devices, column_gradient(): summed = lax.psum_scatter(partial, 'dp', scatter_dimension=0, tiled=True)  146 us
    all_to_all x5, blocking collectives, column_weight(): lax.all_to_all(weight, 'context', split_axis=1, concat_axis=0, tiled=True)  118 us
    all_gather x5, waiting for transfers between devices, column_weight(): return lax.all_gather(moved, 'dp', axis=0, tiled=True)  79.4 us
    all_gather x2, waiting for transfers between devices, row_weight(): return lax.all_gather(moved, 'dp', axis=1, tiled=True)  39.9 us
    all_to_all x1, blocking collectives, row_weight(): lax.all_to_all(weight, 'context', split_axis=0, concat_axis=1, tiled=True)  34.6 us
  transfers between devices with their start and end apart: 31, of which 21 were waited for; matrix products, arithmetic and copies ran while one was open for 21% of the time, Pallas kernels for 0%

profile of v1, /device:TPU:0, one launch (start us, length us, event | category | flops | bytes accessed | tf_op | source)
XLA Modules:
  0.0 1463.4 jit_solution(11691576545545180635)
XLA Ops:
  8.5 15.0 %all_to_all.224 = bf16[128,4,256]{0,2,1:T(8,128)(2,1)S(1)} all-to-all(bf16[128,4,256]{0,2,1:T(8,128)(2,1)S(1)} %bitcast.209), channel_id=1, replica_groups=mesh['dp'=4,'context'=4,'tensor'=2] {'context'}, dimensions={1} | all-to-all | bytes 524288 | tf_op jit(solution)/shard_map/all_to_all | solution.py:60
  69.6 65.2 %all-gather.14.cloned.1.call-done = bf16[2,1024,2048]{2,1,0:T(8,128)(2,1)} async-done(((bf16[2,128,2048]{2,1,0:T(8,128)(2,1)}), bf16[2,1024,2048]{2,1,0:T(8,128)(2,1)}) %all-gather.14.cloned.1.call-update) | async-done | bytes 8388624 | tf_op jit(solution)/shard_map/all_gather | solution.py:52
  142.5 20.0 %all-gather.18.cloned.1.call-done = bf16[2048,256]{0,1:T(8,128)(2,1)} async-done(((bf16[512,256]{0,1:T(8,128)(2,1)}), bf16[2048,256]{0,1:T(8,128)(2,1)}) %all-gather.18.cloned.1.call-update) | async-done | bytes 1048592 | tf_op jit(solution)/shard_map/all_gather | solution.py:61
  171.3 19.9 %all-gather.20.cloned.1.call-done = bf16[2048,256]{0,1:T(8,128)(2,1)} async-done(((bf16[512,256]{0,1:T(8,128)(2,1)}), bf16[2048,256]{0,1:T(8,128)(2,1)}) %all-gather.20.cloned.1.call-update) | async-done | bytes 1048592 | tf_op jit(solution)/shard_map/all_gather | solution.py:61
  201.7 14.3 fusion.76
  237.0 47.7 %all_to_all.227 = bf16[128,4,1024]{0,2,1:T(8,128)(2,1)S(1)} all-to-all(bf16[128,4,1024]{0,2,1:T(8,128)(2,1)} %bitcast.192), channel_id=1, replica_groups=mesh['dp'=4,'context'=4,'tensor'=2] {'context'}, dimensions={1} | all-to-all | bytes 2097152 | tf_op jit(solution)/shard_map/all_to_all | solution.py:60
  286.2 54.8 %reduce-scatter.12.cloned.1.call-done = bf16[2,128,2048]{2,1,0:T(8,128)(2,1)} async-done(((bf16[2,1024,2048]{2,1,0:T(8,128)(2,1)}), bf16[2,128,2048]{2,1,0:T(8,128)(2,1)}) %reduce-scatter.12.cloned.1.call-update) | async-done | bytes 1048592 | tf_op jit(solution)/shard_map/reduce_scatter | solution.py:56
  350.0 33.1 %all_to_all.228 = bf16[128,4,1024]{0,2,1:T(8,128)(2,1)} all-to-all(bf16[128,4,1024]{0,2,1:T(8,128)(2,1)} %bitcast.193), channel_id=1, replica_groups=mesh['dp'=4,'context'=4,'tensor'=2] {'context'}, dimensions={1} | all-to-all | bytes 2097152 | tf_op jit(solution)/shard_map/all_to_all | solution.py:60
  385.4 34.6 %all_to_all.229 = bf16[4,1024,128]{2,1,0:T(8,128)(2,1)} all-to-all(bf16[4,1024,128]{2,1,0:T(8,128)(2,1)} %bitcast.200), channel_id=1, replica_groups=mesh['dp'=4,'context'=4,'tensor'=2] {'context'}, dimensions={0} | all-to-all | bytes 2097152 | tf_op jit(solution)/shard_map/all_to_all | solution.py:65
  423.1 61.3 %all-gather.24.cloned.1.call-done = bf16[2,1024,2048]{2,1,0:T(8,128)(2,1)} async-done(((bf16[2,128,2048]{2,1,0:T(8,128)(2,1)}), bf16[2,1024,2048]{2,1,0:T(8,128)(2,1)}) %all-gather.24.cloned.1.call-update) | async-done | bytes 8388624 | tf_op jit(solution)/shard_map/all_gather | solution.py:52
  484.4 14.5 fusion.78
  498.9 39.5 %all-gather.26.cloned.1.call-done = bf16[2048,1024]{1,0:T(8,128)(2,1)} async-done(((bf16[512,1024]{1,0:T(8,128)(2,1)}), bf16[2048,1024]{1,0:T(8,128)(2,1)}) %all-gather.26.cloned.1.call-update) | async-done | bytes 4194320 | tf_op jit(solution)/shard_map/all_gather | solution.py:61
  538.3 14.4 fusion.77
  552.8 39.9 %all-gather.30.cloned.1.call-done = bf16[1024,2048]{0,1:T(8,128)(2,1)} async-done(((bf16[1024,512]{0,1:T(8,128)(2,1)}), bf16[1024,2048]{0,1:T(8,128)(2,1)}) %all-gather.30.cloned.1.call-update) | async-done | bytes 4194320 | tf_op jit(solution)/shard_map/all_gather | solution.py:66
  592.6 84.3 %all-gather.34.cloned.1.call-done = bf16[2,1024,2048]{2,1,0:T(8,128)(2,1)} async-done(((bf16[2,128,2048]{2,1,0:T(8,128)(2,1)}), bf16[2,1024,2048]{2,1,0:T(8,128)(2,1)}) %all-gather.34.cloned.1.call-update) | async-done | bytes 8388624 | tf_op jit(solution)/shard_map/all_gather | solution.py:52
  676.9 21.7 %multiply_convert_fusion.1 = (bf16[2048,1024]{1,0:T(8,128)(2,1)}, bf16[2048,1024]{1,0:T(8,128)(2,1)}, bf16[2048,1024]{1,0:T(8,128)(2,1)}) fusion(f32[2048,1024]{1,0:T(8,128)} %fusion.77, f32[2048,1024]{1,0:T(8,128)} %fusion.78, bf16[2048,2048]{1,0:T(8,128)(2,1)} %bitcast.227, bf16[1024,2048]{0,1:T(8,128)(2,1)} %all-gather.30.cloned.1.call-done), kind=kOutput, calls=%fused_computation.12 | convolution fusion | flops 8621391872 | bytes 41943040 | tf_op jit(solution)/shard_map/dot_general | solution.py:48
  698.6 15.6 %fusion.79 = f32[2048,2048]{1,0:T(8,128)} fusion(bf16[2048,1024]{1,0:T(8,128)(2,1)} %get-tuple-element.14, bf16[2048,1024]{1,0:T(8,128)(2,1)} %all-gather.26.cloned.1.call-done), kind=kOutput, calls=%fused_computation.146 | convolution fusion | flops 8589934592 | bytes 25165824 | tf_op jit(solution)/shard_map/dot_general | solution.py:48
  714.2 15.9 %add_convert_fusion.1 = bf16[2048,2048]{1,0:T(8,128)(2,1)} fusion(f32[2048,2048]{1,0:T(8,128)} %fusion.79, bf16[2048,1024]{1,0:T(8,128)(2,1)} %get-tuple-element.13, bf16[2048,1024]{1,0:T(8,128)(2,1)S(1)} %copy-done.38), kind=kOutput, calls=%fused_computation.4 | convolution fusion | flops 8598323200 | bytes 33554432 | tf_op jit(solution)/shard_map/dot_general | solution.py:48
  730.2 88.1 %reduce-scatter.16.cloned.1.call-done = bf16[2,128,2048]{2,1,0:T(8,128)(2,1)} async-done(((bf16[2,1024,2048]{2,1,0:T(8,128)(2,1)}), bf16[2,128,2048]{2,1,0:T(8,128)(2,1)}) %reduce-scatter.16.cloned.1.call-update) | async-done | bytes 1048592 | tf_op jit(solution)/shard_map/reduce_scatter | solution.py:56
  824.9 14.5 convolution_convert_fusion.2
  839.5 66.0 %all-gather.36.cloned.1.call-done = bf16[2,1024,2048]{2,1,0:T(8,128)(2,1)} async-done(((bf16[2,128,2048]{2,1,0:T(8,128)(2,1)}), bf16[2,1024,2048]{2,1,0:T(8,128)(2,1)}) %all-gather.36.cloned.1.call-update) | async-done | bytes 8388624 | tf_op jit(solution)/shard_map/all_gather | solution.py:52
  978.0 15.6 %add_convert_fusion = bf16[2048,2048]{1,0:T(8,128)(2,1)} fusion(f32[2048,2048]{1,0:T(8,128)} %fusion.54, f32[2048,2048]{1,0:T(8,128)} %fusion.51, bf16[2048,256]{1,0:T(8,128)(2,1)} %all-gather.16.cloned.1.call-done, bf16[256,8,2,128]{3,2,1,0:T(2,128)(2,1)S(1)} %bitcast.181), kind=kOutput, calls=%fused_computation.1 | convolution fusion | flops 2160066560 | bytes 44040192 | tf_op jit(solution)/shard_map/dot_general | solution.py:48
  993.7 14.1 convolution_convert_fusion
  1007.9 14.5 convolution_convert_fusion.3
  1071.7 17.0 %reduce-scatter.18.cloned.1.call-done = bf16[2,128,2048]{2,1,0:T(8,128)(2,1)} async-done(((bf16[2,1024,2048]{2,1,0:T(8,128)(2,1)}), bf16[2,128,2048]{2,1,0:T(8,128)(2,1)}) %reduce-scatter.18.cloned.1.call-update) | async-done | bytes 1048592 | tf_op jit(solution)/shard_map/reduce_scatter | solution.py:56
  1090.6 97.0 %reduce-scatter.14.cloned.1.call-done = bf16[2,128,2048]{2,1,0:T(8,128)(2,1)} async-done(((bf16[2,1024,2048]{2,1,0:T(8,128)(2,1)}), bf16[2,128,2048]{2,1,0:T(8,128)(2,1)}) %reduce-scatter.14.cloned.1.call-update) | async-done | bytes 1048592 | tf_op jit(solution)/shard_map/reduce_scatter | solution.py:56
  1192.9 48.7 %reduce-scatter.30.cloned.1.call-done = bf16[512,1024]{1,0:T(8,128)(2,1)} async-done(((bf16[2048,1024]{1,0:T(8,128)(2,1)}), bf16[512,1024]{1,0:T(8,128)(2,1)}) %reduce-scatter.30.cloned.1.call-update) | async-done | bytes 1048592 | tf_op jit(solution)/shard_map/reduce_scatter | solution.py:70
  1246.7 50.9 %reduce-scatter.28.cloned.1.call-done = bf16[512,1024]{1,0:T(8,128)(2,1)} async-done(((bf16[2048,1024]{1,0:T(8,128)(2,1)}), bf16[512,1024]{1,0:T(8,128)(2,1)}) %reduce-scatter.28.cloned.1.call-update) | async-done | bytes 1048592 | tf_op jit(solution)/shard_map/reduce_scatter | solution.py:70
  1297.6 30.3 %all_to_all.230 = bf16[4,128,1024]{2,1,0:T(8,128)(2,1)} all-to-all(bf16[4,128,1024]{2,1,0:T(8,128)(2,1)} %bitcast.202), channel_id=1, replica_groups=mesh['dp'=4,'context'=4,'tensor'=2] {'context'}, dimensions={0} | all-to-all | bytes 2097152 | tf_op jit(solution)/shard_map/all_to_all | solution.py:71
  1333.6 26.7 %reduce-scatter.22.cloned.1.call-done = bf16[512,256]{1,0:T(8,128)(2,1)} async-done(((bf16[2048,256]{1,0:T(8,128)(2,1)}), bf16[512,256]{1,0:T(8,128)(2,1)}) %reduce-scatter.22.cloned.1.call-update) | async-done | bytes 262160 | tf_op jit(solution)/shard_map/reduce_scatter | solution.py:70
  1372.5 18.7 %reduce-scatter.20.cloned.1.call-done = bf16[512,256]{1,0:T(8,128)(2,1)} async-done(((bf16[2048,256]{1,0:T(8,128)(2,1)}), bf16[512,256]{1,0:T(8,128)(2,1)}) %reduce-scatter.20.cloned.1.call-update) | async-done | bytes 262160 | tf_op jit(solution)/shard_map/reduce_scatter | solution.py:70
  1395.8 26.2 %reduce-scatter.26.cloned.1.call-done = bf16[256,512]{1,0:T(8,128)(2,1)} async-done(((bf16[256,2048]{1,0:T(8,128)(2,1)}), bf16[256,512]{1,0:T(8,128)(2,1)}) %reduce-scatter.26.cloned.1.call-update) | async-done | bytes 262160 | tf_op jit(solution)/shard_map/reduce_scatter | solution.py:75
  (236 shorter events, 308.1 us)
Async XLA Ops:
  7.2 62.4 %all-gather.16.cloned.1.call-start = ((), (), s32[]{:S(2)}) async-start(), calls=%async_computation.26 | async-start | bytes 1310720 | tf_op jit(solution)/shard_map/all_gather | solution.py:61
  24.4 110.4 %all-gather.14.cloned.1.call-start = ((), (), s32[]{:S(2)}) async-start(), calls=%async_computation.25 | async-start | bytes 9437184 | tf_op jit(solution)/shard_map/all_gather | solution.py:52
  29.5 133.1 %all-gather.18.cloned.1.call-start = ((), (), s32[]{:S(2)}) async-start(), calls=%async_computation.27 | async-start | bytes 1310720 | tf_op jit(solution)/shard_map/all_gather | solution.py:61
  41.7 149.5 %all-gather.20.cloned.1.call-start = ((), (), s32[]{:S(2)}) async-start(), calls=%async_computation.28 | async-start | bytes 1310720 | tf_op jit(solution)/shard_map/all_gather | solution.py:61
  53.9 14.7 %all-to-all-start.3 = ((bf16[4,256,128]{2,1,0:T(8,128)(2,1)}), bf16[4,256,128]{2,1,0:T(8,128)(2,1)S(1)}, u32[]{:S(2)}, u32[]{:S(2)}) async-start(bf16[4,256,128]{2,1,0:T(8,128)(2,1)} %bitcast.20), calls=%async_computation.3 | async-start | bytes 524288 | tf_op jit(solution)/shard_map/all_to_all | solution.py:65
  57.4 169.7 %all-gather.22.cloned.1.call-start = ((), (), s32[]{:S(2)}) async-start(), calls=%async_computation.29 | async-start | bytes 1310720 | tf_op jit(solution)/shard_map/all_gather | solution.py:66
  69.5 271.4 %reduce-scatter.12.cloned.1.call-start = ((), (), s32[]{:S(2)}) async-start(), calls=%async_computation.30 | async-start | bytes 9437184 | tf_op jit(solution)/shard_map/reduce_scatter | solution.py:56
  234.5 188.6 %all-gather.28.cloned.1.call-start = ((), (), s32[]{:S(2)}) async-start(), calls=%async_computation.33 | async-start | bytes 5242880 | tf_op jit(solution)/shard_map/all_gather | solution.py:61
  286.0 198.4 %all-gather.24.cloned.1.call-start = ((), (), s32[]{:S(2)}) async-start(), calls=%async_computation.31 | async-start | bytes 9437184 | tf_op jit(solution)/shard_map/all_gather | solution.py:52
  286.2 534.4 %copy-start.23 = (f32[2,128]{1,0:T(2,128)}, f32[2,128]{1,0:T(2,128)S(1)}, u32[]{:S(2)}) copy-start(f32[2,128]{1,0:T(2,128)S(1)} %compare_convert_fusion) | copy-start | bytes 3076
  347.7 190.7 %all-gather.26.cloned.1.call-start = ((), (), s32[]{:S(2)}) async-start(), calls=%async_computation.32 | async-start | bytes 5242880 | tf_op jit(solution)/shard_map/all_gather | solution.py:61
  385.4 207.3 %all-gather.30.cloned.1.call-start = ((), (), s32[]{:S(2)}) async-start(), calls=%async_computation.34 | async-start | bytes 5242880 | tf_op jit(solution)/shard_map/all_gather | solution.py:66
  422.3 254.6 %all-gather.34.cloned.1.call-start = ((), (), s32[]{:S(2)}) async-start(), calls=%async_computation.37 | async-start | bytes 9437184 | tf_op jit(solution)/shard_map/all_gather | solution.py:52
  423.0 395.3 %reduce-scatter.16.cloned.1.call-start = ((), (), s32[]{:S(2)}) async-start(), calls=%async_computation.38 | async-start | bytes 9437184 | tf_op jit(solution)/shard_map/reduce_scatter | solution.py:56
  730.1 175.4 %all-gather.36.cloned.1.call-start = ((), (), s32[]{:S(2)}) async-start(), calls=%async_computation.39 | async-start | bytes 9437184 | tf_op jit(solution)/shard_map/all_gather | solution.py:52
  824.9 239.9 %reduce-scatter.32.cloned.1.call-start = ((), (), s32[]{:S(2)}) async-start(), calls=%async_computation.48 | async-start | bytes 5242880 | tf_op jit(solution)/shard_map/reduce_scatter | solution.py:75
  839.4 249.3 %reduce-scatter.18.cloned.1.call-start = ((), (), s32[]{:S(2)}) async-start(), calls=%async_computation.40 | async-start | bytes 9437184 | tf_op jit(solution)/shard_map/reduce_scatter | solution.py:56
  993.6 194.0 %reduce-scatter.14.cloned.1.call-start = ((), (), s32[]{:S(2)}) async-start(), calls=%async_computation.35 | async-start | bytes 9437184 | tf_op jit(solution)/shard_map/reduce_scatter | solution.py:56
  1007.8 233.8 %reduce-scatter.30.cloned.1.call-start = ((), (), s32[]{:S(2)}) async-start(), calls=%async_computation.47 | async-start | bytes 5242880 | tf_op jit(solution)/shard_map/reduce_scatter | solution.py:70
  1022.4 275.2 %reduce-scatter.28.cloned.1.call-start = ((), (), s32[]{:S(2)}) async-start(), calls=%async_computation.46 | async-start | bytes 5242880 | tf_op jit(solution)/shard_map/reduce_scatter | solution.py:70
  1036.6 292.5 %reduce-scatter.24.cloned.1.call-start = ((), (), s32[]{:S(2)}) async-start(), calls=%async_computation.44 | async-start | bytes 1310720 | tf_op jit(solution)/shard_map/reduce_scatter | solution.py:70
  1043.6 316.7 %reduce-scatter.22.cloned.1.call-start = ((), (), s32[]{:S(2)}) async-start(), calls=%async_computation.43 | async-start | bytes 1310720 | tf_op jit(solution)/shard_map/reduce_scatter | solution.py:70
  1050.7 340.4 %reduce-scatter.20.cloned.1.call-start = ((), (), s32[]{:S(2)}) async-start(), calls=%async_computation.42 | async-start | bytes 1310720 | tf_op jit(solution)/shard_map/reduce_scatter | solution.py:70
  1057.9 364.2 %reduce-scatter.26.cloned.1.call-start = ((), (), s32[]{:S(2)}) async-start(), calls=%async_computation.45 | async-start | bytes 1310720 | tf_op jit(solution)/shard_map/reduce_scatter | solution.py:75
  1067.3 174.2 %all-to-all-start.13 = ((bf16[1024,4,128]{2,0,1:T(8,128)(2,1)}), bf16[1024,4,128]{2,0,1:T(8,128)(2,1)}, u32[]{:S(2)}, u32[]{:S(2)}) async-start(bf16[1024,4,128]{2,0,1:T(8,128)(2,1)} %copy_bitcast_fusion), calls=%async_computation.24 | async-start | bytes 2097152 | tf_op jit(solution)/shard_map/all_to_all | solution.py:76
  1071.6 367.2 %all-gather.32.cloned.1.call-start = ((), (), s32[]{:S(2)}) async-start(), calls=%async_computation.36 | async-start | bytes 3145728 | tf_op jit(solution)/shard_map/all_gather | solution.py:153
  1241.6 56.0 %all-to-all-start.12 = ((bf16[4,128,1024]{2,1,0:T(8,128)(2,1)}), bf16[4,128,1024]{2,1,0:T(8,128)(2,1)S(1)}, u32[]{:S(2)}, u32[]{:S(2)}) async-start(bf16[4,128,1024]{2,1,0:T(8,128)(2,1)} %bitcast.201), calls=%async_computation.22 | async-start | bytes 2097152 | tf_op jit(solution)/shard_map/all_to_all | solution.py:71
  1246.2 204.9 %all-gather.38.cloned.1.call-start = ((), (), s32[]{:S(2)}) async-start(), calls=%async_computation.41 | async-start | bytes 6291456 | tf_op jit(solution)/shard_map/all_gather | solution.py:179
  1329.0 31.3 %all-to-all-start.9 = ((bf16[4,128,256]{2,1,0:T(8,128)(2,1)}), bf16[4,128,256]{2,1,0:T(8,128)(2,1)S(1)}, u32[]{:S(2)}, u32[]{:S(2)}) async-start(bf16[4,128,256]{2,1,0:T(8,128)(2,1)} %bitcast.218), calls=%async_computation.16 | async-start | bytes 524288 | tf_op jit(solution)/shard_map/all_to_all | solution.py:71
  1360.3 30.9 %all-to-all-start.8 = ((bf16[4,128,256]{2,1,0:T(8,128)(2,1)}), bf16[4,128,256]{2,1,0:T(8,128)(2,1)}, u32[]{:S(2)}, u32[]{:S(2)}) async-start(bf16[4,128,256]{2,1,0:T(8,128)(2,1)} %bitcast.217), calls=%async_computation.14 | async-start | bytes 524288 | tf_op jit(solution)/shard_map/all_to_all | solution.py:71
  1391.2 33.4 %all-to-all-start.7 = ((bf16[4,128,256]{2,1,0:T(8,128)(2,1)}), bf16[4,128,256]{2,1,0:T(8,128)(2,1)S(1)}, u32[]{:S(2)}, u32[]{:S(2)}) async-start(bf16[4,128,256]{2,1,0:T(8,128)(2,1)} %bitcast.216), calls=%async_computation.12 | async-start | bytes 524288 | tf_op jit(solution)/shard_map/all_to_all | solution.py:71
  1424.6 13.4 all-to-all-start.10
  (38 other events, 2023.2 us)
Sparse Core Ops, SparseCore 0:
  24.5 25.5 all-gather.15
  52.4 82.4 all-gather.13
  137.3 25.2 all-gather.17
  164.8 26.3 all-gather.19
  192.9 26.4 all-gather.21
  234.6 106.3 reduce-scatter.11
  343.4 55.7 all-gather.27
  401.3 83.0 all-gather.23
  486.8 51.4 all-gather.25
  540.0 52.5 all-gather.29
  594.8 82.0 all-gather.33
  730.2 88.0 reduce-scatter.15
  825.0 80.4 all-gather.35
  908.4 51.0 reduce-scatter.31
  993.8 94.8 reduce-scatter.17
  1090.8 96.7 reduce-scatter.13
  1190.5 51.0 reduce-scatter.29
  1245.0 52.5 reduce-scatter.27
  1301.1 27.9 reduce-scatter.23
  1332.4 27.9 reduce-scatter.21
  1363.2 27.9 reduce-scatter.19
  1394.1 27.9 reduce-scatter.25
  1423.6 10.5 all-gather.31
  1436.2 14.8 all-gather.37

commit v2 on v1

v2 whole, which is shorter than its diff:
```python
import math

import jax
import jax.numpy as jnp
from jax import lax
from jax.sharding import PartitionSpec as P

HEAD_DIM = 128
ROWS = ("context", "tensor")


def rope_tables(positions, head_dim):
    half_dim = head_dim // 2
    inverse_freq = jnp.exp(
        -math.log(10000.0) * jnp.arange(half_dim, dtype=jnp.float32) * 2.0 / head_dim
    )
    angles = positions.astype(jnp.float32)[:, None] * inverse_freq[None, :]
    angles = jnp.concatenate([angles, angles], axis=-1)
    return (jnp.cos(angles)[:, None, :], jnp.sin(angles)[:, None, :])


def rotate(values, cosine, sine):
    half_dim = values.shape[-1] // 2
    turned = jnp.concatenate([-values[..., half_dim:], values[..., :half_dim]], axis=-1)
    return values * cosine + turned * sine


def unrotate(upstream, cosine, sine):
    half_dim = upstream.shape[-1] // 2
    scaled = upstream * sine
    turned = jnp.concatenate([scaled[..., half_dim:], -scaled[..., :half_dim]], axis=-1)
    return upstream * cosine + turned


def normalize(values):
    centered = values - jnp.mean(values, axis=-1, keepdims=True)
    inverse = lax.rsqrt(jnp.mean(centered * centered, axis=-1, keepdims=True) + 1e-05)
    return (centered * inverse, inverse)


def normalize_back(normed, inverse, upstream):
    mean_grad = jnp.mean(upstream, axis=-1, keepdims=True)
    mean_cross = jnp.mean(upstream * normed, axis=-1, keepdims=True)
    return inverse * (upstream - mean_grad - normed * mean_cross)


def dot(left, right, dims):
    return lax.dot_general(left, right, (dims, ((), ())), preferred_element_type=jnp.float32)


def gather_rows(values):
    return lax.all_gather(values, ROWS, axis=0, tiled=True)


def scatter_rows(values):
    return lax.psum_scatter(values.astype(jnp.bfloat16), ROWS, scatter_dimension=0, tiled=True).astype(
        jnp.float32
    )


def put(buffer, piece, index):
    return lax.dynamic_update_slice_in_dim(buffer, piece[None], index, 0)


def take(buffer, index):
    return lax.dynamic_index_in_dim(buffer, index, 0, keepdims=False)


def spread_weight(weight):
    rows, contexts, columns = weight.shape
    groups = lax.axis_size("dp")
    here, group = lax.axis_index("context"), lax.axis_index("dp")
    pieces = jnp.moveaxis(weight, 1, 0)
    mine = jnp.zeros((contexts, rows, columns), weight.dtype)
    mine = put(mine, take(pieces, here), here)
    for step in range(1, contexts):
        route = [(i, (i + step) % contexts) for i in range(contexts)]
        piece = lax.ppermute(take(pieces, (here + step) % contexts), "context", route)
        mine = put(mine, piece, (here - step) % contexts)
    whole = jnp.zeros((groups,) + mine.shape, weight.dtype)
    whole = put(whole, mine, group)
    for step in range(1, groups):
        route = [(i, i ^ step) for i in range(groups)]
        whole = put(whole, lax.ppermute(mine, "dp", route), group ^ step)
    return whole.reshape(groups * contexts * rows, columns)


def collect_gradient(partial, contexts):
    groups = lax.axis_size("dp")
    here, group = lax.axis_index("context"), lax.axis_index("dp")
    columns = partial.shape[1]
    rows = partial.shape[0] // (groups * contexts)
    parts = partial.reshape(groups, contexts * rows, columns)
    total = take(parts, group).astype(jnp.float32)
    for step in range(1, groups):
        route = [(i, i ^ step) for i in range(groups)]
        total = total + lax.ppermute(take(parts, group ^ step), "dp", route).astype(jnp.float32)
    pieces = total.astype(jnp.bfloat16).reshape(contexts, rows, columns)
    mine = jnp.zeros_like(pieces)
    mine = put(mine, take(pieces, here), here)
    for step in range(1, contexts):
        route = [(i, (i + step) % contexts) for i in range(contexts)]
        piece = lax.ppermute(take(pieces, (here + step) % contexts), "context", route)
        mine = put(mine, piece, (here - step) % contexts)
    return jnp.moveaxis(mine, 0, 1)


def per_device(tokens, lengths, w_query, w_key, w_value, w_out, w_gate, w_up, w_down, cotangent):
    low = jnp.bfloat16
    slots, chip_rows, width = tokens.shape
    contexts, cores = lax.axis_size("context"), lax.axis_size("tensor")
    rows = chip_rows // cores
    seq = chip_rows * contexts
    head_cols = w_query.shape[1] // contexts
    units = w_gate.shape[1] // contexts
    heads = head_cols // HEAD_DIM
    scale = 1.0 / math.sqrt(HEAD_DIM)
    core = lax.axis_index("tensor")
    own_start = lax.axis_index("context") * chip_rows + core * rows
    own_positions = own_start + jnp.arange(rows, dtype=jnp.int32)
    positions = jnp.arange(seq, dtype=jnp.int32)
    rope_cos, rope_sin = rope_tables(positions, HEAD_DIM)
    causal = positions[None, :] <= positions[:, None]

    def by_context(weight):
        return weight.reshape(weight.shape[0], contexts, -1)

    attention_w = spread_weight(
        jnp.concatenate([by_context(w) for w in (w_query, w_key, w_value, w_out.T)], axis=2)
    )
    qkv_w, out_w = attention_w[:, : 3 * head_cols], attention_w[:, 3 * head_cols :]
    ffn_w = spread_weight(
        jnp.concatenate([by_context(w) for w in (w_gate, w_up, w_down.T)], axis=2)
    )
    gate_up_w, down_w = ffn_w[:, : 2 * units], ffn_w[:, 2 * units :]

    def einsum(form, left, right):
        return jnp.einsum(form, left, right, preferred_element_type=jnp.float32)

    def split(values):
        return values.reshape(seq, heads, HEAD_DIM)

    def slot_pass(slot):
        own_tokens = lax.dynamic_slice_in_dim(tokens[slot], core * rows, rows, 0).astype(jnp.float32)
        own_cotangent = lax.dynamic_slice_in_dim(cotangent[slot], core * rows, rows, 0).astype(
            jnp.float32
        )
        length = lengths[slot]
        valid_rows = (own_positions < length).astype(jnp.float32)[:, None]
        allowed = (causal & (positions < length)[None, :])[None]
        norm_one, inverse_one = normalize(own_tokens)
        norm_one_all = gather_rows(norm_one.astype(low))
        out_grad = own_cotangent * valid_rows
        ffn_grad_all = gather_rows((valid_rows * out_grad).astype(low))

        qkv = dot(norm_one_all, qkv_w, ((1,), (0,)))
        query, key, value = (qkv[:, i * head_cols : (i + 1) * head_cols] for i in range(3))
        query = rotate(split(query), rope_cos, rope_sin).astype(low)
        key = rotate(split(key), rope_cos, rope_sin).astype(low)
        value = split(value.astype(low))
        scores = einsum("qhd,khd->hqk", query, key) * scale
        masked = jnp.where(allowed, scores, -1e30)
        row_top = jnp.max(masked, axis=-1, keepdims=True)
        exponent = jnp.where(allowed, jnp.exp(masked - row_top), 0.0)
        probabilities = exponent / jnp.sum(exponent, axis=-1, keepdims=True)
        attended = einsum("hqk,khd->qhd", probabilities.astype(low), value)
        attended = attended.reshape(seq, heads * HEAD_DIM).astype(low)

        branch = scatter_rows(dot(attended, out_w, ((1,), (1,))))
        middle = own_tokens + valid_rows * branch
        norm_two, inverse_two = normalize(middle)
        norm_two_all = gather_rows(norm_two.astype(low))

        gate_up = dot(norm_two_all, gate_up_w, ((1,), (0,)))
        gate, upper = gate_up[:, :units], gate_up[:, units:]
        sigmoid = jax.nn.sigmoid(gate)
        silu = gate * sigmoid
        hidden = (silu * upper).astype(low)
        hidden_grad = dot(ffn_grad_all, down_w, ((1,), (0,)))
        gate_grad = (hidden_grad * upper * sigmoid * (1.0 + gate * (1.0 - sigmoid))).astype(low)
        upper_grad = (hidden_grad * silu).astype(low)
        gate_up_grad = jnp.concatenate([gate_grad, upper_grad], axis=1)
        norm_two_grad = scatter_rows(dot(gate_up_grad, gate_up_w, ((1,), (1,))))
        middle_grad = out_grad + normalize_back(norm_two, inverse_two, norm_two_grad)
        branch_grad_all = gather_rows((valid_rows * middle_grad).astype(low))

        feedforward = scatter_rows(dot(hidden, down_w, ((1,), (1,))))
        layer_out = (middle + valid_rows * feedforward).astype(low)
        ffn_grads = (dot(norm_two_all, gate_up_grad, ((0,), (0,))), dot(ffn_grad_all, hidden, ((0,), (0,))))

        attended_grad = split(dot(branch_grad_all, out_w, ((1,), (0,))).astype(low))
        grad_out = dot(branch_grad_all, attended, ((0,), (0,)))
        prob_grad = einsum("qhd,khd->hqk", attended_grad, value)
        row_delta = jnp.sum(probabilities * prob_grad, axis=-1, keepdims=True)
        score_grad = (probabilities * (prob_grad - row_delta)).astype(low)
        query_grad = einsum("hqk,khd->qhd", score_grad, key) * scale
        key_grad = einsum("hqk,qhd->khd", score_grad, query) * scale
        value_grad = einsum("hqk,qhd->khd", probabilities.astype(low), attended_grad)
        qkv_grad = jnp.concatenate(
            [
                unrotate(query_grad, rope_cos, rope_sin).astype(low).reshape(seq, -1),
                unrotate(key_grad, rope_cos, rope_sin).astype(low).reshape(seq, -1),
                value_grad.astype(low).reshape(seq, -1),
            ],
            axis=1,
        )
        norm_one_grad = scatter_rows(dot(qkv_grad, qkv_w, ((1,), (1,))))
        input_grad = middle_grad + normalize_back(norm_one, inverse_one, norm_one_grad)
        attention_grads = (dot(norm_one_all, qkv_grad, ((0,), (0,))), grad_out)
        return layer_out, input_grad, attention_grads, ffn_grads

    results = [slot_pass(slot) for slot in range(slots)]
    layer_out = lax.all_gather(jnp.stack([r[0] for r in results]), "tensor", axis=1, tiled=True)
    input_grad = lax.all_gather(jnp.stack([r[1] for r in results]), "tensor", axis=1, tiled=True)

    def summed(group, item):
        total = results[0][group][item]
        for other in results[1:]:
            total = total + other[group][item]
        return total.astype(low)

    attention = collect_gradient(jnp.concatenate([summed(2, 0), summed(2, 1)], axis=1), contexts)
    ffn = collect_gradient(jnp.concatenate([summed(3, 0), summed(3, 1)], axis=1), contexts)
    attention, ffn = attention.astype(jnp.float32), ffn.astype(jnp.float32)

    def piece(array, start, size):
        return array[:, :, start : start + size].reshape(array.shape[0], -1)

    grads = tuple(piece(attention, i * head_cols, head_cols) for i in range(3)) + (
        piece(attention, 3 * head_cols, head_cols).T,
        piece(ffn, 0, units),
        piece(ffn, units, units),
        piece(ffn, 2 * units, units).T,
    )
    return (layer_out, input_grad) + grads


def solution(mesh):
    tokens = P("dp", "context", None)
    column = P(("dp", "context"), "tensor")
    row = P("tensor", ("dp", "context"))
    weights = (column, column, column, row, column, column, row)
    return jax.shard_map(
        per_device,
        mesh=mesh,
        in_specs=(tokens, P("dp")) + weights + (tokens,),
        out_specs=(tokens, tokens) + weights,
        check_vma=False,
    )
```

time: 1470 us -> 1350 us (0.918)
  blocking collectives: 183 us -> 0 us
  local copies, waits for them, and re-layouts: 47.5 us -> 146 us
  waiting for transfers between devices: 851 us -> 806 us
  matrix products: 280 us -> 248 us
  other arithmetic: 55.2 us -> 78.9 us
  starting transfers between devices: 31.8 us -> 50 us
    ppermute x0 -> x24, waiting for transfers between devices: none -> 493 us  [the longest x6 174 us: collect_gradient(): lax.ppermute(take(parts, group ^ step), 'dp', route).astype(jnp.float32)]
    all_gather x13 -> x10, waiting for transfers between devices: 408 us -> 82.8 us  [the longest x8 82.8 us: gather_rows(): return lax.all_gather(values, ROWS, axis=0, tiled=True)]
    reduce_scatter x11 -> x8, waiting for transfers between devices: 429 us -> 230 us  [scatter_rows(): lax.psum_scatter(values.astype(jnp.bfloat16), ROWS, scatter_dimension=0,...]
    all_to_all x7 -> x0, blocking collectives: 183 us -> none  [the longest x5 118 us: column_weight(): lax.all_to_all(weight, 'context', split_axis=1, concat_axis=0, tiled=True)]
    ppermute x0 -> x24, starting transfers between devices: none -> 48.7 us  [the longest x6 23.8 us: collect_gradient(): lax.ppermute(take(pieces, (here + step) % contexts), 'context', route)]
    dynamic_update_slice x0 -> x22, local copies, waits for them, and re-layouts: none -> 37.9 us  [put(): return lax.dynamic_update_slice_in_dim(buffer, piece[None], index, 0)]
    all_to_all x7 -> x0, starting transfers between devices: 30.7 us -> none  [the longest x4 18.4 us: column_gradient(): lax.all_to_all(summed, 'context', split_axis=0, concat_axis=1, tiled=True)]
    dot_general x21 -> x24, matrix products: 231 us -> 201 us  [dot(): lax.dot_general(left, right, (dims, ((), ())), preferred_element_type=jnp...]
  transfers between devices with their start and end apart: 31 -> 42, of which waited for: 21 -> 27; matrix products, arithmetic and copies ran while one was open for 21% -> 29% of each run, Pallas kernels for 0% -> 0%
where the time goes in v2:
time: 1350 us
  waiting for transfers between devices  806 us (60%)
  matrix products  248 us (18%)
  local copies, waits for them, and re-layouts  146 us (11%)
  other arithmetic  78.9 us (6%)
  starting transfers between devices  50 us (4%)
  between operations  16.1 us (1%)
    reduce_scatter x8, waiting for transfers between devices, scatter_rows(): lax.psum_scatter(values.astype(jnp.bfloat16), ROWS, scatter_dimension=0,...  230 us
    dot_general x24, matrix products, dot(): lax.dot_general(left, right, (dims, ((), ())), preferred_element_type=jnp...  201 us
    ppermute x6, waiting for transfers between devices, collect_gradient(): lax.ppermute(take(parts, group ^ step), 'dp', route).astype(jnp.float32)  174 us
    ppermute x6, waiting for transfers between devices, spread_weight(): whole = put(whole, lax.ppermute(mine, 'dp', route), group ^ step)  158 us
    ppermute x6, waiting for transfers between devices, spread_weight(): lax.ppermute(take(pieces, (here + step) % contexts), 'context', route)  104 us
    all_gather x8, waiting for transfers between devices, gather_rows(): return lax.all_gather(values, ROWS, axis=0, tiled=True)  82.8 us
    ppermute x6, waiting for transfers between devices, collect_gradient(): lax.ppermute(take(pieces, (here + step) % contexts), 'context', route)  57.6 us
    dynamic_update_slice x22, local copies, waits for them, and re-layouts, put(): return lax.dynamic_update_slice_in_dim(buffer, piece[None], index, 0)  37.9 us
  transfers between devices with their start and end apart: 42, of which 27 were waited for; matrix products, arithmetic and copies ran while one was open for 29% of the time, Pallas kernels for 0%

profile of v2, /device:TPU:0, one launch (start us, length us, event | category | flops | bytes accessed | tf_op | source)
XLA Modules:
  0.0 1345.1 jit_solution(2698371108870244064)
XLA Ops:
  33.9 18.7 %collective-permute-done.1 = bf16[128,1024]{1,0:T(8,128)(2,1)} collective-permute-done((bf16[128,1024]{1,0:T(8,128)(2,1)}, bf16[128,1024]{1,0:T(8,128)(2,1)}, u32[]{:S(2)}, u32[]{:S(2)}) %collective-permute-start.1) | collective-permute-done | bytes 262176 | tf_op jit(solution)/shard_map/ppermute | solution.py:78
  67.4 14.9 %collective-permute-done.3 = bf16[4,128,1024]{2,1,0:T(8,128)(2,1)} collective-permute-done((bf16[4,128,1024]{2,1,0:T(8,128)(2,1)}, bf16[4,128,1024]{2,1,0:T(8,128)(2,1)}, u32[]{:S(2)}, u32[]{:S(2)}) %collective-permute-start.3) | collective-permute-done | bytes 1048608 | tf_op jit(solution)/shard_map/ppermute | solution.py:84
  84.5 21.5 %collective-permute-done.4 = bf16[4,128,1024]{2,1,0:T(8,128)(2,1)} collective-permute-done((bf16[4,128,1024]{2,1,0:T(8,128)(2,1)}, bf16[4,128,1024]{2,1,0:T(8,128)(2,1)}, u32[]{:S(2)}, u32[]{:S(2)}) %collective-permute-start.4) | collective-permute-done | bytes 1048608 | tf_op jit(solution)/shard_map/ppermute | solution.py:84
  184.9 28.6 %reduce-scatter.13.cloned.1.call-done = bf16[128,2048]{1,0:T(8,128)(2,1)} async-done(((bf16[1024,2048]{1,0:T(8,128)(2,1)}), bf16[128,2048]{1,0:T(8,128)(2,1)}) %reduce-scatter.13.cloned.1.call-update) | async-done | bytes 524304 | tf_op jit(solution)/shard_map/reduce_scatter | solution.py:56
  220.1 43.9 %reduce-scatter.9.cloned.1.call-done = bf16[128,2048]{1,0:T(8,128)(2,1)} async-done(((bf16[1024,2048]{1,0:T(8,128)(2,1)}), bf16[128,2048]{1,0:T(8,128)(2,1)}) %reduce-scatter.9.cloned.1.call-update) | async-done | bytes 524304 | tf_op jit(solution)/shard_map/reduce_scatter | solution.py:56
  279.9 32.3 %collective-permute-done.6 = bf16[128,3072]{1,0:T(8,128)(2,1)S(1)} collective-permute-done((bf16[128,3072]{1,0:T(8,128)(2,1)S(1)}, bf16[128,3072]{1,0:T(8,128)(2,1)S(1)}, u32[]{:S(2)}, u32[]{:S(2)}) %collective-permute-start.6) | collective-permute-done | bytes 786464 | tf_op jit(solution)/shard_map/ppermute | solution.py:78
  313.1 46.6 %collective-permute-done.7 = bf16[128,3072]{1,0:T(8,128)(2,1)S(1)} collective-permute-done((bf16[128,3072]{1,0:T(8,128)(2,1)S(1)}, bf16[128,3072]{1,0:T(8,128)(2,1)S(1)}, u32[]{:S(2)}, u32[]{:S(2)}) %collective-permute-start.7) | collective-permute-done | bytes 786464 | tf_op jit(solution)/shard_map/ppermute | solution.py:78
  375.5 57.4 %collective-permute-done.9 = bf16[4,128,3072]{2,1,0:T(8,128)(2,1)} collective-permute-done((bf16[4,128,3072]{2,1,0:T(8,128)(2,1)}, bf16[4,128,3072]{2,1,0:T(8,128)(2,1)}, u32[]{:S(2)}, u32[]{:S(2)}) %collective-permute-start.9) | collective-permute-done | bytes 3145760 | tf_op jit(solution)/shard_map/ppermute | solution.py:84
  436.7 64.0 %collective-permute-done.10 = bf16[4,128,3072]{2,1,0:T(8,128)(2,1)} collective-permute-done((bf16[4,128,3072]{2,1,0:T(8,128)(2,1)}, bf16[4,128,3072]{2,1,0:T(8,128)(2,1)}, u32[]{:S(2)}, u32[]{:S(2)}) %collective-permute-start.10) | collective-permute-done | bytes 3145760 | tf_op jit(solution)/shard_map/ppermute | solution.py:84
  508.3 14.8 %fusion.11 = f32[1024,2048]{1,0:T(8,128)} fusion(bf16[1024,2048]{1,0:T(8,128)(2,1)} %all-gather.17.cloned.1.call-done, bf16[2048,3072]{1,0:T(8,128)(2,1)} %bitcast.315), kind=kOutput, calls=%fused_computation.25 | convolution fusion | flops 8589934592 | bytes 20971520 | tf_op jit(solution)/shard_map/dot_general | solution.py:48
  523.1 12.0 multiply_convert_fusion.3
  537.1 12.6 fusion.28
  559.8 14.6 %fusion.13 = f32[1024,2048]{1,0:T(8,128)} fusion(bf16[1024,2048]{1,0:T(8,128)(2,1)} %all-gather.13.cloned.1.call-done, bf16[2048,3072]{1,0:T(8,128)(2,1)} %bitcast.319), kind=kOutput, calls=%fused_computation.27 | convolution fusion | flops 8589934592 | bytes 20971520 | tf_op jit(solution)/shard_map/dot_general | solution.py:48
  574.4 12.1 multiply_convert_fusion.5
  588.4 12.7 fusion.25
  611.1 12.0 reduce-scatter.21.cloned.1.call-done
  624.6 49.0 %reduce-scatter.15.cloned.1.call-done = bf16[128,2048]{1,0:T(8,128)(2,1)} async-done(((bf16[1024,2048]{1,0:T(8,128)(2,1)}), bf16[128,2048]{1,0:T(8,128)(2,1)}) %reduce-scatter.15.cloned.1.call-update) | async-done | bytes 524304 | tf_op jit(solution)/shard_map/reduce_scatter | solution.py:56
  677.2 47.1 %reduce-scatter.17.cloned.1.call-done = bf16[128,2048]{1,0:T(8,128)(2,1)} async-done(((bf16[1024,2048]{1,0:T(8,128)(2,1)}), bf16[128,2048]{1,0:T(8,128)(2,1)}) %reduce-scatter.17.cloned.1.call-update) | async-done | bytes 524304 | tf_op jit(solution)/shard_map/reduce_scatter | solution.py:56
  725.9 49.0 %reduce-scatter.11.cloned.1.call-done = bf16[128,2048]{1,0:T(8,128)(2,1)} async-done(((bf16[1024,2048]{1,0:T(8,128)(2,1)}), bf16[128,2048]{1,0:T(8,128)(2,1)}) %reduce-scatter.11.cloned.1.call-update) | async-done | bytes 524304 | tf_op jit(solution)/shard_map/reduce_scatter | solution.py:56
  778.6 43.3 %all-gather.27.cloned.1.call-done = bf16[1024,2048]{1,0:T(8,128)(2,1)} async-done(((bf16[128,2048]{1,0:T(8,128)(2,1)}), bf16[1024,2048]{1,0:T(8,128)(2,1)}) %all-gather.27.cloned.1.call-update) | async-done | bytes 4194320 | tf_op jit(solution)/shard_map/all_gather | solution.py:52
  839.8 29.2 %all-gather.23.cloned.1.call-done = bf16[1024,2048]{1,0:T(8,128)(2,1)} async-done(((bf16[128,2048]{1,0:T(8,128)(2,1)}), bf16[1024,2048]{1,0:T(8,128)(2,1)}) %all-gather.23.cloned.1.call-update) | async-done | bytes 4194320 | tf_op jit(solution)/shard_map/all_gather | solution.py:52
  909.6 13.0 fusion.31
  922.6 16.8 %add_convert_fusion = bf16[2048,2048]{0,1:T(8,128)(2,1)} fusion(f32[2048,2048]{0,1:T(8,128)} %fusion.31, bf16[1024,2048]{1,0:T(8,128)(2,1)} %all-gather.17.cloned.1.call-done, bf16[1024,1024]{1,0:T(8,128)(2,1)} %copy-done.76, bf16[1024,1024]{1,0:T(8,128)(2,1)} %copy-done.75), kind=kOutput, calls=%fused_computation.2 | convolution fusion | flops 8606711808 | bytes 33554432 | tf_op jit(solution)/shard_map/dot_general | solution.py:48
  952.1 14.9 %pad_maximum_fusion = bf16[2048,3072]{0,1:T(8,128)(2,1)} fusion(bf16[2048,1024]{0,1:T(8,128)(2,1)} %add_convert_fusion.1, bf16[2048,2048]{0,1:T(8,128)(2,1)} %add_convert_fusion), kind=kLoop, calls=%fused_computation.3 | loop fusion | flops 25165824 | bytes 25165824 | tf_op jit(solution)/shard_map/concatenate | solution.py:223
  967.0 16.7 %copy.152 = bf16[2048,3072]{1,0:T(8,128)(2,1)} copy(bf16[2048,3072]{0,1:T(8,128)(2,1)} %pad_maximum_fusion) | data formatting | bytes 25165824 | tf_op jit(solution)/shard_map/reshape | solution.py:93
  993.6 68.6 %collective-permute-done.20 = bf16[512,3072]{1,0:T(8,128)(2,1)S(1)} collective-permute-done((bf16[512,3072]{1,0:T(8,128)(2,1)}, bf16[512,3072]{1,0:T(8,128)(2,1)S(1)}, u32[]{:S(2)}, u32[]{:S(2)}) %collective-permute-start.20) | collective-permute-done | bytes 3145760 | tf_op jit(solution)/shard_map/ppermute | solution.py:97
  1062.3 66.6 %collective-permute-done.19 = bf16[512,3072]{1,0:T(8,128)(2,1)S(1)} collective-permute-done((bf16[512,3072]{1,0:T(8,128)(2,1)S(1)}, bf16[512,3072]{1,0:T(8,128)(2,1)S(1)}, u32[]{:S(2)}, u32[]{:S(2)}) %collective-permute-start.19) | collective-permute-done | bytes 3145760 | tf_op jit(solution)/shard_map/ppermute | solution.py:97
  1141.1 18.1 %collective-permute-done.21 = bf16[128,3072]{1,0:T(8,128)(2,1)S(1)} collective-permute-done((bf16[128,3072]{1,0:T(8,128)(2,1)S(1)}, bf16[128,3072]{1,0:T(8,128)(2,1)S(1)}, u32[]{:S(2)}, u32[]{:S(2)}) %collective-permute-start.21) | collective-permute-done | bytes 786464 | tf_op jit(solution)/shard_map/ppermute | solution.py:103
  1160.2 31.7 %collective-permute-done.22 = bf16[128,3072]{1,0:T(8,128)(2,1)S(1)} collective-permute-done((bf16[128,3072]{1,0:T(8,128)(2,1)S(1)}, bf16[128,3072]{1,0:T(8,128)(2,1)S(1)}, u32[]{:S(2)}, u32[]{:S(2)}) %collective-permute-start.22) | collective-permute-done | bytes 786464 | tf_op jit(solution)/shard_map/ppermute | solution.py:103
  1239.7 18.3 %collective-permute-done.14 = bf16[512,1024]{1,0:T(8,128)(2,1)S(1)} collective-permute-done((bf16[512,1024]{1,0:T(8,128)(2,1)S(1)}, bf16[512,1024]{1,0:T(8,128)(2,1)S(1)}, u32[]{:S(2)}, u32[]{:S(2)}) %collective-permute-start.14) | collective-permute-done | bytes 1048608 | tf_op jit(solution)/shard_map/ppermute | solution.py:97
  1257.9 19.9 %collective-permute-done.13 = bf16[512,1024]{1,0:T(8,128)(2,1)S(1)} collective-permute-done((bf16[512,1024]{1,0:T(8,128)(2,1)S(1)}, bf16[512,1024]{1,0:T(8,128)(2,1)S(1)}, u32[]{:S(2)}, u32[]{:S(2)}) %collective-permute-start.13) | collective-permute-done | bytes 1048608 | tf_op jit(solution)/shard_map/ppermute | solution.py:97
  1281.1 15.8 %collective-permute-start.15 = (bf16[128,1024]{1,0:T(8,128)(2,1)}, bf16[128,1024]{1,0:T(8,128)(2,1)}, u32[]{:S(2)}, u32[]{:S(2)}) collective-permute-start(bf16[128,1024]{1,0:T(8,128)(2,1)} %get-tuple-element.68), channel_id=1, source_target_pairs={{0,2},{2,4},{4,6},{6,0},{1,3},{3,5},{5,7},{7,1},{8,10},{10,12},{12... | collective-permute-start | bytes 786440 | tf_op jit(solution)/shard_map/ppermute | solution.py:103
  (402 shorter events, 392.2 us)
Async XLA Ops:
  7.2 103.4 %all-gather.15.cloned.1.call-start = ((), (), s32[]{:S(2)}) async-start(), calls=%async_computation.12 | async-start | bytes 4718592 | tf_op jit(solution)/shard_map/all_gather | solution.py:52
  11.5 117.6 %all-gather.11.cloned.1.call-start = ((), (), s32[]{:S(2)}) async-start(), calls=%async_computation.8 | async-start | bytes 4718592 | tf_op jit(solution)/shard_map/all_gather | solution.py:52
  13.9 199.6 %reduce-scatter.13.cloned.1.call-start = ((), (), s32[]{:S(2)}) async-start(), calls=%async_computation.13 | async-start | bytes 4718592 | tf_op jit(solution)/shard_map/reduce_scatter | solution.py:56
  58.8 47.3 %collective-permute-start.4 = (bf16[4,128,1024]{2,1,0:T(8,128)(2,1)}, bf16[4,128,1024]{2,1,0:T(8,128)(2,1)}, u32[]{:S(2)}, u32[]{:S(2)}) collective-permute-start(bf16[4,128,1024]{2,1,0:T(8,128)(2,1)} %bitcast_dynamic-update-slice_fusion.18), channel_id=1, source_target_pairs={{0,16},{8,24},{16,0},{24,8},{1,17},{9,25},{17,1},{25,9},{2,18},{10... | collective-permute-start | bytes 3145736 | tf_op jit(solution)/shard_map/ppermute | solution.py:84
  60.3 48.1 %collective-permute-start.5 = (bf16[4,128,1024]{2,1,0:T(8,128)(2,1)}, bf16[4,128,1024]{2,1,0:T(8,128)(2,1)}, u32[]{:S(2)}, u32[]{:S(2)}) collective-permute-start(bf16[4,128,1024]{2,1,0:T(8,128)(2,1)} %bitcast_dynamic-update-slice_fusion.18), channel_id=1, source_target_pairs={{0,24},{8,16},{16,8},{24,0},{1,25},{9,17},{17,9},{25,1},{2,26},{10... | collective-permute-start | bytes 3145736 | tf_op jit(solution)/shard_map/ppermute | solution.py:84
  159.8 104.3 %reduce-scatter.9.cloned.1.call-start = ((), (), s32[]{:S(2)}) async-start(), calls=%async_computation.9 | async-start | bytes 4718592 | tf_op jit(solution)/shard_map/reduce_scatter | solution.py:56
  181.6 326.8 %all-gather.17.cloned.1.call-start = ((), (), s32[]{:S(2)}) async-start(), calls=%async_computation.14 | async-start | bytes 4718592 | tf_op jit(solution)/shard_map/all_gather | solution.py:52
  218.8 304.2 %all-gather.25.cloned.1.call-start = ((), (), s32[]{:S(2)}) async-start(), calls=%async_computation.21 | async-start | bytes 4718592 | tf_op jit(solution)/shard_map/all_gather | solution.py:52
  219.4 340.4 %all-gather.13.cloned.1.call-start = ((), (), s32[]{:S(2)}) async-start(), calls=%async_computation.10 | async-start | bytes 4718592 | tf_op jit(solution)/shard_map/all_gather | solution.py:52
  269.3 305.1 %all-gather.21.cloned.1.call-start = ((), (), s32[]{:S(2)}) async-start(), calls=%async_computation.17 | async-start | bytes 4718592 | tf_op jit(solution)/shard_map/all_gather | solution.py:52
  273.2 86.5 %collective-permute-start.7 = (bf16[128,3072]{1,0:T(8,128)(2,1)S(1)}, bf16[128,3072]{1,0:T(8,128)(2,1)S(1)}, u32[]{:S(2)}, u32[]{:S(2)}) collective-permute-start(bf16[128,3072]{1,0:T(8,128)(2,1)S(1)} %get-tuple-element.52), channel_id=1, source_target_pairs={{0,4},{2,6},{4,0},{6,2},{1,5},{3,7},{5,1},{7,3},{8,12},{10,14},{12... | collective-permute-start | bytes 2359304 | tf_op jit(solution)/shard_map/ppermute | solution.py:78
  274.4 86.2 %collective-permute-start.8 = (bf16[128,3072]{1,0:T(8,128)(2,1)S(1)}, bf16[128,3072]{1,0:T(8,128)(2,1)S(1)}, u32[]{:S(2)}, u32[]{:S(2)}) collective-permute-start(bf16[128,3072]{1,0:T(8,128)(2,1)S(1)} %get-tuple-element.51), channel_id=1, source_target_pairs={{0,6},{2,0},{4,2},{6,4},{1,7},{3,1},{5,3},{7,5},{8,14},{10,8},{12,... | collective-permute-start | bytes 2359304 | tf_op jit(solution)/shard_map/ppermute | solution.py:78
  361.6 71.3 %collective-permute-start.9 = (bf16[4,128,3072]{2,1,0:T(8,128)(2,1)}, bf16[4,128,3072]{2,1,0:T(8,128)(2,1)}, u32[]{:S(2)}, u32[]{:S(2)}) collective-permute-start(bf16[4,128,3072]{2,1,0:T(8,128)(2,1)} %bitcast_dynamic-update-slice_fusion.11), channel_id=1, source_target_pairs={{0,8},{8,0},{16,24},{24,16},{1,9},{9,1},{17,25},{25,17},{2,10},{10... | collective-permute-start | bytes 9437192 | tf_op jit(solution)/shard_map/ppermute | solution.py:84
  363.1 137.6 %collective-permute-start.10 = (bf16[4,128,3072]{2,1,0:T(8,128)(2,1)}, bf16[4,128,3072]{2,1,0:T(8,128)(2,1)}, u32[]{:S(2)}, u32[]{:S(2)}) collective-permute-start(bf16[4,128,3072]{2,1,0:T(8,128)(2,1)} %bitcast_dynamic-update-slice_fusion.11), channel_id=1, source_target_pairs={{0,16},{8,24},{16,0},{24,8},{1,17},{9,25},{17,1},{25,9},{2,18},{10... | collective-permute-start | bytes 9437192 | tf_op jit(solution)/shard_map/ppermute | solution.py:84
  364.6 139.9 %collective-permute-start.11 = (bf16[4,128,3072]{2,1,0:T(8,128)(2,1)}, bf16[4,128,3072]{2,1,0:T(8,128)(2,1)}, u32[]{:S(2)}, u32[]{:S(2)}) collective-permute-start(bf16[4,128,3072]{2,1,0:T(8,128)(2,1)} %bitcast_dynamic-update-slice_fusion.11), channel_id=1, source_target_pairs={{0,24},{8,16},{16,8},{24,0},{1,25},{9,17},{17,9},{25,1},{2,26},{10... | collective-permute-start | bytes 9437192 | tf_op jit(solution)/shard_map/ppermute | solution.py:84
  375.5 247.6 %reduce-scatter.21.cloned.1.call-start = ((), (), s32[]{:S(2)}) async-start(), calls=%async_computation.22 | async-start | bytes 4718592 | tf_op jit(solution)/shard_map/reduce_scatter | solution.py:56
  549.8 123.8 %reduce-scatter.15.cloned.1.call-start = ((), (), s32[]{:S(2)}) async-start(), calls=%async_computation.15 | async-start | bytes 4718592 | tf_op jit(solution)/shard_map/reduce_scatter | solution.py:56
  559.3 165.1 %reduce-scatter.17.cloned.1.call-start = ((), (), s32[]{:S(2)}) async-start(), calls=%async_computation.18 | async-start | bytes 4718592 | tf_op jit(solution)/shard_map/reduce_scatter | solution.py:56
  601.1 173.8 %reduce-scatter.11.cloned.1.call-start = ((), (), s32[]{:S(2)}) async-start(), calls=%async_computation.11 | async-start | bytes 4718592 | tf_op jit(solution)/shard_map/reduce_scatter | solution.py:56
  611.0 210.9 %all-gather.27.cloned.1.call-start = ((), (), s32[]{:S(2)}) async-start(), calls=%async_computation.23 | async-start | bytes 4718592 | tf_op jit(solution)/shard_map/all_gather | solution.py:52
  677.2 191.9 %all-gather.23.cloned.1.call-start = ((), (), s32[]{:S(2)}) async-start(), calls=%async_computation.19 | async-start | bytes 4718592 | tf_op jit(solution)/shard_map/all_gather | solution.py:52
  778.5 432.3 %reduce-scatter.23.cloned.1.call-start = ((), (), s32[]{:S(2)}) async-start(), calls=%async_computation.24 | async-start | bytes 4718592 | tf_op jit(solution)/shard_map/reduce_scatter | solution.py:56
  894.6 317.7 %reduce-scatter.19.cloned.1.call-start = ((), (), s32[]{:S(2)}) async-start(), calls=%async_computation.20 | async-start | bytes 4718592 | tf_op jit(solution)/shard_map/reduce_scatter | solution.py:56
  952.1 361.8 %all-gather.19.cloned.1.call-start = ((), (), s32[]{:S(2)}) async-start(), calls=%async_computation.16 | async-start | bytes 3145728 | tf_op jit(solution)/shard_map/all_gather | solution.py:213
  990.1 72.1 %collective-permute-start.20 = (bf16[512,3072]{1,0:T(8,128)(2,1)}, bf16[512,3072]{1,0:T(8,128)(2,1)S(1)}, u32[]{:S(2)}, u32[]{:S(2)}) collective-permute-start(bf16[512,3072]{1,0:T(8,128)(2,1)} %get-tuple-element.31), channel_id=1, source_target_pairs={{0,24},{8,16},{16,8},{24,0},{1,25},{9,17},{17,9},{25,1},{2,26},{10... | collective-permute-start | bytes 9437192 | tf_op jit(solution)/shard_map/ppermute | solution.py:97
  992.6 136.3 %collective-permute-start.19 = (bf16[512,3072]{1,0:T(8,128)(2,1)S(1)}, bf16[512,3072]{1,0:T(8,128)(2,1)S(1)}, u32[]{:S(2)}, u32[]{:S(2)}) collective-permute-start(bf16[512,3072]{1,0:T(8,128)(2,1)S(1)} %get-tuple-element.32), channel_id=1, source_target_pairs={{0,16},{8,24},{16,0},{24,8},{1,17},{9,25},{17,1},{25,9},{2,18},{10... | collective-permute-start | bytes 9437192 | tf_op jit(solution)/shard_map/ppermute | solution.py:97
  993.1 135.9 %collective-permute-start.18 = (bf16[512,3072]{1,0:T(8,128)(2,1)S(1)}, bf16[512,3072]{1,0:T(8,128)(2,1)S(1)}, u32[]{:S(2)}, u32[]{:S(2)}) collective-permute-start(bf16[512,3072]{1,0:T(8,128)(2,1)S(1)} %get-tuple-element.30), channel_id=1, source_target_pairs={{0,8},{8,0},{16,24},{24,16},{1,9},{9,1},{17,25},{25,17},{2,10},{10... | collective-permute-start | bytes 9437192 | tf_op jit(solution)/shard_map/ppermute | solution.py:97
  1137.3 54.7 %collective-permute-start.22 = (bf16[128,3072]{1,0:T(8,128)(2,1)S(1)}, bf16[128,3072]{1,0:T(8,128)(2,1)S(1)}, u32[]{:S(2)}, u32[]{:S(2)}) collective-permute-start(bf16[128,3072]{1,0:T(8,128)(2,1)S(1)} %get-tuple-element.46), channel_id=1, source_target_pairs={{0,4},{2,6},{4,0},{6,2},{1,5},{3,7},{5,1},{7,3},{8,12},{10,14},{12... | collective-permute-start | bytes 2359304 | tf_op jit(solution)/shard_map/ppermute | solution.py:103
  1139.1 95.4 %collective-permute-start.23 = (bf16[128,3072]{1,0:T(8,128)(2,1)}, bf16[128,3072]{1,0:T(8,128)(2,1)}, u32[]{:S(2)}, u32[]{:S(2)}) collective-permute-start(bf16[128,3072]{1,0:T(8,128)(2,1)} %get-tuple-element.45), channel_id=1, source_target_pairs={{0,6},{2,0},{4,2},{6,4},{1,7},{3,1},{5,3},{7,5},{8,14},{10,8},{12,... | collective-permute-start | bytes 2359304 | tf_op jit(solution)/shard_map/ppermute | solution.py:103
  1194.0 138.8 %all-gather.29.cloned.1.call-start = ((), (), s32[]{:S(2)}) async-start(), calls=%async_computation.25 | async-start | bytes 6291456 | tf_op jit(solution)/shard_map/all_gather | solution.py:214
  1232.0 45.9 %collective-permute-start.13 = (bf16[512,1024]{1,0:T(8,128)(2,1)S(1)}, bf16[512,1024]{1,0:T(8,128)(2,1)S(1)}, u32[]{:S(2)}, u32[]{:S(2)}) collective-permute-start(bf16[512,1024]{1,0:T(8,128)(2,1)S(1)} %get-tuple-element.44), channel_id=1, source_target_pairs={{0,16},{8,24},{16,0},{24,8},{1,17},{9,25},{17,1},{25,9},{2,18},{10... | collective-permute-start | bytes 3145736 | tf_op jit(solution)/shard_map/ppermute | solution.py:97
  1234.0 44.0 %collective-permute-start.12 = (bf16[512,1024]{1,0:T(8,128)(2,1)S(1)}, bf16[512,1024]{1,0:T(8,128)(2,1)S(1)}, u32[]{:S(2)}, u32[]{:S(2)}) collective-permute-start(bf16[512,1024]{1,0:T(8,128)(2,1)S(1)} %get-tuple-element.42), channel_id=1, source_target_pairs={{0,8},{8,0},{16,24},{24,16},{1,9},{9,1},{17,25},{25,17},{2,10},{10... | collective-permute-start | bytes 3145736 | tf_op jit(solution)/shard_map/ppermute | solution.py:97
  (91 other events, 2573.5 us)
Sparse Core Ops, SparseCore 0:
  11.6 68.9 all-gather.14
  82.8 46.2 all-gather.10
  159.9 53.5 reduce-scatter.12
  215.7 48.3 reduce-scatter.8
  266.1 95.0 all-gather.16
  363.2 48.5 all-gather.24
  414.0 46.2 all-gather.12
  462.4 45.6 all-gather.20
  549.9 73.1 reduce-scatter.20
  625.2 48.3 reduce-scatter.14
  675.9 48.4 reduce-scatter.16
  726.5 48.3 reduce-scatter.10
  776.5 45.3 all-gather.26
  823.3 45.6 all-gather.22
  894.7 48.7 reduce-scatter.22
  952.2 48.6 reduce-scatter.18
  1194.1 24.3 all-gather.18
  1220.5 24.8 all-gather.28

commit v3 on v2

v3 whole, which is shorter than its diff:
```python
import math

import jax
import jax.numpy as jnp
from jax import lax
from jax.sharding import PartitionSpec as P

HEAD_DIM = 128
SEQUENCE_ROWS = ("context", "tensor")
PLANE_ROWS = ("dp", "tensor")


def rope_tables(positions, head_dim):
    half_dim = head_dim // 2
    inverse_freq = jnp.exp(
        -math.log(10000.0) * jnp.arange(half_dim, dtype=jnp.float32) * 2.0 / head_dim
    )
    angles = positions.astype(jnp.float32)[:, None] * inverse_freq[None, :]
    angles = jnp.concatenate([angles, angles], axis=-1)
    return (jnp.cos(angles)[:, None, :], jnp.sin(angles)[:, None, :])


def rotate(values, cosine, sine):
    half_dim = values.shape[-1] // 2
    turned = jnp.concatenate([-values[..., half_dim:], values[..., :half_dim]], axis=-1)
    return values * cosine + turned * sine


def unrotate(upstream, cosine, sine):
    half_dim = upstream.shape[-1] // 2
    scaled = upstream * sine
    turned = jnp.concatenate([scaled[..., half_dim:], -scaled[..., :half_dim]], axis=-1)
    return upstream * cosine + turned


def normalize(values):
    centered = values - jnp.mean(values, axis=-1, keepdims=True)
    inverse = lax.rsqrt(jnp.mean(centered * centered, axis=-1, keepdims=True) + 1e-05)
    return (centered * inverse, inverse)


def normalize_back(normed, inverse, upstream):
    mean_grad = jnp.mean(upstream, axis=-1, keepdims=True)
    mean_cross = jnp.mean(upstream * normed, axis=-1, keepdims=True)
    return inverse * (upstream - mean_grad - normed * mean_cross)


def dot(left, right, dims):
    return lax.dot_general(left, right, (dims, ((), ())), preferred_element_type=jnp.float32)


def gather_rows(values, axes):
    return lax.all_gather(values, axes, axis=0, tiled=True)


def scatter_rows(values, axes):
    return lax.psum_scatter(values.astype(jnp.bfloat16), axes, scatter_dimension=0, tiled=True).astype(
        jnp.float32
    )


def join_cores(values):
    cores = lax.axis_size("tensor")
    core, rows = lax.axis_index("tensor"), values.shape[1]
    whole = jnp.concatenate([values] * cores, axis=1)
    for step in range(1, cores):
        route = [(i, (i + step) % cores) for i in range(cores)]
        other = lax.ppermute(values, "tensor", route)
        whole = lax.dynamic_update_slice_in_dim(whole, other, ((core - step) % cores) * rows, 1)
    return whole


def put(buffer, piece, index):
    return lax.dynamic_update_slice_in_dim(buffer, piece[None], index, 0)


def take(buffer, index):
    return lax.dynamic_index_in_dim(buffer, index, 0, keepdims=False)


def spread_weight(weight):
    rows, contexts, columns = weight.shape
    groups = lax.axis_size("dp")
    here, group = lax.axis_index("context"), lax.axis_index("dp")
    pieces = jnp.moveaxis(weight, 1, 0)
    mine = jnp.zeros((contexts, rows, columns), weight.dtype)
    mine = put(mine, take(pieces, here), here)
    for step in range(1, contexts):
        route = [(i, (i + step) % contexts) for i in range(contexts)]
        piece = lax.ppermute(take(pieces, (here + step) % contexts), "context", route)
        mine = put(mine, piece, (here - step) % contexts)
    whole = jnp.zeros((groups,) + mine.shape, weight.dtype)
    whole = put(whole, mine, group)
    for step in range(1, groups):
        route = [(i, i ^ step) for i in range(groups)]
        whole = put(whole, lax.ppermute(mine, "dp", route), group ^ step)
    return whole.reshape(groups * contexts * rows, columns)


def collect_pieces(partial, contexts):
    groups = lax.axis_size("dp")
    group = lax.axis_index("dp")
    columns = partial.shape[1]
    rows = partial.shape[0] // (groups * contexts)
    parts = partial.reshape(groups, contexts * rows, columns)
    total = take(parts, group).astype(jnp.float32)
    for step in range(1, groups):
        route = [(i, i ^ step) for i in range(groups)]
        total = total + lax.ppermute(take(parts, group ^ step), "dp", route).astype(jnp.float32)
    return swap(total.astype(jnp.bfloat16).reshape(contexts, rows, columns), "context")


def swap(pieces, axis):
    members, here = lax.axis_size(axis), lax.axis_index(axis)
    arrived = [take(pieces, here)]
    for step in range(1, members):
        route = [(i, i ^ step) for i in range(members)]
        arrived.append(lax.ppermute(take(pieces, here ^ step), axis, route))
    return arrived


def exchange(pieces, axis):
    here = lax.axis_index(axis)
    mine = jnp.zeros_like(pieces)
    for step, piece in enumerate(swap(pieces, axis)):
        mine = put(mine, piece, here ^ step)
    return mine


def relay_hops(block):
    n = lax.axis_size("context")
    up, down = [], []
    moving_up = moving_down = block
    for step in range(1, n):
        moving_up = lax.ppermute(moving_up, "context", [(i, i + 1) for i in range(step - 1, n - 1)])
        moving_down = lax.ppermute(moving_down, "context", [(i, i - 1) for i in range(1, n - step + 1)])
        up.append(moving_up)
        down.append(moving_down)
    return up, down


def hold(value, hops, index):
    up, down = hops
    if index < len(up):
        value, up[index], down[index] = lax.optimization_barrier((value, up[index], down[index]))
    return value


def assemble(block, hops):
    n, here = lax.axis_size("context"), lax.axis_index("context")
    up, down = hops
    groups, rows, columns = block.shape
    whole = jnp.zeros((groups, n, rows, columns), block.dtype)
    whole = lax.dynamic_update_slice_in_dim(whole, block[:, None], here, 1)
    for step in range(1, n):
        piece = jnp.where(here >= step, up[step - 1], down[n - step - 1])
        whole = lax.dynamic_update_slice_in_dim(whole, piece[:, None], (here - step) % n, 1)
    return whole.reshape(-1, columns)


def scatter_plane(values):
    low = jnp.bfloat16
    cores, groups = lax.axis_size("tensor"), lax.axis_size("dp")
    core, group = lax.axis_index("tensor"), lax.axis_index("dp")
    width = values.shape[1]
    parts = values.astype(low).reshape(groups, cores, -1, width)

    def of_core(index):
        return lax.dynamic_index_in_dim(parts, index % cores, 1, keepdims=False)

    total = of_core(core).astype(jnp.float32)
    for step in range(1, cores):
        route = [(i, (i + step) % cores) for i in range(cores)]
        total = total + lax.ppermute(of_core(core + step), "tensor", route).astype(jnp.float32)
    total = total.astype(low)
    bits = list(range(groups.bit_length() - 1))
    results = []
    for part, order in enumerate((bits, bits[::-1])):
        half = width // 2
        block = total[:, :, part * half : (part + 1) * half]
        rows = block.shape[1]
        block = block.reshape((2,) * len(bits) + (rows, half))
        left = bits[::-1]
        for bit in order:
            axis, mine = left.index(bit), (group >> bit) & 1
            keep = lax.dynamic_index_in_dim(block, mine, axis, keepdims=False)
            send = lax.dynamic_index_in_dim(block, 1 - mine, axis, keepdims=False)
            route = [(i, i ^ (1 << bit)) for i in range(groups)]
            other = lax.ppermute(send, "dp", route)
            block = keep.astype(jnp.float32) + other.astype(jnp.float32)
            left.remove(bit)
            if left:
                block = block.astype(low)
        results.append(block)
    return jnp.concatenate(results, axis=1)


class Reduction:
    def __init__(self, partial, groups, contexts):
        self.parts = partial.reshape(groups, contexts, -1, partial.shape[1])
        self.n, self.here = contexts, lax.axis_index("context")
        self.above = self.below = None
        self.step = 0

    def term(self, index):
        picked = lax.dynamic_index_in_dim(self.parts, index % self.n, 1, keepdims=False)
        return picked.astype(jnp.float32)

    def hop(self):
        if self.step == self.n - 1:
            return
        self.step += 1
        step, n = self.step, self.n
        above, below = self.term(self.here - step), self.term(self.here + step)
        if self.above is not None:
            above, below = above + self.above.astype(jnp.float32), below + self.below.astype(jnp.float32)
        self.above = lax.ppermute(
            above.astype(jnp.bfloat16), "context", [(i, i + 1) for i in range(min(step, n - 1))]
        )
        self.below = lax.ppermute(
            below.astype(jnp.bfloat16), "context", [(i, i - 1) for i in range(max(1, n - step), n)]
        )

    def hold(self, value):
        value, self.above, self.below = lax.optimization_barrier((value, self.above, self.below))
        return value

    def finish(self):
        while self.step < self.n - 1:
            self.hop()
        total = self.term(self.here) + self.above.astype(jnp.float32) + self.below.astype(jnp.float32)
        return swap(total.astype(jnp.bfloat16), "dp")


def per_device(tokens, lengths, w_query, w_key, w_value, w_out, w_gate, w_up, w_down, cotangent):
    low = jnp.bfloat16
    slots, chip_rows, width = tokens.shape
    contexts, cores = lax.axis_size("context"), lax.axis_size("tensor")
    rows = chip_rows // cores
    seq = chip_rows * contexts
    head_cols = w_query.shape[1] // contexts
    groups = lax.axis_size("dp")
    units = w_gate.shape[1] // groups
    heads = head_cols // HEAD_DIM
    scale = 1.0 / math.sqrt(HEAD_DIM)
    core = lax.axis_index("tensor")
    own_start = lax.axis_index("context") * chip_rows + core * rows
    own_positions = own_start + jnp.arange(rows, dtype=jnp.int32)
    positions = jnp.arange(seq, dtype=jnp.int32)
    rope_cos, rope_sin = rope_tables(positions, HEAD_DIM)
    causal = positions[None, :] <= positions[:, None]

    def by_context(weight):
        return weight.reshape(weight.shape[0], contexts, -1)

    attention_w = spread_weight(
        jnp.concatenate([by_context(w) for w in (w_query, w_key, w_value, w_out.T)], axis=2)
    )
    qkv_w, out_w = attention_w[:, : 3 * head_cols], attention_w[:, 3 * head_cols :]

    def by_group(weight):
        return jnp.moveaxis(weight.reshape(weight.shape[0], groups, -1), 1, 0)

    gate_up_block = exchange(jnp.concatenate([by_group(w_gate), by_group(w_up)], axis=2), "dp")
    down_block = exchange(by_group(w_down.T), "dp")

    def einsum(form, left, right):
        return jnp.einsum(form, left, right, preferred_element_type=jnp.float32)

    def split(values):
        return values.reshape(seq, heads, HEAD_DIM)

    def own(array, slot):
        return lax.dynamic_slice_in_dim(array[slot], core * rows, rows, 0).astype(jnp.float32)

    each = range(slots)
    own_tokens = [own(tokens, slot) for slot in each]
    valid_rows = [(own_positions < lengths[slot]).astype(jnp.float32)[:, None] for slot in each]
    allowed = [(causal & (positions < lengths[slot])[None, :])[None] for slot in each]
    out_grad = [own(cotangent, slot) * valid_rows[slot] for slot in each]
    ffn_grad = [(valid_rows[slot] * out_grad[slot]).astype(low) for slot in each]
    norm_one, inverse_one = zip(*[normalize(own_tokens[slot]) for slot in each])
    norm_one_all = [gather_rows(norm_one[slot].astype(low), SEQUENCE_ROWS) for slot in each]

    norm_one_all[0], gate_up_block, down_block = lax.optimization_barrier(
        (norm_one_all[0], gate_up_block, down_block)
    )
    gate_up_hops, down_hops = relay_hops(gate_up_block), relay_hops(down_block)
    last = slots - 1
    norm_one_all[last], *ffn_grad = lax.optimization_barrier((norm_one_all[last], *ffn_grad))
    ffn_grad_all = [gather_rows(ffn_grad[slot], PLANE_ROWS) for slot in each]
    norm_one_all[last] = hold(norm_one_all[last], gate_up_hops, 0)

    def attend(slot):
        qkv = dot(norm_one_all[slot], qkv_w, ((1,), (0,)))
        query, key, value = (qkv[:, i * head_cols : (i + 1) * head_cols] for i in range(3))
        query = rotate(split(query), rope_cos, rope_sin).astype(low)
        key = rotate(split(key), rope_cos, rope_sin).astype(low)
        value = split(value.astype(low))
        scores = einsum("qhd,khd->hqk", query, key) * scale
        masked = jnp.where(allowed[slot], scores, -1e30)
        row_top = jnp.max(masked, axis=-1, keepdims=True)
        exponent = jnp.where(allowed[slot], jnp.exp(masked - row_top), 0.0)
        probabilities = exponent / jnp.sum(exponent, axis=-1, keepdims=True)
        attended = einsum("hqk,khd->qhd", probabilities.astype(low), value)
        attended = attended.reshape(seq, heads * HEAD_DIM).astype(low)
        return query, key, value, probabilities, attended

    saved, branch = [], []
    for slot in each:
        kept = attend(slot)
        attended = kept[4]
        if slot == 0:
            attended, *ffn_grad_all = lax.optimization_barrier((attended, *ffn_grad_all))
        if slot == last:
            attended = hold(attended, gate_up_hops, 1)
        saved.append(kept[:4] + (attended,))
        branch.append(scatter_rows(dot(attended, out_w, ((1,), (1,))), SEQUENCE_ROWS))
    middle, norm_two, inverse_two, norm_two_all = [], [], [], []
    for slot in each:
        summed_branch = branch[slot]
        if slot == 0:
            summed_branch = hold(summed_branch, gate_up_hops, 2)
        if slot == last:
            summed_branch = hold(summed_branch, down_hops, 0)
        middle.append(own_tokens[slot] + valid_rows[slot] * summed_branch)
        normed, inverse = normalize(middle[slot])
        norm_two.append(normed)
        inverse_two.append(inverse)
        norm_two_all.append(gather_rows(normed.astype(low), PLANE_ROWS))
    for slot in each:
        norm_two_all[slot] = hold(norm_two_all[slot], down_hops, 1 + slot)
    gate_up_w, down_w = assemble(gate_up_block, gate_up_hops), assemble(down_block, down_hops)

    hidden, gate_up_grad, norm_two_grad = [], [], []
    for slot in each:
        gate_up = dot(norm_two_all[slot], gate_up_w, ((1,), (0,)))
        gate, upper = gate_up[:, :units], gate_up[:, units:]
        sigmoid = jax.nn.sigmoid(gate)
        silu = gate * sigmoid
        hidden.append((silu * upper).astype(low))
        hidden_grad = dot(ffn_grad_all[slot], down_w, ((1,), (0,)))
        gate_grad = (hidden_grad * upper * sigmoid * (1.0 + gate * (1.0 - sigmoid))).astype(low)
        upper_grad = (hidden_grad * silu).astype(low)
        gate_up_grad.append(jnp.concatenate([gate_grad, upper_grad], axis=1))
        norm_two_grad.append(scatter_plane(dot(gate_up_grad[slot], gate_up_w, ((1,), (1,)))))

    def over_slots(terms):
        total = terms[0]
        for other in terms[1:]:
            total = total + other
        return total.astype(low)

    down_sum = over_slots([dot(ffn_grad_all[slot], hidden[slot], ((0,), (0,))) for slot in each])
    down_sum = Reduction(down_sum, groups, contexts)
    gate_up_sum = over_slots([dot(norm_two_all[slot], gate_up_grad[slot], ((0,), (0,))) for slot in each])
    gate_up_sum = Reduction(gate_up_sum, groups, contexts)

    middle_grad, branch_grad_all = [], []
    for slot in each:
        upstream = norm_two_grad[slot]
        if slot == last:
            down_sum.hop()
            upstream = down_sum.hold(upstream)
        middle_grad.append(
            out_grad[slot] + normalize_back(norm_two[slot], inverse_two[slot], upstream)
        )
        branch_grad_all.append(
            gather_rows((valid_rows[slot] * middle_grad[slot]).astype(low), SEQUENCE_ROWS)
        )
    down_sum.hop()
    branch_grad_all[0] = down_sum.hold(branch_grad_all[0])
    down_sum.hop()
    gate_up_sum.hop()
    branch_grad_all[last] = down_sum.hold(gate_up_sum.hold(branch_grad_all[last]))
    branch_grad_all[last], *hidden_late = lax.optimization_barrier((branch_grad_all[last], *hidden))

    qkv_grad, norm_one_grad = [], []
    for slot in each:
        query, key, value, probabilities, attended = saved[slot]
        attended_grad = split(dot(branch_grad_all[slot], out_w, ((1,), (0,))).astype(low))
        prob_grad = einsum("qhd,khd->hqk", attended_grad, value)
        row_delta = jnp.sum(probabilities * prob_grad, axis=-1, keepdims=True)
        score_grad = (probabilities * (prob_grad - row_delta)).astype(low)
        query_grad = einsum("hqk,khd->qhd", score_grad, key) * scale
        key_grad = einsum("hqk,qhd->khd", score_grad, query) * scale
        value_grad = einsum("hqk,qhd->khd", probabilities.astype(low), attended_grad)
        qkv_grad.append(
            jnp.concatenate(
                [
                    unrotate(query_grad, rope_cos, rope_sin).astype(low).reshape(seq, -1),
                    unrotate(key_grad, rope_cos, rope_sin).astype(low).reshape(seq, -1),
                    value_grad.astype(low).reshape(seq, -1),
                ],
                axis=1,
            )
        )
        if slot == last:
            gate_up_sum.hop()
            qkv_grad[slot] = gate_up_sum.hold(qkv_grad[slot])
        norm_one_grad.append(
            scatter_rows(dot(qkv_grad[slot], qkv_w, ((1,), (1,))), SEQUENCE_ROWS)
        )
    out_sum = over_slots([dot(branch_grad_all[slot], saved[slot][4], ((0,), (0,))) for slot in each])
    qkv_sum = over_slots([dot(norm_one_all[slot], qkv_grad[slot], ((0,), (0,))) for slot in each])

    layer_out, input_grad = [], []
    for slot in each:
        feedforward = scatter_plane(dot(hidden_late[slot], down_w, ((1,), (1,))))
        layer_out.append((middle[slot] + valid_rows[slot] * feedforward).astype(low))
    gate_up_sum.hop()
    norm_one_grad[0] = gate_up_sum.hold(norm_one_grad[0])
    down_pieces = down_sum.finish()
    norm_one_grad[last], *rest = lax.optimization_barrier((norm_one_grad[last], *layer_out, *down_pieces))
    layer_out, down_pieces = rest[:slots], rest[slots:]
    for slot in each:
        upstream = norm_one_grad[slot]
        input_grad.append(
            middle_grad[slot] + normalize_back(norm_one[slot], inverse_one[slot], upstream)
        )
    layer_out, input_grad = join_cores(jnp.stack(layer_out)), join_cores(jnp.stack(input_grad))

    gate_up_pieces = gate_up_sum.finish()
    out_pieces = collect_pieces(out_sum, contexts)
    qkv_pieces = collect_pieces(qkv_sum, contexts)

    def column_output(pieces, axis, start, size):
        members, here = lax.axis_size(axis), lax.axis_index(axis)
        whole = jnp.zeros((pieces[0].shape[0], members * size), jnp.float32)
        for step, piece in enumerate(pieces):
            block = piece[:, start : start + size].astype(jnp.float32)
            whole = lax.dynamic_update_slice_in_dim(whole, block, (here ^ step) * size, 1)
        return whole

    def row_output(pieces, axis, size):
        members, here = lax.axis_size(axis), lax.axis_index(axis)
        whole = jnp.zeros((members * size, pieces[0].shape[0]), jnp.float32)
        for step, piece in enumerate(pieces):
            block = piece.astype(jnp.float32).T
            whole = lax.dynamic_update_slice_in_dim(whole, block, (here ^ step) * size, 0)
        return whole

    grads = tuple(column_output(qkv_pieces, "context", i * head_cols, head_cols) for i in range(3)) + (
        row_output(out_pieces, "context", head_cols),
        column_output(gate_up_pieces, "dp", 0, units),
        column_output(gate_up_pieces, "dp", units, units),
        row_output(down_pieces, "dp", units),
    )
    return (layer_out, input_grad) + grads


def solution(mesh):
    tokens = P("dp", "context", None)
    column = P(("dp", "context"), "tensor")
    row = P("tensor", ("dp", "context"))
    weights = (column, column, column, row, column, column, row)
    return jax.shard_map(
        per_device,
        mesh=mesh,
        in_specs=(tokens, P("dp")) + weights + (tokens,),
        out_specs=(tokens, tokens) + weights,
        check_vma=False,
    )
```

time: 1350 us -> 1170 us (0.87)
  waiting for transfers between devices: 806 us -> 523 us
  starting transfers between devices: 50 us -> 132 us
  other arithmetic: 78.9 us -> 111 us
  local copies, waits for them, and re-layouts: 146 us -> 125 us
    ppermute x6 -> x3, waiting for transfers between devices: 158 us -> 43.5 us  [spread_weight(): whole = put(whole, lax.ppermute(mine, 'dp', route), group ^ step)]
    reduce_scatter x8 -> x4, waiting for transfers between devices: 230 us -> 118 us  [scatter_rows(): lax.psum_scatter(values.astype(jnp.bfloat16), axes, scatter_dimension=0,...]
    ppermute x6 -> x3, waiting for transfers between devices: 104 us -> 0.01 us  [spread_weight(): lax.ppermute(take(pieces, (here + step) % contexts), 'context', route)]
    ppermute x12 -> x70, starting transfers between devices: 30.8 us -> 124 us  [the longest x6 38.5 us: hop(): lax.ppermute(above.astype(jnp.bfloat16), 'context', [(i, i + 1) for i in...]
    ppermute x12 -> x70, waiting for transfers between devices: 231 us -> 304 us  [the longest x18 128 us: swap(): arrived.append(lax.ppermute(take(pieces, here ^ step), axis, route))]
    convert_element_type x16 -> x39, other arithmetic: 34 us -> 63.1 us  [the longest x4 23.5 us: hop(): below.astype(jnp.bfloat16)]
    dynamic_update_slice x0 -> x21, other arithmetic: none -> 27.4 us  [the longest x6 18.2 us: assemble(): lax.dynamic_update_slice_in_dim(whole, piece[:, None], (here - step) % n, 1)]
    all_gather x10 -> x8, waiting for transfers between devices: 82.8 us -> 57 us  [gather_rows(): return lax.all_gather(values, axes, axis=0, tiled=True)]
  transfers between devices with their start and end apart: 42 -> 88, of which waited for: 27 -> 39; matrix products, arithmetic and copies ran while one was open for 29% -> 36% of each run, Pallas kernels for 0% -> 0%
where the time goes in v3:
time: 1170 us; the launch traced here: 1160 us
  waiting for transfers between devices  523 us (45%)
  matrix products  247 us (21%)
  starting transfers between devices  132 us (11%)
  local copies, waits for them, and re-layouts  125 us (11%)
  other arithmetic  111 us (9%)
  between operations  16.9 us (1%)
    dot_general x24, matrix products, dot(): lax.dot_general(left, right, (dims, ((), ())), preferred_element_type=jnp...  204 us
    ppermute x18, waiting for transfers between devices, swap(): arrived.append(lax.ppermute(take(pieces, here ^ step), axis, route))  128 us
    reduce_scatter x4, waiting for transfers between devices, scatter_rows(): lax.psum_scatter(values.astype(jnp.bfloat16), axes, scatter_dimension=0,...  118 us
    ppermute x6, waiting for transfers between devices, relay_hops(): lax.ppermute(moving_down, 'context', [(i, i - 1) for i in range(1, n - st...  63.9 us
    ppermute x6, waiting for transfers between devices, hop(): lax.ppermute(above.astype(jnp.bfloat16), 'context', [(i, i + 1) for i in...  62.1 us
    all_gather x8, waiting for transfers between devices, gather_rows(): return lax.all_gather(values, axes, axis=0, tiled=True)  57 us
    ppermute x16, waiting for transfers between devices, scatter_plane(): other = lax.ppermute(send, 'dp', route)  48.1 us
    ppermute x3, waiting for transfers between devices, spread_weight(): whole = put(whole, lax.ppermute(mine, 'dp', route), group ^ step)  43.5 us
  transfers between devices with their start and end apart: 88, of which 39 were waited for; matrix products, arithmetic and copies ran while one was open for 36% of the time, Pallas kernels for 0%

profile of v3, /device:TPU:0, one launch (start us, length us, event | category | flops | bytes accessed | tf_op | source)
XLA Modules:
  0.0 1155.3 jit_solution(3441711448766385651)
XLA Ops:
  20.5 40.7 %all-gather.9.cloned.1.call-done = bf16[1024,2048]{1,0:T(8,128)(2,1)} async-done(((bf16[128,2048]{1,0:T(8,128)(2,1)}), bf16[1024,2048]{1,0:T(8,128)(2,1)}) %all-gather.9.cloned.1.call-update) | async-done | bytes 4194320 | tf_op jit(solution)/shard_map/all_gather | solution.py:53
  119.9 29.1 %collective-permute-done.4 = bf16[128,1024]{1,0:T(8,128)(2,1)S(1)} collective-permute-done((bf16[128,1024]{1,0:T(8,128)(2,1)S(1)}, bf16[128,1024]{1,0:T(8,128)(2,1)S(1)}, u32[]{:S(2)}, u32[]{:S(2)}) %collective-permute-start.4) | collective-permute-done | bytes 262176 | tf_op jit(solution)/shard_map/ppermute | solution.py:118
  164.4 22.1 %collective-permute-done.11 = bf16[4,128,1024]{2,1,0:T(8,128)(2,1)} collective-permute-done((bf16[4,128,1024]{2,1,0:T(8,128)(2,1)}, bf16[4,128,1024]{2,1,0:T(8,128)(2,1)}, u32[]{:S(2)}, u32[]{:S(2)}) %collective-permute-start.11) | collective-permute-done | bytes 1048608 | tf_op jit(solution)/shard_map/ppermute | solution.py:96
  193.3 21.4 %collective-permute-done.12 = bf16[4,128,1024]{2,1,0:T(8,128)(2,1)S(1)} collective-permute-done((bf16[4,128,1024]{2,1,0:T(8,128)(2,1)}, bf16[4,128,1024]{2,1,0:T(8,128)(2,1)S(1)}, u32[]{:S(2)}, u32[]{:S(2)}) %collective-permute-start.12) | collective-permute-done | bytes 1048608 | tf_op jit(solution)/shard_map/ppermute | solution.py:96
  239.9 9.6 fusion.172
  253.9 30.6 %collective-permute-done.15 = bf16[4,128,2048]{2,1,0:T(8,128)(2,1)} collective-permute-done((bf16[4,128,2048]{2,1,0:T(8,128)(2,1)}, bf16[4,128,2048]{2,1,0:T(8,128)(2,1)}, u32[]{:S(2)}, u32[]{:S(2)}) %collective-permute-start.15) | collective-permute-done | bytes 2097184 | tf_op jit(solution)/shard_map/ppermute | solution.py:136
  293.8 7.7 fusion.171
  316.6 41.4 %reduce-scatter.5.cloned.1.call-done = bf16[128,2048]{1,0:T(8,128)(2,1)} async-done(((bf16[1024,2048]{1,0:T(8,128)(2,1)}), bf16[128,2048]{1,0:T(8,128)(2,1)}) %reduce-scatter.5.cloned.1.call-update) | async-done | bytes 524304 | tf_op jit(solution)/shard_map/reduce_scatter | solution.py:57
  363.7 76.6 %reduce-scatter.7.cloned.1.call-done = bf16[128,2048]{1,0:T(8,128)(2,1)} async-done(((bf16[1024,2048]{1,0:T(8,128)(2,1)}), bf16[128,2048]{1,0:T(8,128)(2,1)}) %reduce-scatter.7.cloned.1.call-update) | async-done | bytes 524304 | tf_op jit(solution)/shard_map/reduce_scatter | solution.py:57
  466.6 13.1 %collective-permute-done.20 = bf16[4,128,1024]{2,1,0:T(8,128)(2,1)} collective-permute-done((bf16[4,128,1024]{2,1,0:T(8,128)(2,1)}, bf16[4,128,1024]{2,1,0:T(8,128)(2,1)}, u32[]{:S(2)}, u32[]{:S(2)}) %collective-permute-start.20) | collective-permute-done | bytes 1048608 | tf_op jit(solution)/shard_map/ppermute | solution.py:136
  493.6 12.2 %collective-permute-done.21 = bf16[4,128,1024]{2,1,0:T(8,128)(2,1)} collective-permute-done((bf16[4,128,1024]{2,1,0:T(8,128)(2,1)}, bf16[4,128,1024]{2,1,0:T(8,128)(2,1)}, u32[]{:S(2)}, u32[]{:S(2)}) %collective-permute-start.21) | collective-permute-done | bytes 1048608 | tf_op jit(solution)/shard_map/ppermute | solution.py:136
  508.5 16.2 %all-gather.19.cloned.1.call-done = bf16[1024,2048]{1,0:T(8,128)(2,1)} async-done(((bf16[128,2048]{1,0:T(8,128)(2,1)}), bf16[1024,2048]{1,0:T(8,128)(2,1)}) %all-gather.19.cloned.1.call-update) | async-done | bytes 4194320 | tf_op jit(solution)/shard_map/all_gather | solution.py:53
  524.7 14.8 %fusion.174 = f32[1024,2048]{0,1:T(8,128)} fusion(bf16[1024,2048]{1,0:T(8,128)(2,1)} %all-gather.19.cloned.1.call-done, bf16[2048,2048]{1,0:T(8,128)(2,1)} %bitcast.66), kind=kOutput, calls=%fused_computation.426 | convolution fusion | flops 8589934592 | bytes 20971520 | tf_op jit(solution)/shard_map/dot_general | solution.py:49
  543.7 10.9 multiply_convert_fusion.3
  554.6 12.8 %convolution_convert_fusion = bf16[1024,2048]{1,0:T(8,128)(2,1)S(1)} fusion(bf16[2048,2048]{1,0:T(8,128)(2,1)} %bitcast.66, bf16[1024,1024]{0,1:T(8,128)(2,1)S(1)} %get-tuple-element.138, bf16[1024,1024]{0,1:T(8,128)(2,1)S(1)} %get-tuple-element.137), kind=kOutput, calls=%fused_computation.58 | convolution fusion | flops 8600420352 | bytes 16777216 | tf_op jit(solution)/shard_map/dot_general | solution.py:49
  569.6 13.9 %fusion.173 = f32[1024,2048]{0,1:T(8,128)} fusion(bf16[1024,2048]{1,0:T(8,128)(2,1)S(1)} %copy-done.93, bf16[2048,2048]{1,0:T(8,128)(2,1)} %bitcast.66), kind=kOutput, calls=%fused_computation.425 | convolution fusion | flops 8589934592 | bytes 20971520 | tf_op jit(solution)/shard_map/dot_general | solution.py:49
  583.5 12.0 %multiply_convert_fusion.7 = (bf16[1024,1024]{0,1:T(8,128)(2,1)}, bf16[1024,1024]{0,1:T(8,128)(2,1)}, bf16[1024,1024]{0,1:T(8,128)(2,1)}) fusion(f32[1024,2048]{0,1:T(8,128)} %fusion.173, bf16[1024,2048]{1,0:T(8,128)(2,1)S(1)} %copy-done.91, bf16[2048,1024]{1,0:T(8,128)(2,1)} %bitcast.58), kind=kOutput, calls=%fused_computation.44 | convolution fusion | flops 4310695936 | bytes 23068672 | tf_op jit(solution)/shard_map/dot_general | solution.py:49
  598.9 11.3 convolution_convert_fusion.1
  622.6 10.9 fusion.175
  651.3 7.7 collective-permute-done.27
  665.9 20.1 %collective-permute-done.29 = bf16[4,128,1024]{2,1,0:T(8,128)(2,1)S(1)} collective-permute-done((bf16[4,128,1024]{2,1,0:T(8,128)(2,1)S(1)}, bf16[4,128,1024]{2,1,0:T(8,128)(2,1)S(1)}, u32[]{:S(2)}, u32[]{:S(2)}) %collective-permute-start.29) | collective-permute-done | bytes 1048608 | tf_op jit(solution)/shard_map/ppermute | solution.py:217
  688.6 15.3 %fusion.24 = f32[2048,2048]{1,0:T(8,128)} fusion(bf16[1024,2048]{1,0:T(8,128)(2,1)} %all-gather.19.cloned.1.call-done, bf16[1024,1024]{0,1:T(8,128)(2,1)} %copy-done.104, bf16[1024,1024]{0,1:T(8,128)(2,1)} %copy-done.103), kind=kOutput, calls=%fused_computation.74 | convolution fusion | flops 8598323200 | bytes 25165824 | tf_op jit(solution)/shard_map/dot_general | solution.py:49
  703.9 16.5 %add_convert_fusion = bf16[2048,2048]{1,0:T(8,128)(2,1)} fusion(f32[2048,2048]{1,0:T(8,128)} %fusion.24, bf16[1024,2048]{1,0:T(8,128)(2,1)} %all-gather.17.cloned.1.call-done, bf16[1024,1024]{0,1:T(8,128)(2,1)} %get-tuple-element.140, bf16[1024,1024]{0,1:T(8,128)(2,1)} %get-tuple-element.139), kind=kOutput, calls=%fused_computation.2 | convolution fusion | flops 8606711808 | bytes 33554432 | tf_op jit(solution)/shard_map/dot_general | solution.py:49
  741.4 14.4 %collective-permute-done.38 = bf16[4,128,1024]{2,1,0:T(8,128)(2,1)} collective-permute-done((bf16[4,128,1024]{2,1,0:T(8,128)(2,1)}, bf16[4,128,1024]{2,1,0:T(8,128)(2,1)}, u32[]{:S(2)}, u32[]{:S(2)}) %collective-permute-start.38) | collective-permute-done | bytes 1048608 | tf_op jit(solution)/shard_map/ppermute | solution.py:217
  773.1 27.6 %collective-permute-done.31 = bf16[4,128,2048]{2,1,0:T(8,128)(2,1)S(1)} collective-permute-done((bf16[4,128,2048]{2,1,0:T(8,128)(2,1)}, bf16[4,128,2048]{2,1,0:T(8,128)(2,1)S(1)}, u32[]{:S(2)}, u32[]{:S(2)}) %collective-permute-start.31) | collective-permute-done | bytes 2097184 | tf_op jit(solution)/shard_map/ppermute | solution.py:217
  877.4 8.6 convolution_convert_fusion.6
  886.0 8.7 convolution_convert_fusion.7
  924.3 8.2 add_convert_fusion.2
  944.4 7.9 fusion.6
  954.7 14.9 %collective-permute-start.58 = (bf16[4,128,2048]{2,1,0:T(8,128)(2,1)}, bf16[4,128,2048]{2,1,0:T(8,128)(2,1)}, u32[]{:S(2)}, u32[]{:S(2)}) collective-permute-start(bf16[4,128,2048]{2,1,0:T(8,128)(2,1)} %get-tuple-element.142), channel_id=1, source_target_pairs={{0,2},{2,4},{4,6},{1,3},{3,5},{5,7},{8,10},{10,12},{12,14},{9,11},... | collective-permute-start | bytes 6291464 | tf_op jit(solution)/shard_map/ppermute | solution.py:217
  972.7 67.3 %collective-permute-done.64 = bf16[128,768]{1,0:T(8,128)(2,1)S(1)} collective-permute-done((bf16[128,768]{1,0:T(8,128)(2,1)S(1)}, bf16[128,768]{1,0:T(8,128)(2,1)S(1)}, u32[]{:S(2)}, u32[]{:S(2)}) %collective-permute-start.64) | collective-permute-done | bytes 196640 | tf_op jit(solution)/shard_map/ppermute | solution.py:118
  1041.6 9.9 collective-permute-done.65
  (645 shorter events, 504.0 us)
Async XLA Ops:
  7.2 54.1 %all-gather.9.cloned.1.call-start = ((), (), s32[]{:S(2)}) async-start(), calls=%async_computation.4 | async-start | bytes 4718592 | tf_op jit(solution)/shard_map/all_gather | solution.py:53
  11.5 177.3 %all-gather.11.cloned.1.call-start = ((), (), s32[]{:S(2)}) async-start(), calls=%async_computation.5 | async-start | bytes 4718592 | tf_op jit(solution)/shard_map/all_gather | solution.py:53
  13.9 292.0 %all-gather.13.cloned.1.call-start = ((), (), s32[]{:S(2)}) async-start(), calls=%async_computation.7 | async-start | bytes 4718592 | tf_op jit(solution)/shard_map/all_gather | solution.py:53
  61.3 244.7 %all-gather.15.cloned.1.call-start = ((), (), s32[]{:S(2)}) async-start(), calls=%async_computation.8 | async-start | bytes 4718592 | tf_op jit(solution)/shard_map/all_gather | solution.py:53
  80.9 77.8 %collective-permute-start = (bf16[128,2048]{1,0:T(8,128)(2,1)}, bf16[128,2048]{1,0:T(8,128)(2,1)}, u32[]{:S(2)}, u32[]{:S(2)}) collective-permute-start(bf16[128,2048]{1,0:T(8,128)(2,1)} %bitcast.587), channel_id=1, source_target_pairs={{0,8},{8,0},{16,24},{24,16},{1,9},{9,1},{17,25},{25,17},{2,10},{10... | collective-permute-start | bytes 1572872 | tf_op jit(solution)/shard_map/ppermute | solution.py:118
  108.2 52.5 %collective-permute-start.1 = (bf16[128,2048]{1,0:T(8,128)(2,1)}, bf16[128,2048]{1,0:T(8,128)(2,1)}, u32[]{:S(2)}, u32[]{:S(2)}) collective-permute-start(bf16[128,2048]{1,0:T(8,128)(2,1)} %bitcast.12), channel_id=1, source_target_pairs={{0,16},{8,24},{16,0},{24,8},{1,17},{9,25},{17,1},{25,9},{2,18},{10... | collective-permute-start | bytes 1572872 | tf_op jit(solution)/shard_map/ppermute | solution.py:118
  111.4 51.2 %collective-permute-start.2 = (bf16[128,2048]{1,0:T(8,128)(2,1)}, bf16[128,2048]{1,0:T(8,128)(2,1)}, u32[]{:S(2)}, u32[]{:S(2)}) collective-permute-start(bf16[128,2048]{1,0:T(8,128)(2,1)} %bitcast.14), channel_id=1, source_target_pairs={{0,24},{8,16},{16,8},{24,0},{1,25},{9,17},{17,9},{25,1},{2,26},{10... | collective-permute-start | bytes 1572872 | tf_op jit(solution)/shard_map/ppermute | solution.py:118
  156.3 58.4 %collective-permute-start.12 = (bf16[4,128,1024]{2,1,0:T(8,128)(2,1)}, bf16[4,128,1024]{2,1,0:T(8,128)(2,1)S(1)}, u32[]{:S(2)}, u32[]{:S(2)}) collective-permute-start(bf16[4,128,1024]{2,1,0:T(8,128)(2,1)} %bitcast_dynamic-update-slice_fusion.19), channel_id=1, source_target_pairs={{0,16},{8,24},{16,0},{24,8},{1,17},{9,25},{17,1},{25,9},{2,18},{10... | collective-permute-start | bytes 3145736 | tf_op jit(solution)/shard_map/ppermute | solution.py:96
  158.7 57.0 %collective-permute-start.13 = (bf16[4,128,1024]{2,1,0:T(8,128)(2,1)}, bf16[4,128,1024]{2,1,0:T(8,128)(2,1)}, u32[]{:S(2)}, u32[]{:S(2)}) collective-permute-start(bf16[4,128,1024]{2,1,0:T(8,128)(2,1)} %bitcast_dynamic-update-slice_fusion.19), channel_id=1, source_target_pairs={{0,24},{8,16},{16,8},{24,0},{1,25},{9,17},{17,9},{25,1},{2,26},{10... | collective-permute-start | bytes 3145736 | tf_op jit(solution)/shard_map/ppermute | solution.py:96
  160.6 197.4 %reduce-scatter.5.cloned.1.call-start = ((), (), s32[]{:S(2)}) async-start(), calls=%async_computation.6 | async-start | bytes 4718592 | tf_op jit(solution)/shard_map/reduce_scatter | solution.py:57
  235.7 48.7 %collective-permute-start.15 = (bf16[4,128,2048]{2,1,0:T(8,128)(2,1)}, bf16[4,128,2048]{2,1,0:T(8,128)(2,1)}, u32[]{:S(2)}, u32[]{:S(2)}) collective-permute-start(bf16[4,128,2048]{2,1,0:T(8,128)(2,1)} %collective-permute-done.7), channel_id=1, source_target_pairs={{2,0},{4,2},{3,1},{5,3},{10,8},{12,10},{11,9},{13,11},{18,16},{20,... | collective-permute-start | bytes 6291464 | tf_op jit(solution)/shard_map/ppermute | solution.py:136
  289.1 151.3 %reduce-scatter.7.cloned.1.call-start = ((), (), s32[]{:S(2)}) async-start(), calls=%async_computation.10 | async-start | bytes 4718592 | tf_op jit(solution)/shard_map/reduce_scatter | solution.py:57
  310.7 195.1 %all-gather.17.cloned.1.call-start = ((), (), s32[]{:S(2)}) async-start(), calls=%async_computation.9 | async-start | bytes 4718592 | tf_op jit(solution)/shard_map/all_gather | solution.py:53
  361.5 163.2 %all-gather.19.cloned.1.call-start = ((), (), s32[]{:S(2)}) async-start(), calls=%async_computation.11 | async-start | bytes 4718592 | tf_op jit(solution)/shard_map/all_gather | solution.py:53
  361.6 79.9 %collective-permute-start.22 = (bf16[4,128,2048]{2,1,0:T(8,128)(2,1)}, bf16[4,128,2048]{2,1,0:T(8,128)(2,1)S(1)}, u32[]{:S(2)}, u32[]{:S(2)}) collective-permute-start(bf16[4,128,2048]{2,1,0:T(8,128)(2,1)} %collective-permute-done.14), channel_id=1, source_target_pairs={{4,6},{5,7},{12,14},{13,15},{20,22},{21,23},{28,30},{29,31}} | collective-permute-start | bytes 6291464 | tf_op jit(solution)/shard_map/ppermute | solution.py:135
  362.4 85.9 %collective-permute-start.23 = (bf16[4,128,2048]{2,1,0:T(8,128)(2,1)}, bf16[4,128,2048]{2,1,0:T(8,128)(2,1)}, u32[]{:S(2)}, u32[]{:S(2)}) collective-permute-start(bf16[4,128,2048]{2,1,0:T(8,128)(2,1)} %collective-permute-done.15), channel_id=1, source_target_pairs={{2,0},{3,1},{10,8},{11,9},{18,16},{19,17},{26,24},{27,25}} | collective-permute-start | bytes 6291464 | tf_op jit(solution)/shard_map/ppermute | solution.py:136
  451.2 304.6 %all-gather.23.cloned.1.call-start = ((), (), s32[]{:S(2)}) async-start(), calls=%async_computation.13 | async-start | bytes 4718592 | tf_op jit(solution)/shard_map/all_gather | solution.py:53
  622.4 178.3 %all-gather.21.cloned.1.call-start = ((), (), s32[]{:S(2)}) async-start(), calls=%async_computation.12 | async-start | bytes 4718592 | tf_op jit(solution)/shard_map/all_gather | solution.py:53
  688.2 425.3 %reduce-scatter.11.cloned.1.call-start = ((), (), s32[]{:S(2)}) async-start(), calls=%async_computation.15 | async-start | bytes 4718592 | tf_op jit(solution)/shard_map/reduce_scatter | solution.py:57
  736.2 64.6 %collective-permute-start.31 = (bf16[4,128,2048]{2,1,0:T(8,128)(2,1)}, bf16[4,128,2048]{2,1,0:T(8,128)(2,1)S(1)}, u32[]{:S(2)}, u32[]{:S(2)}) collective-permute-start(bf16[4,128,2048]{2,1,0:T(8,128)(2,1)} %get-tuple-element.146), channel_id=1, source_target_pairs={{0,2},{1,3},{8,10},{9,11},{16,18},{17,19},{24,26},{25,27}} | collective-permute-start | bytes 6291464 | tf_op jit(solution)/shard_map/ppermute | solution.py:217
  739.4 61.3 %collective-permute-start.32 = (bf16[4,128,2048]{2,1,0:T(8,128)(2,1)}, bf16[4,128,2048]{2,1,0:T(8,128)(2,1)}, u32[]{:S(2)}, u32[]{:S(2)}) collective-permute-start(bf16[4,128,2048]{2,1,0:T(8,128)(2,1)} %get-tuple-element.145), channel_id=1, source_target_pairs={{6,4},{7,5},{14,12},{15,13},{22,20},{23,21},{30,28},{31,29}} | collective-permute-start | bytes 6291464 | tf_op jit(solution)/shard_map/ppermute | solution.py:220
  760.5 67.0 %collective-permute-start.40 = (bf16[4,128,1024]{2,1,0:T(8,128)(2,1)}, bf16[4,128,1024]{2,1,0:T(8,128)(2,1)}, u32[]{:S(2)}, u32[]{:S(2)}) collective-permute-start(bf16[4,128,1024]{2,1,0:T(8,128)(2,1)} %get-tuple-element.150), channel_id=1, source_target_pairs={{0,2},{2,4},{4,6},{1,3},{3,5},{5,7},{8,10},{10,12},{12,14},{9,11},... | collective-permute-start | bytes 3145736 | tf_op jit(solution)/shard_map/ppermute | solution.py:217
  766.6 60.9 %collective-permute-start.41 = (bf16[4,128,1024]{2,1,0:T(8,128)(2,1)}, bf16[4,128,1024]{2,1,0:T(8,128)(2,1)}, u32[]{:S(2)}, u32[]{:S(2)}) collective-permute-start(bf16[4,128,1024]{2,1,0:T(8,128)(2,1)} %get-tuple-element.149), channel_id=1, source_target_pairs={{2,0},{4,2},{6,4},{3,1},{5,3},{7,5},{10,8},{12,10},{14,12},{11,9},... | collective-permute-start | bytes 3145736 | tf_op jit(solution)/shard_map/ppermute | solution.py:220
  807.7 115.8 %collective-permute-start.42 = (bf16[4,128,2048]{2,1,0:T(8,128)(2,1)}, bf16[4,128,2048]{2,1,0:T(8,128)(2,1)}, u32[]{:S(2)}, u32[]{:S(2)}) collective-permute-start(bf16[4,128,2048]{2,1,0:T(8,128)(2,1)} %get-tuple-element.144), channel_id=1, source_target_pairs={{0,2},{2,4},{1,3},{3,5},{8,10},{10,12},{9,11},{11,13},{16,18},{18,... | collective-permute-start | bytes 6291464 | tf_op jit(solution)/shard_map/ppermute | solution.py:217
  813.2 111.1 %collective-permute-start.43 = (bf16[4,128,2048]{2,1,0:T(8,128)(2,1)}, bf16[4,128,2048]{2,1,0:T(8,128)(2,1)}, u32[]{:S(2)}, u32[]{:S(2)}) collective-permute-start(bf16[4,128,2048]{2,1,0:T(8,128)(2,1)} %get-tuple-element.143), channel_id=1, source_target_pairs={{4,2},{6,4},{5,3},{7,5},{12,10},{14,12},{13,11},{15,13},{20,18},{2... | collective-permute-start | bytes 6291464 | tf_op jit(solution)/shard_map/ppermute | solution.py:220
  862.2 269.9 %reduce-scatter.9.cloned.1.call-start = ((), (), s32[]{:S(2)}) async-start(), calls=%async_computation.14 | async-start | bytes 4718592 | tf_op jit(solution)/shard_map/reduce_scatter | solution.py:57
  903.3 230.0 %collective-permute-start.54 = (bf16[128,1024]{0,1:T(8,128)(2,1)}, bf16[128,1024]{0,1:T(8,128)(2,1)}, u32[]{:S(2)}, u32[]{:S(2)}) collective-permute-start(bf16[128,1024]{0,1:T(8,128)(2,1)} %bitcast.140), channel_id=1, source_target_pairs={{0,8},{8,0},{16,24},{24,16},{1,9},{9,1},{17,25},{25,17},{2,10},{10... | collective-permute-start | bytes 786440 | tf_op jit(solution)/shard_map/ppermute | solution.py:118
  904.5 156.8 %collective-permute-start.49 = (bf16[4,128,2048]{2,1,0:T(8,128)(2,1)}, bf16[4,128,2048]{2,1,0:T(8,128)(2,1)}, u32[]{:S(2)}, u32[]{:S(2)}) collective-permute-start(bf16[4,128,2048]{2,1,0:T(8,128)(2,1)} %dynamic-slice_bitcast_fusion), channel_id=1, source_target_pairs={{0,1},{1,0},{2,3},{3,2},{4,5},{5,4},{6,7},{7,6},{8,9},{9,8},{10,11... | collective-permute-start | bytes 6291464 | tf_op jit(solution)/shard_map/ppermute | solution.py:174
  954.7 115.2 %collective-permute-start.44 = (bf16[4,128,2048]{2,1,0:T(8,128)(2,1)S(1)}, bf16[4,128,2048]{2,1,0:T(8,128)(2,1)S(1)}, u32[]{:S(2)}, u32[]{:S(2)}) collective-permute-start(bf16[4,128,2048]{2,1,0:T(8,128)(2,1)S(1)} %copy-done.29), channel_id=1, source_target_pairs={{0,1},{1,0},{2,3},{3,2},{4,5},{5,4},{6,7},{7,6},{8,9},{9,8},{10,11... | collective-permute-start | bytes 6291464 | tf_op jit(solution)/shard_map/ppermute | solution.py:174
  954.7 159.9 %collective-permute-start.58 = (bf16[4,128,2048]{2,1,0:T(8,128)(2,1)}, bf16[4,128,2048]{2,1,0:T(8,128)(2,1)}, u32[]{:S(2)}, u32[]{:S(2)}) collective-permute-start(bf16[4,128,2048]{2,1,0:T(8,128)(2,1)} %get-tuple-element.142), channel_id=1, source_target_pairs={{0,2},{2,4},{4,6},{1,3},{3,5},{5,7},{8,10},{10,12},{12,14},{9,11},... | collective-permute-start | bytes 6291464 | tf_op jit(solution)/shard_map/ppermute | solution.py:217
  972.2 67.8 %collective-permute-start.64 = (bf16[128,768]{1,0:T(8,128)(2,1)S(1)}, bf16[128,768]{1,0:T(8,128)(2,1)S(1)}, u32[]{:S(2)}, u32[]{:S(2)}) collective-permute-start(bf16[128,768]{1,0:T(8,128)(2,1)S(1)} %get-tuple-element.218), channel_id=1, source_target_pairs={{0,2},{2,0},{4,6},{6,4},{1,3},{3,1},{5,7},{7,5},{8,10},{10,8},{12,... | collective-permute-start | bytes 589832 | tf_op jit(solution)/shard_map/ppermute | solution.py:118
  1059.7 54.9 %collective-permute-start.59 = (bf16[4,128,2048]{2,1,0:T(8,128)(2,1)}, bf16[4,128,2048]{2,1,0:T(8,128)(2,1)S(1)}, u32[]{:S(2)}, u32[]{:S(2)}) collective-permute-start(bf16[4,128,2048]{2,1,0:T(8,128)(2,1)} %get-tuple-element.141), channel_id=1, source_target_pairs={{2,0},{4,2},{6,4},{3,1},{5,3},{7,5},{10,8},{12,10},{14,12},{11,9},... | collective-permute-start | bytes 6291464 | tf_op jit(solution)/shard_map/ppermute | solution.py:220
  (169 other events, 4117.8 us)
Sparse Core Ops, SparseCore 0:
  11.6 49.5 all-gather.8
  62.9 66.0 all-gather.10
  130.9 51.0 all-gather.12
  183.7 47.5 all-gather.14
  289.2 68.7 reduce-scatter.4
  360.1 80.1 reduce-scatter.6
  442.8 43.3 all-gather.16
  488.1 36.5 all-gather.18
  622.5 56.9 all-gather.22
  688.3 48.9 all-gather.20
  862.3 51.1 reduce-scatter.10
  944.5 75.0 reduce-scatter.8

commit v4 on v3

--- a/solution.py
+++ b/solution.py
@@ -78,36 +78,32 @@
     return lax.dynamic_index_in_dim(buffer, index, 0, keepdims=False)
 
 
-def spread_weight(weight):
-    rows, contexts, columns = weight.shape
-    groups = lax.axis_size("dp")
-    here, group = lax.axis_index("context"), lax.axis_index("dp")
-    pieces = jnp.moveaxis(weight, 1, 0)
-    mine = jnp.zeros((contexts, rows, columns), weight.dtype)
-    mine = put(mine, take(pieces, here), here)
-    for step in range(1, contexts):
-        route = [(i, (i + step) % contexts) for i in range(contexts)]
-        piece = lax.ppermute(take(pieces, (here + step) % contexts), "context", route)
-        mine = put(mine, piece, (here - step) % contexts)
-    whole = jnp.zeros((groups,) + mine.shape, weight.dtype)
+def trade(weight, axis):
+    return exchange(jnp.moveaxis(weight, 1, 0), axis)
+
+
+def gather_groups(mine):
+    group, groups = lax.axis_index("dp"), lax.axis_size("dp")
+    whole = jnp.zeros((groups,) + mine.shape, mine.dtype)
     whole = put(whole, mine, group)
     for step in range(1, groups):
         route = [(i, i ^ step) for i in range(groups)]
         whole = put(whole, lax.ppermute(mine, "dp", route), group ^ step)
-    return whole.reshape(groups * contexts * rows, columns)
-
-
-def collect_pieces(partial, contexts):
-    groups = lax.axis_size("dp")
-    group = lax.axis_index("dp")
-    columns = partial.shape[1]
-    rows = partial.shape[0] // (groups * contexts)
-    parts = partial.reshape(groups, contexts * rows, columns)
-    total = take(parts, group).astype(jnp.float32)
+    return whole.reshape(-1, mine.shape[-1])
+
+
+def reduce_groups(partials):
+    group, groups = lax.axis_index("dp"), lax.axis_size("dp")
+    parts = [partial.reshape(groups, -1, partial.shape[1]) for partial in partials]
+
+    def term(index):
+        return jnp.concatenate([take(part, index) for part in parts], axis=1)
+
+    total = term(group).astype(jnp.float32)
     for step in range(1, groups):
         route = [(i, i ^ step) for i in range(groups)]
-        total = total + lax.ppermute(take(parts, group ^ step), "dp", route).astype(jnp.float32)
-    return swap(total.astype(jnp.bfloat16).reshape(contexts, rows, columns), "context")
+        total = total + lax.ppermute(term(group ^ step), "dp", route).astype(jnp.float32)
+    return total.astype(jnp.bfloat16)
 
 
 def swap(pieces, axis):
@@ -196,15 +192,15 @@
 
 
 class Reduction:
-    def __init__(self, partial, groups, contexts):
-        self.parts = partial.reshape(groups, contexts, -1, partial.shape[1])
+    def __init__(self, partials, groups, contexts):
+        self.parts = [partial.reshape(groups, contexts, -1, partial.shape[1]) for partial in partials]
         self.n, self.here = contexts, lax.axis_index("context")
         self.above = self.below = None
         self.step = 0
 
     def term(self, index):
-        picked = lax.dynamic_index_in_dim(self.parts, index % self.n, 1, keepdims=False)
-        return picked.astype(jnp.float32)
+        picked = [lax.dynamic_index_in_dim(part, index % self.n, 1, keepdims=False) for part in self.parts]
+        return jnp.concatenate(picked, axis=-1).astype(jnp.float32)
 
     def hop(self):
         if self.step == self.n - 1:
@@ -253,16 +249,16 @@
     def by_context(weight):
         return weight.reshape(weight.shape[0], contexts, -1)
 
-    attention_w = spread_weight(
-        jnp.concatenate([by_context(w) for w in (w_query, w_key, w_value, w_out.T)], axis=2)
-    )
-    qkv_w, out_w = attention_w[:, : 3 * head_cols], attention_w[:, 3 * head_cols :]
+    attention_part = trade(
+        jnp.concatenate([by_context(w) for w in (w_query, w_key, w_value, w_out.T)], axis=2), "context"
+    )
 
     def by_group(weight):
         return jnp.moveaxis(weight.reshape(weight.shape[0], groups, -1), 1, 0)
 
-    gate_up_block = exchange(jnp.concatenate([by_group(w_gate), by_group(w_up)], axis=2), "dp")
-    down_block = exchange(by_group(w_down.T), "dp")
+    ffn_block = exchange(
+        jnp.concatenate([by_group(w) for w in (w_gate, w_up, w_down.T)], axis=2), "dp"
+    )
 
     def einsum(form, left, right):
         return jnp.einsum(form, left, right, preferred_element_type=jnp.float32)
@@ -282,14 +278,13 @@
     norm_one, inverse_one = zip(*[normalize(own_tokens[slot]) for slot in each])
     norm_one_all = [gather_rows(norm_one[slot].astype(low), SEQUENCE_ROWS) for slot in each]
 
-    norm_one_all[0], gate_up_block, down_block = lax.optimization_barrier(
-        (norm_one_all[0], gate_up_block, down_block)
-    )
-    gate_up_hops, down_hops = relay_hops(gate_up_block), relay_hops(down_block)
+    attention_part, *ffn_grad = lax.optimization_barrier((attention_part, *ffn_grad))
+    attention_w = gather_groups(attention_part)
+    qkv_w, out_w = attention_w[:, : 3 * head_cols], attention_w[:, 3 * head_cols :]
+    norm_one_all[0], ffn_block = lax.optimization_barrier((norm_one_all[0], ffn_block))
+    hops = relay_hops(ffn_block)
     last = slots - 1
-    norm_one_all[last], *ffn_grad = lax.optimization_barrier((norm_one_all[last], *ffn_grad))
     ffn_grad_all = [gather_rows(ffn_grad[slot], PLANE_ROWS) for slot in each]
-    norm_one_all[last] = hold(norm_one_all[last], gate_up_hops, 0)
 
     def attend(slot):
         qkv = dot(norm_one_all[slot], qkv_w, ((1,), (0,)))
@@ -312,25 +307,23 @@
         attended = kept[4]
         if slot == 0:
             attended, *ffn_grad_all = lax.optimization_barrier((attended, *ffn_grad_all))
+            attended = hold(attended, hops, 0)
         if slot == last:
-            attended = hold(attended, gate_up_hops, 1)
+            attended = hold(attended, hops, 1)
         saved.append(kept[:4] + (attended,))
         branch.append(scatter_rows(dot(attended, out_w, ((1,), (1,))), SEQUENCE_ROWS))
     middle, norm_two, inverse_two, norm_two_all = [], [], [], []
     for slot in each:
         summed_branch = branch[slot]
-        if slot == 0:
-            summed_branch = hold(summed_branch, gate_up_hops, 2)
         if slot == last:
-            summed_branch = hold(summed_branch, down_hops, 0)
+            summed_branch = hold(summed_branch, hops, 2)
         middle.append(own_tokens[slot] + valid_rows[slot] * summed_branch)
         normed, inverse = normalize(middle[slot])
         norm_two.append(normed)
         inverse_two.append(inverse)
         norm_two_all.append(gather_rows(normed.astype(low), PLANE_ROWS))
-    for slot in each:
-        norm_two_all[slot] = hold(norm_two_all[slot], down_hops, 1 + slot)
-    gate_up_w, down_w = assemble(gate_up_block, gate_up_hops), assemble(down_block, down_hops)
+    ffn_w = assemble(ffn_block, hops)
+    gate_up_w, down_w = ffn_w[:, : 2 * units], ffn_w[:, 2 * units :]
 
     hidden, gate_up_grad, norm_two_grad = [], [], []
     for slot in each:
@@ -352,33 +345,28 @@
         return total.astype(low)
 
     down_sum = over_slots([dot(ffn_grad_all[slot], hidden[slot], ((0,), (0,))) for slot in each])
-    down_sum = Reduction(down_sum, groups, contexts)
     gate_up_sum = over_slots([dot(norm_two_all[slot], gate_up_grad[slot], ((0,), (0,))) for slot in each])
-    gate_up_sum = Reduction(gate_up_sum, groups, contexts)
+    ffn_sum = Reduction([gate_up_sum, down_sum], groups, contexts)
 
     middle_grad, branch_grad_all = [], []
     for slot in each:
         upstream = norm_two_grad[slot]
-        if slot == last:
-            down_sum.hop()
-            upstream = down_sum.hold(upstream)
         middle_grad.append(
             out_grad[slot] + normalize_back(norm_two[slot], inverse_two[slot], upstream)
         )
         branch_grad_all.append(
             gather_rows((valid_rows[slot] * middle_grad[slot]).astype(low), SEQUENCE_ROWS)
         )
-    down_sum.hop()
-    branch_grad_all[0] = down_sum.hold(branch_grad_all[0])
-    down_sum.hop()
-    gate_up_sum.hop()
-    branch_grad_all[last] = down_sum.hold(gate_up_sum.hold(branch_grad_all[last]))
-    branch_grad_all[last], *hidden_late = lax.optimization_barrier((branch_grad_all[last], *hidden))
+    branch_grad_all[0], *ffn_sum.parts = lax.optimization_barrier((branch_grad_all[0], *ffn_sum.parts))
+    ffn_sum.hop()
 
     qkv_grad, norm_one_grad = [], []
     for slot in each:
         query, key, value, probabilities, attended = saved[slot]
-        attended_grad = split(dot(branch_grad_all[slot], out_w, ((1,), (0,))).astype(low))
+        attended_grad = dot(branch_grad_all[slot], out_w, ((1,), (0,))).astype(low)
+        if slot == last:
+            attended_grad = ffn_sum.hold(attended_grad)
+        attended_grad = split(attended_grad)
         prob_grad = einsum("qhd,khd->hqk", attended_grad, value)
         row_delta = jnp.sum(probabilities * prob_grad, axis=-1, keepdims=True)
         score_grad = (probabilities * (prob_grad - row_delta)).astype(low)
@@ -395,24 +383,28 @@
                 axis=1,
             )
         )
-        if slot == last:
-            gate_up_sum.hop()
-            qkv_grad[slot] = gate_up_sum.hold(qkv_grad[slot])
-        norm_one_grad.append(
-            scatter_rows(dot(qkv_grad[slot], qkv_w, ((1,), (1,))), SEQUENCE_ROWS)
-        )
+        part = dot(qkv_grad[slot], qkv_w, ((1,), (1,))).astype(low)
+        if slot + 1 < slots:
+            part, branch_grad_all[slot + 1] = lax.optimization_barrier((part, branch_grad_all[slot + 1]))
+        if slot + 1 == last:
+            branch_grad_all[last], *hidden_late = lax.optimization_barrier(
+                (branch_grad_all[last], *hidden)
+            )
+        norm_one_grad.append(scatter_rows(part, SEQUENCE_ROWS))
     out_sum = over_slots([dot(branch_grad_all[slot], saved[slot][4], ((0,), (0,))) for slot in each])
     qkv_sum = over_slots([dot(norm_one_all[slot], qkv_grad[slot], ((0,), (0,))) for slot in each])
 
+    ffn_sum.hop()
+    qkv_sum, norm_one_grad[0] = lax.optimization_barrier((qkv_sum, norm_one_grad[0]))
+    qkv_sum = ffn_sum.hold(qkv_sum)
+
     layer_out, input_grad = [], []
     for slot in each:
         feedforward = scatter_plane(dot(hidden_late[slot], down_w, ((1,), (1,))))
         layer_out.append((middle[slot] + valid_rows[slot] * feedforward).astype(low))
-    gate_up_sum.hop()
-    norm_one_grad[0] = gate_up_sum.hold(norm_one_grad[0])
-    down_pieces = down_sum.finish()
-    norm_one_grad[last], *rest = lax.optimization_barrier((norm_one_grad[last], *layer_out, *down_pieces))
-    layer_out, down_pieces = rest[:slots], rest[slots:]
+    ffn_sum.hop()
+    norm_one_grad[0], *layer_out = lax.optimization_barrier((norm_one_grad[0], *layer_out))
+    attention_total = ffn_sum.hold(reduce_groups([qkv_sum, out_sum]))
     for slot in each:
         upstream = norm_one_grad[slot]
         input_grad.append(
@@ -420,9 +412,8 @@
         )
     layer_out, input_grad = join_cores(jnp.stack(layer_out)), join_cores(jnp.stack(input_grad))
 
-    gate_up_pieces = gate_up_sum.finish()
-    out_pieces = collect_pieces(out_sum, contexts)
-    qkv_pieces = collect_pieces(qkv_sum, contexts)
+    ffn_pieces = ffn_sum.finish()
+    attention_pieces = swap(attention_total.reshape(contexts, -1, 4 * head_cols), "context")
 
     def column_output(pieces, axis, start, size):
         members, here = lax.axis_size(axis), lax.axis_index(axis)
@@ -432,19 +423,19 @@
             whole = lax.dynamic_update_slice_in_dim(whole, block, (here ^ step) * size, 1)
         return whole
 
-    def row_output(pieces, axis, size):
+    def row_output(pieces, axis, start, size):
         members, here = lax.axis_size(axis), lax.axis_index(axis)
         whole = jnp.zeros((members * size, pieces[0].shape[0]), jnp.float32)
         for step, piece in enumerate(pieces):
-            block = piece.astype(jnp.float32).T
+            block = piece[:, start : start + size].astype(jnp.float32).T
             whole = lax.dynamic_update_slice_in_dim(whole, block, (here ^ step) * size, 0)
         return whole
 
-    grads = tuple(column_output(qkv_pieces, "context", i * head_cols, head_cols) for i in range(3)) + (
-        row_output(out_pieces, "context", head_cols),
-        column_output(gate_up_pieces, "dp", 0, units),
-        column_output(gate_up_pieces, "dp", units, units),
-        row_output(down_pieces, "dp", units),
+    grads = tuple(column_output(attention_pieces, "context", i * head_cols, head_cols) for i in range(3)) + (
+        row_output(attention_pieces, "context", 3 * head_cols, head_cols),
+        column_output(ffn_pieces, "dp", 0, units),
+        column_output(ffn_pieces, "dp", units, units),
+        row_output(ffn_pieces, "dp", 2 * units, units),
     )
     return (layer_out, input_grad) + grads
 

time: 1170 us -> 1090 us (0.932)
  waiting for transfers between devices: 523 us -> 460 us
  starting transfers between devices: 132 us -> 105 us
  other arithmetic: 111 us -> 129 us
    ppermute x18 -> x12, waiting for transfers between devices: 128 us -> 51.1 us  [swap(): arrived.append(lax.ppermute(take(pieces, here ^ step), axis, route))]
    ppermute x6 -> x3, waiting for transfers between devices: 63.9 us -> 127 us  [relay_hops(): lax.ppermute(moving_down, 'context', [(i, i - 1) for i in range(1, n - st...]
    all_gather x8, waiting for transfers between devices: 57 us -> 18.4 us  [gather_rows(): return lax.all_gather(values, axes, axis=0, tiled=True)]
    reduce_scatter x4, waiting for transfers between devices: 118 us -> 82.3 us  [scatter_rows(): lax.psum_scatter(values.astype(jnp.bfloat16), axes, scatter_dimension=0,...]
    ppermute x12 -> x6, waiting for transfers between devices: 46.2 us -> 81.2 us  [the longest x3 42.6 us: reduce_groups(): lax.ppermute(term(group ^ step), 'dp', route).astype(jnp.float32)]
    ppermute x6 -> x3, starting transfers between devices: 38.5 us -> 18.7 us  [hop(): lax.ppermute(above.astype(jnp.bfloat16), 'context', [(i, i + 1) for i in...]
    convert_element_type x4 -> x2, other arithmetic: 23.5 us -> 10.4 us  [hop(): below.astype(jnp.bfloat16)]
    ppermute x6 -> x3, starting transfers between devices: 11.9 us -> 24.1 us  [relay_hops(): lax.ppermute(moving_up, 'context', [(i, i + 1) for i in range(step - 1, n...]
  transfers between devices with their start and end apart: 88 -> 64, of which waited for: 39 -> 28; matrix products, arithmetic and copies ran while one was open for 36% -> 38% of each run, Pallas kernels for 0% -> 0%
where the time goes in v4:
time: 1090 us; the launch traced here: 1080 us
  waiting for transfers between devices  460 us (42%)
  matrix products  246 us (23%)
  other arithmetic  129 us (12%)
  local copies, waits for them, and re-layouts  122 us (11%)
  starting transfers between devices  105 us (10%)
  between operations  17 us (2%)
    dot_general x24, matrix products, dot(): lax.dot_general(left, right, (dims, ((), ())), preferred_element_type=jnp...  208 us
    ppermute x3, waiting for transfers between devices, relay_hops(): lax.ppermute(moving_down, 'context', [(i, i - 1) for i in range(1, n - st...  127 us
    reduce_scatter x4, waiting for transfers between devices, scatter_rows(): lax.psum_scatter(values.astype(jnp.bfloat16), axes, scatter_dimension=0,...  82.3 us
    ppermute x3, waiting for transfers between devices, hop(): lax.ppermute(above.astype(jnp.bfloat16), 'context', [(i, i + 1) for i in...  55.5 us
    ppermute x12, waiting for transfers between devices, swap(): arrived.append(lax.ppermute(take(pieces, here ^ step), axis, route))  51.1 us
    ppermute x3, waiting for transfers between devices, reduce_groups(): lax.ppermute(term(group ^ step), 'dp', route).astype(jnp.float32)  42.6 us
    ppermute x16, waiting for transfers between devices, scatter_plane(): other = lax.ppermute(send, 'dp', route)  39 us
    ppermute x3, waiting for transfers between devices, gather_groups(): whole = put(whole, lax.ppermute(mine, 'dp', route), group ^ step)  38.7 us
  transfers between devices with their start and end apart: 64, of which 28 were waited for; matrix products, arithmetic and copies ran while one was open for 38% of the time, Pallas kernels for 0%

profile of v4, /device:TPU:0, one launch (start us, length us, event | category | flops | bytes accessed | tf_op | source)
XLA Modules:
  0.0 1080.0 jit_solution(12656121401369030211)
XLA Ops:
  39.9 12.2 %collective-permute-done.4 = bf16[128,1024]{1,0:T(8,128)(2,1)} collective-permute-done((bf16[128,1024]{1,0:T(8,128)(2,1)}, bf16[128,1024]{1,0:T(8,128)(2,1)}, u32[]{:S(2)}, u32[]{:S(2)}) %collective-permute-start.4) | collective-permute-done | bytes 262176 | tf_op jit(solution)/shard_map/ppermute | solution.py:114
  92.6 14.4 %collective-permute-done.1 = bf16[128,3072]{1,0:T(8,128)(2,1)} collective-permute-done((bf16[128,3072]{1,0:T(8,128)(2,1)}, bf16[128,3072]{1,0:T(8,128)(2,1)}, u32[]{:S(2)}, u32[]{:S(2)}) %collective-permute-start.1) | collective-permute-done | bytes 786464 | tf_op jit(solution)/shard_map/ppermute | solution.py:114
  111.2 14.5 %collective-permute-done.6 = bf16[4,128,1024]{2,1,0:T(8,128)(2,1)} collective-permute-done((bf16[4,128,1024]{2,1,0:T(8,128)(2,1)}, bf16[4,128,1024]{2,1,0:T(8,128)(2,1)}, u32[]{:S(2)}, u32[]{:S(2)}) %collective-permute-start.6) | collective-permute-done | bytes 1048608 | tf_op jit(solution)/shard_map/ppermute | solution.py:91
  127.9 24.2 %collective-permute-done.7 = bf16[4,128,1024]{2,1,0:T(8,128)(2,1)S(1)} collective-permute-done((bf16[4,128,1024]{2,1,0:T(8,128)(2,1)}, bf16[4,128,1024]{2,1,0:T(8,128)(2,1)S(1)}, u32[]{:S(2)}, u32[]{:S(2)}) %collective-permute-start.7) | collective-permute-done | bytes 1048608 | tf_op jit(solution)/shard_map/ppermute | solution.py:91
  155.5 19.1 %collective-permute-start.9 = (bf16[4,128,3072]{2,1,0:T(8,128)(2,1)}, bf16[4,128,3072]{2,1,0:T(8,128)(2,1)}, u32[]{:S(2)}, u32[]{:S(2)}) collective-permute-start(bf16[4,128,3072]{2,1,0:T(8,128)(2,1)} %bitcast_dynamic-update-slice_fusion.8), channel_id=1, source_target_pairs={{0,2},{2,4},{4,6},{1,3},{3,5},{5,7},{8,10},{10,12},{12,14},{9,11},... | collective-permute-start | bytes 9437192 | tf_op jit(solution)/shard_map/ppermute | solution.py:131
  196.3 9.6 fusion.169
  210.8 13.0 %all-gather.13.cloned.1.call-done = bf16[1024,2048]{1,0:T(8,128)(2,1)} async-done(((bf16[128,2048]{1,0:T(8,128)(2,1)}), bf16[1024,2048]{1,0:T(8,128)(2,1)}) %all-gather.13.cloned.1.call-update) | async-done | bytes 4194320 | tf_op jit(solution)/shard_map/all_gather | solution.py:53
  242.6 7.7 fusion.170
  254.7 90.4 %collective-permute-done.12 = bf16[4,128,3072]{2,1,0:T(8,128)(2,1)} collective-permute-done((bf16[4,128,3072]{2,1,0:T(8,128)(2,1)}, bf16[4,128,3072]{2,1,0:T(8,128)(2,1)}, u32[]{:S(2)}, u32[]{:S(2)}) %collective-permute-start.12) | collective-permute-done | bytes 3145760 | tf_op jit(solution)/shard_map/ppermute | solution.py:132
  368.6 58.6 %reduce-scatter.7.cloned.1.call-done = bf16[128,2048]{1,0:T(8,128)(2,1)} async-done(((bf16[1024,2048]{1,0:T(8,128)(2,1)}), bf16[128,2048]{1,0:T(8,128)(2,1)}) %reduce-scatter.7.cloned.1.call-update) | async-done | bytes 524304 | tf_op jit(solution)/shard_map/reduce_scatter | solution.py:57
  428.4 31.4 %collective-permute-done.14 = bf16[4,128,3072]{2,1,0:T(8,128)(2,1)} collective-permute-done((bf16[4,128,3072]{2,1,0:T(8,128)(2,1)}, bf16[4,128,3072]{2,1,0:T(8,128)(2,1)}, u32[]{:S(2)}, u32[]{:S(2)}) %collective-permute-start.14) | collective-permute-done | bytes 3145760 | tf_op jit(solution)/shard_map/ppermute | solution.py:132
  477.4 14.8 %fusion.10 = f32[1024,2048]{0,1:T(8,128)} fusion(bf16[1024,2048]{1,0:T(8,128)(2,1)} %all-gather.17.cloned.1.call-done, bf16[2048,3072]{1,0:T(8,128)(2,1)} %bitcast.454), kind=kOutput, calls=%fused_computation.26 | convolution fusion | flops 8589934592 | bytes 20971520 | tf_op jit(solution)/shard_map/dot_general | solution.py:49
  492.3 10.4 multiply_convert_fusion.7
  502.6 12.2 %fusion.26 = bf16[1024,2048]{1,0:T(8,128)(2,1)} fusion(bf16[2048,3072]{1,0:T(8,128)(2,1)S(1)} %bitcast.460, bf16[1024,1024]{0,1:T(8,128)(2,1)} %get-tuple-element.108, bf16[1024,1024]{0,1:T(8,128)(2,1)} %get-tuple-element.107), kind=kOutput, calls=%fused_computation.60 | convolution fusion | flops 8600420352 | bytes 16777216 | tf_op jit(solution)/shard_map/dot_general | solution.py:49
  528.3 11.7 %collective-permute-done.16 = bf16[2,128,1024]{2,1,0:T(8,128)(2,1)S(1)} collective-permute-done((bf16[2,128,1024]{2,1,0:T(8,128)(2,1)}, bf16[2,128,1024]{2,1,0:T(8,128)(2,1)S(1)}, u32[]{:S(2)}, u32[]{:S(2)}) %collective-permute-start.16) | collective-permute-done | bytes 524320 | tf_op jit(solution)/shard_map/ppermute | solution.py:185
  542.9 13.9 %fusion.32 = f32[2048,2048]{1,0:T(8,128)} fusion(bf16[1024,2048]{1,0:T(8,128)(2,1)S(1)} %copy-done.113, bf16[1024,1024]{0,1:T(8,128)(2,1)} %get-tuple-element.108, bf16[1024,1024]{0,1:T(8,128)(2,1)} %get-tuple-element.107), kind=kOutput, calls=%fused_computation.75 | convolution fusion | flops 8598323200 | bytes 25165824 | tf_op jit(solution)/shard_map/dot_general | solution.py:49
  557.1 15.0 %fusion.6 = f32[1024,2048]{0,1:T(8,128)} fusion(bf16[1024,2048]{1,0:T(8,128)(2,1)} %all-gather.21.cloned.1.call-done, bf16[2048,3072]{1,0:T(8,128)(2,1)} %bitcast.455), kind=kOutput, calls=%fused_computation.22 | convolution fusion | flops 8589934592 | bytes 20971520 | tf_op jit(solution)/shard_map/dot_general | solution.py:49
  572.1 11.8 %multiply_convert_fusion.5 = (bf16[1024,1024]{0,1:T(8,128)(2,1)}, bf16[1024,1024]{0,1:T(8,128)(2,1)}, bf16[1024,1024]{0,1:T(8,128)(2,1)}) fusion(f32[1024,2048]{0,1:T(8,128)} %fusion.6, bf16[1024,2048]{1,0:T(8,128)(2,1)S(1)} %copy-done.111, bf16[2048,3072]{1,0:T(8,128)(2,1)} %bitcast.456), kind=kOutput, calls=%fused_computation.42 | convolution fusion | flops 4310695936 | bytes 23068672 | tf_op jit(solution)/shard_map/dot_general | solution.py:49
  583.9 12.4 %fusion.29 = bf16[1024,2048]{1,0:T(8,128)(2,1)} fusion(bf16[2048,3072]{1,0:T(8,128)(2,1)S(1)} %bitcast.463, bf16[1024,1024]{0,1:T(8,128)(2,1)} %get-tuple-element.106, bf16[1024,1024]{0,1:T(8,128)(2,1)} %get-tuple-element.105), kind=kOutput, calls=%fused_computation.61 | convolution fusion | flops 8600420352 | bytes 16777216 | tf_op jit(solution)/shard_map/dot_general | solution.py:49
  602.0 10.9 %fusion.171 = f32[2048,1024]{1,0:T(8,128)} fusion(bf16[1024,2048]{1,0:T(8,128)(2,1)} %all-gather.11.cloned.1.call-done, bf16[1024,1024]{0,1:T(8,128)(2,1)} %get-tuple-element.73), kind=kOutput, calls=%fused_computation.414 | convolution fusion | flops 4294967296 | bytes 14680064 | tf_op jit(solution)/shard_map/dot_general | solution.py:49
  619.1 16.7 %add_convert_fusion = bf16[2048,2048]{1,0:T(8,128)(2,1)} fusion(f32[2048,2048]{1,0:T(8,128)} %fusion.32, bf16[1024,2048]{1,0:T(8,128)(2,1)} %all-gather.21.cloned.1.call-done, bf16[1024,1024]{0,1:T(8,128)(2,1)} %get-tuple-element.106, bf16[1024,1024]{0,1:T(8,128)(2,1)} %get-tuple-element.105), kind=kOutput, calls=%fused_computation.2 | convolution fusion | flops 8606711808 | bytes 33554432 | tf_op jit(solution)/shard_map/dot_general | solution.py:49
  638.7 9.1 add_convert_fusion.1
  650.8 9.8 dynamic-slice_bitcast_fusion
  696.0 8.8 fusion.131
  714.8 43.3 %collective-permute-done.25 = bf16[4,128,3072]{2,1,0:T(8,128)(2,1)} collective-permute-done((bf16[4,128,3072]{2,1,0:T(8,128)(2,1)}, bf16[4,128,3072]{2,1,0:T(8,128)(2,1)}, u32[]{:S(2)}, u32[]{:S(2)}) %collective-permute-start.25) | collective-permute-done | bytes 3145760 | tf_op jit(solution)/shard_map/ppermute | solution.py:213
  836.6 8.4 collective-permute-done.33
  847.6 8.1 collective-permute-done.28
  875.1 12.1 %collective-permute-done.39 = bf16[4,128,3072]{2,1,0:T(8,128)(2,1)} collective-permute-done((bf16[4,128,3072]{2,1,0:T(8,128)(2,1)}, bf16[4,128,3072]{2,1,0:T(8,128)(2,1)}, u32[]{:S(2)}, u32[]{:S(2)}) %collective-permute-start.39) | collective-permute-done | bytes 3145760 | tf_op jit(solution)/shard_map/ppermute | solution.py:213
  899.1 10.3 collective-permute-start.44
  913.6 23.6 %reduce-scatter.11.cloned.1.call-done = bf16[128,2048]{1,0:T(8,128)(2,1)} async-done(((bf16[1024,2048]{1,0:T(8,128)(2,1)}), bf16[128,2048]{1,0:T(8,128)(2,1)}) %reduce-scatter.11.cloned.1.call-update) | async-done | bytes 524304 | tf_op jit(solution)/shard_map/reduce_scatter | solution.py:57
  957.1 42.6 %collective-permute-done.42 = bf16[512,1024]{1,0:T(8,128)(2,1)} collective-permute-done((bf16[512,1024]{1,0:T(8,128)(2,1)}, bf16[512,1024]{1,0:T(8,128)(2,1)}, u32[]{:S(2)}, u32[]{:S(2)}) %collective-permute-start.42) | collective-permute-done | bytes 1048608 | tf_op jit(solution)/shard_map/ppermute | solution.py:105
  1034.2 11.3 %collective-permute-done.47 = bf16[128,1024]{1,0:T(8,128)(2,1)} collective-permute-done((bf16[128,1024]{1,0:T(8,128)(2,1)}, bf16[128,1024]{1,0:T(8,128)(2,1)}, u32[]{:S(2)}, u32[]{:S(2)}) %collective-permute-start.47) | collective-permute-done | bytes 262176 | tf_op jit(solution)/shard_map/ppermute | solution.py:114
  (609 shorter events, 450.6 us)
Async XLA Ops:
  7.2 147.1 %all-gather.9.cloned.1.call-start = ((), (), s32[]{:S(2)}) async-start(), calls=%async_computation.4 | async-start | bytes 4718592 | tf_op jit(solution)/shard_map/all_gather | solution.py:53
  11.5 172.0 %all-gather.15.cloned.1.call-start = ((), (), s32[]{:S(2)}) async-start(), calls=%async_computation.8 | async-start | bytes 4718592 | tf_op jit(solution)/shard_map/all_gather | solution.py:53
  14.0 196.7 %all-gather.11.cloned.1.call-start = ((), (), s32[]{:S(2)}) async-start(), calls=%async_computation.5 | async-start | bytes 4718592 | tf_op jit(solution)/shard_map/all_gather | solution.py:53
  56.2 167.6 %all-gather.13.cloned.1.call-start = ((), (), s32[]{:S(2)}) async-start(), calls=%async_computation.6 | async-start | bytes 4718592 | tf_op jit(solution)/shard_map/all_gather | solution.py:53
  82.0 43.7 %collective-permute-start.6 = (bf16[4,128,1024]{2,1,0:T(8,128)(2,1)}, bf16[4,128,1024]{2,1,0:T(8,128)(2,1)}, u32[]{:S(2)}, u32[]{:S(2)}) collective-permute-start(bf16[4,128,1024]{2,1,0:T(8,128)(2,1)} %bitcast_dynamic-update-slice_fusion.11), channel_id=1, source_target_pairs={{0,8},{8,0},{16,24},{24,16},{1,9},{9,1},{17,25},{25,17},{2,10},{10... | collective-permute-start | bytes 3145736 | tf_op jit(solution)/shard_map/ppermute | solution.py:91
  83.5 68.6 %collective-permute-start.7 = (bf16[4,128,1024]{2,1,0:T(8,128)(2,1)}, bf16[4,128,1024]{2,1,0:T(8,128)(2,1)S(1)}, u32[]{:S(2)}, u32[]{:S(2)}) collective-permute-start(bf16[4,128,1024]{2,1,0:T(8,128)(2,1)} %bitcast_dynamic-update-slice_fusion.11), channel_id=1, source_target_pairs={{0,16},{8,24},{16,0},{24,8},{1,17},{9,25},{17,1},{25,9},{2,18},{10... | collective-permute-start | bytes 3145736 | tf_op jit(solution)/shard_map/ppermute | solution.py:91
  90.0 259.8 %reduce-scatter.5.cloned.1.call-start = ((), (), s32[]{:S(2)}) async-start(), calls=%async_computation.7 | async-start | bytes 4718592 | tf_op jit(solution)/shard_map/reduce_scatter | solution.py:57
  90.0 63.2 %collective-permute-start.8 = (bf16[4,128,1024]{2,1,0:T(8,128)(2,1)}, bf16[4,128,1024]{2,1,0:T(8,128)(2,1)S(1)}, u32[]{:S(2)}, u32[]{:S(2)}) collective-permute-start(bf16[4,128,1024]{2,1,0:T(8,128)(2,1)} %bitcast_dynamic-update-slice_fusion.11), channel_id=1, source_target_pairs={{0,24},{8,16},{16,8},{24,0},{1,25},{9,17},{17,9},{25,1},{2,26},{10... | collective-permute-start | bytes 3145736 | tf_op jit(solution)/shard_map/ppermute | solution.py:91
  154.2 74.5 %collective-permute-start.10 = (bf16[4,128,3072]{2,1,0:T(8,128)(2,1)}, bf16[4,128,3072]{2,1,0:T(8,128)(2,1)}, u32[]{:S(2)}, u32[]{:S(2)}) collective-permute-start(bf16[4,128,3072]{2,1,0:T(8,128)(2,1)} %bitcast_dynamic-update-slice_fusion.8), channel_id=1, source_target_pairs={{2,0},{4,2},{6,4},{3,1},{5,3},{7,5},{10,8},{12,10},{14,12},{11,9},... | collective-permute-start | bytes 9437192 | tf_op jit(solution)/shard_map/ppermute | solution.py:132
  155.5 74.4 %collective-permute-start.9 = (bf16[4,128,3072]{2,1,0:T(8,128)(2,1)}, bf16[4,128,3072]{2,1,0:T(8,128)(2,1)}, u32[]{:S(2)}, u32[]{:S(2)}) collective-permute-start(bf16[4,128,3072]{2,1,0:T(8,128)(2,1)} %bitcast_dynamic-update-slice_fusion.8), channel_id=1, source_target_pairs={{0,2},{2,4},{4,6},{1,3},{3,5},{5,7},{8,10},{10,12},{12,14},{9,11},... | collective-permute-start | bytes 9437192 | tf_op jit(solution)/shard_map/ppermute | solution.py:131
  234.5 192.7 %reduce-scatter.7.cloned.1.call-start = ((), (), s32[]{:S(2)}) async-start(), calls=%async_computation.9 | async-start | bytes 4718592 | tf_op jit(solution)/shard_map/reduce_scatter | solution.py:57
  237.2 107.9 %collective-permute-start.12 = (bf16[4,128,3072]{2,1,0:T(8,128)(2,1)}, bf16[4,128,3072]{2,1,0:T(8,128)(2,1)}, u32[]{:S(2)}, u32[]{:S(2)}) collective-permute-start(bf16[4,128,3072]{2,1,0:T(8,128)(2,1)} %collective-permute-done.10), channel_id=1, source_target_pairs={{2,0},{4,2},{3,1},{5,3},{10,8},{12,10},{11,9},{13,11},{18,16},{20,... | collective-permute-start | bytes 9437192 | tf_op jit(solution)/shard_map/ppermute | solution.py:132
  349.7 127.8 %all-gather.17.cloned.1.call-start = ((), (), s32[]{:S(2)}) async-start(), calls=%async_computation.10 | async-start | bytes 4718592 | tf_op jit(solution)/shard_map/all_gather | solution.py:53
  354.9 202.2 %all-gather.21.cloned.1.call-start = ((), (), s32[]{:S(2)}) async-start(), calls=%async_computation.12 | async-start | bytes 4718592 | tf_op jit(solution)/shard_map/all_gather | solution.py:53
  354.9 73.5 %collective-permute-start.13 = (bf16[4,128,3072]{2,1,0:T(8,128)(2,1)}, bf16[4,128,3072]{2,1,0:T(8,128)(2,1)}, u32[]{:S(2)}, u32[]{:S(2)}) collective-permute-start(bf16[4,128,3072]{2,1,0:T(8,128)(2,1)} %collective-permute-done.11), channel_id=1, source_target_pairs={{4,6},{5,7},{12,14},{13,15},{20,22},{21,23},{28,30},{29,31}} | collective-permute-start | bytes 9437192 | tf_op jit(solution)/shard_map/ppermute | solution.py:131
  357.3 102.5 %collective-permute-start.14 = (bf16[4,128,3072]{2,1,0:T(8,128)(2,1)}, bf16[4,128,3072]{2,1,0:T(8,128)(2,1)}, u32[]{:S(2)}, u32[]{:S(2)}) collective-permute-start(bf16[4,128,3072]{2,1,0:T(8,128)(2,1)} %collective-permute-done.12), channel_id=1, source_target_pairs={{2,0},{3,1},{10,8},{11,9},{18,16},{19,17},{26,24},{27,25}} | collective-permute-start | bytes 9437192 | tf_op jit(solution)/shard_map/ppermute | solution.py:132
  462.6 188.2 %all-gather.19.cloned.1.call-start = ((), (), s32[]{:S(2)}) async-start(), calls=%async_computation.11 | async-start | bytes 4718592 | tf_op jit(solution)/shard_map/all_gather | solution.py:53
  602.0 108.2 %all-gather.23.cloned.1.call-start = ((), (), s32[]{:S(2)}) async-start(), calls=%async_computation.13 | async-start | bytes 4718592 | tf_op jit(solution)/shard_map/all_gather | solution.py:53
  650.7 223.2 %reduce-scatter.9.cloned.1.call-start = ((), (), s32[]{:S(2)}) async-start(), calls=%async_computation.14 | async-start | bytes 4718592 | tf_op jit(solution)/shard_map/reduce_scatter | solution.py:57
  665.2 49.7 %collective-permute-start.26 = (bf16[4,128,3072]{2,1,0:T(8,128)(2,1)}, bf16[4,128,3072]{2,1,0:T(8,128)(2,1)}, u32[]{:S(2)}, u32[]{:S(2)}) collective-permute-start(bf16[4,128,3072]{2,1,0:T(8,128)(2,1)} %pad_maximum_fusion.4), channel_id=1, source_target_pairs={{6,4},{7,5},{14,12},{15,13},{22,20},{23,21},{30,28},{31,29}} | collective-permute-start | bytes 9437192 | tf_op jit(solution)/shard_map/ppermute | solution.py:216
  669.5 88.7 %collective-permute-start.25 = (bf16[4,128,3072]{2,1,0:T(8,128)(2,1)}, bf16[4,128,3072]{2,1,0:T(8,128)(2,1)}, u32[]{:S(2)}, u32[]{:S(2)}) collective-permute-start(bf16[4,128,3072]{2,1,0:T(8,128)(2,1)} %pad_maximum_fusion.3), channel_id=1, source_target_pairs={{0,2},{1,3},{8,10},{9,11},{16,18},{17,19},{24,26},{25,27}} | collective-permute-start | bytes 9437192 | tf_op jit(solution)/shard_map/ppermute | solution.py:213
  762.9 112.2 %collective-permute-start.40 = (bf16[4,128,3072]{2,1,0:T(8,128)(2,1)}, bf16[4,128,3072]{2,1,0:T(8,128)(2,1)}, u32[]{:S(2)}, u32[]{:S(2)}) collective-permute-start(bf16[4,128,3072]{2,1,0:T(8,128)(2,1)} %add_convert_fusion.5), channel_id=1, source_target_pairs={{4,2},{6,4},{5,3},{7,5},{12,10},{14,12},{13,11},{15,13},{20,18},{2... | collective-permute-start | bytes 9437192 | tf_op jit(solution)/shard_map/ppermute | solution.py:216
  770.0 117.3 %collective-permute-start.39 = (bf16[4,128,3072]{2,1,0:T(8,128)(2,1)}, bf16[4,128,3072]{2,1,0:T(8,128)(2,1)}, u32[]{:S(2)}, u32[]{:S(2)}) collective-permute-start(bf16[4,128,3072]{2,1,0:T(8,128)(2,1)} %add_convert_fusion.6), channel_id=1, source_target_pairs={{0,2},{2,4},{1,3},{3,5},{8,10},{10,12},{9,11},{11,13},{16,18},{18,... | collective-permute-start | bytes 9437192 | tf_op jit(solution)/shard_map/ppermute | solution.py:213
  776.3 161.0 %reduce-scatter.11.cloned.1.call-start = ((), (), s32[]{:S(2)}) async-start(), calls=%async_computation.15 | async-start | bytes 4718592 | tf_op jit(solution)/shard_map/reduce_scatter | solution.py:57
  892.9 111.5 %collective-permute-start.45 = (bf16[4,128,3072]{2,1,0:T(8,128)(2,1)}, bf16[4,128,3072]{2,1,0:T(8,128)(2,1)}, u32[]{:S(2)}, u32[]{:S(2)}) collective-permute-start(bf16[4,128,3072]{2,1,0:T(8,128)(2,1)} %add_convert_fusion.3), channel_id=1, source_target_pairs={{2,0},{4,2},{6,4},{3,1},{5,3},{7,5},{10,8},{12,10},{14,12},{11,9},... | collective-permute-start | bytes 9437192 | tf_op jit(solution)/shard_map/ppermute | solution.py:216
  899.1 105.2 %collective-permute-start.44 = (bf16[4,128,3072]{2,1,0:T(8,128)(2,1)}, bf16[4,128,3072]{2,1,0:T(8,128)(2,1)}, u32[]{:S(2)}, u32[]{:S(2)}) collective-permute-start(bf16[4,128,3072]{2,1,0:T(8,128)(2,1)} %add_convert_fusion.4), channel_id=1, source_target_pairs={{0,2},{2,4},{4,6},{1,3},{3,5},{5,7},{8,10},{10,12},{12,14},{9,11},... | collective-permute-start | bytes 9437192 | tf_op jit(solution)/shard_map/ppermute | solution.py:213
  949.1 53.4 %collective-permute-start.38 = (f32[2,128,2048]{2,1,0:T(8,128)}, f32[2,128,2048]{2,1,0:T(8,128)}, u32[]{:S(2)}, u32[]{:S(2)}) collective-permute-start(f32[2,128,2048]{2,1,0:T(8,128)} %pad_maximum_fusion.9), channel_id=1, source_target_pairs={{0,1},{1,0},{2,3},{3,2},{4,5},{5,4},{6,7},{7,6},{8,9},{9,8},{10,11... | collective-permute-start | bytes 6291464 | tf_op jit(solution)/shard_map/ppermute | solution.py:68
  951.3 48.3 %collective-permute-start.42 = (bf16[512,1024]{1,0:T(8,128)(2,1)}, bf16[512,1024]{1,0:T(8,128)(2,1)}, u32[]{:S(2)}, u32[]{:S(2)}) collective-permute-start(bf16[512,1024]{1,0:T(8,128)(2,1)} %pad_maximum_fusion.17), channel_id=1, source_target_pairs={{0,16},{8,24},{16,0},{24,8},{1,17},{9,25},{17,1},{25,9},{2,18},{10... | collective-permute-start | bytes 3145736 | tf_op jit(solution)/shard_map/ppermute | solution.py:105
  952.8 46.9 %collective-permute-start.43 = (bf16[512,1024]{1,0:T(8,128)(2,1)}, bf16[512,1024]{1,0:T(8,128)(2,1)}, u32[]{:S(2)}, u32[]{:S(2)}) collective-permute-start(bf16[512,1024]{1,0:T(8,128)(2,1)} %pad_maximum_fusion.18), channel_id=1, source_target_pairs={{0,24},{8,16},{16,8},{24,0},{1,25},{9,17},{17,9},{25,1},{2,26},{10... | collective-permute-start | bytes 3145736 | tf_op jit(solution)/shard_map/ppermute | solution.py:105
  1011.1 45.6 %collective-permute-start.49 = (bf16[128,3072]{1,0:T(8,128)(2,1)S(1)}, bf16[128,3072]{1,0:T(8,128)(2,1)}, u32[]{:S(2)}, u32[]{:S(2)}) collective-permute-start(bf16[128,3072]{1,0:T(8,128)(2,1)S(1)} %get-tuple-element.127), channel_id=1, source_target_pairs={{0,8},{8,0},{16,24},{24,16},{1,9},{9,1},{17,25},{25,17},{2,10},{10... | collective-permute-start | bytes 2359304 | tf_op jit(solution)/shard_map/ppermute | solution.py:114
  1013.3 44.6 %collective-permute-start.50 = (bf16[128,3072]{1,0:T(8,128)(2,1)}, bf16[128,3072]{1,0:T(8,128)(2,1)}, u32[]{:S(2)}, u32[]{:S(2)}) collective-permute-start(bf16[128,3072]{1,0:T(8,128)(2,1)} %get-tuple-element.126), channel_id=1, source_target_pairs={{0,16},{8,24},{16,0},{24,8},{1,17},{9,25},{17,1},{25,9},{2,18},{10... | collective-permute-start | bytes 2359304 | tf_op jit(solution)/shard_map/ppermute | solution.py:114
  1014.4 46.6 %collective-permute-start.51 = (bf16[128,3072]{1,0:T(8,128)(2,1)}, bf16[128,3072]{1,0:T(8,128)(2,1)}, u32[]{:S(2)}, u32[]{:S(2)}) collective-permute-start(bf16[128,3072]{1,0:T(8,128)(2,1)} %get-tuple-element.125), channel_id=1, source_target_pairs={{0,24},{8,16},{16,8},{24,0},{1,25},{9,17},{17,9},{25,1},{2,26},{10... | collective-permute-start | bytes 2359304 | tf_op jit(solution)/shard_map/ppermute | solution.py:114
  (156 other events, 3320.1 us)
Sparse Core Ops, SparseCore 0:
  11.6 69.4 all-gather.8
  83.2 46.9 all-gather.14
  132.2 53.2 all-gather.10
  187.2 36.5 all-gather.12
  234.6 84.4 reduce-scatter.4
  349.8 77.4 reduce-scatter.6
  429.7 45.1 all-gather.16
  476.8 36.5 all-gather.20
  602.1 44.6 all-gather.18
  650.8 59.2 all-gather.22
  776.4 91.6 reduce-scatter.8
  870.2 67.0 reduce-scatter.10

commit v5 on v4

--- a/solution.py
+++ b/solution.py
@@ -278,16 +278,21 @@
     norm_one, inverse_one = zip(*[normalize(own_tokens[slot]) for slot in each])
     norm_one_all = [gather_rows(norm_one[slot].astype(low), SEQUENCE_ROWS) for slot in each]
 
-    attention_part, *ffn_grad = lax.optimization_barrier((attention_part, *ffn_grad))
+    attention_part, ffn_block, *ffn_grad = lax.optimization_barrier(
+        (attention_part, ffn_block, *ffn_grad)
+    )
     attention_w = gather_groups(attention_part)
     qkv_w, out_w = attention_w[:, : 3 * head_cols], attention_w[:, 3 * head_cols :]
-    norm_one_all[0], ffn_block = lax.optimization_barrier((norm_one_all[0], ffn_block))
     hops = relay_hops(ffn_block)
     last = slots - 1
     ffn_grad_all = [gather_rows(ffn_grad[slot], PLANE_ROWS) for slot in each]
 
     def attend(slot):
         qkv = dot(norm_one_all[slot], qkv_w, ((1,), (0,)))
+        if slot + 1 < slots:
+            qkv, norm_one_all[slot + 1] = lax.optimization_barrier((qkv, norm_one_all[slot + 1]))
+        if slot + 1 == last:
+            norm_one_all[last] = hold(norm_one_all[last], hops, 0)
         query, key, value = (qkv[:, i * head_cols : (i + 1) * head_cols] for i in range(3))
         query = rotate(split(query), rope_cos, rope_sin).astype(low)
         key = rotate(split(key), rope_cos, rope_sin).astype(low)
@@ -301,21 +306,22 @@
         attended = attended.reshape(seq, heads * HEAD_DIM).astype(low)
         return query, key, value, probabilities, attended
 
-    saved, branch = [], []
-    for slot in each:
-        kept = attend(slot)
-        attended = kept[4]
+    saved = [attend(slot) for slot in each]
+    attended = [kept[4] for kept in saved]
+    branch = []
+    for slot in each:
+        if slot == last:
+            attended[slot], *ffn_grad_all = lax.optimization_barrier((attended[slot], *ffn_grad_all))
+        part = dot(attended[slot], out_w, ((1,), (1,))).astype(low)
+        if slot + 1 < slots:
+            part, attended[slot + 1] = lax.optimization_barrier((part, attended[slot + 1]))
         if slot == 0:
-            attended, *ffn_grad_all = lax.optimization_barrier((attended, *ffn_grad_all))
-            attended = hold(attended, hops, 0)
-        if slot == last:
-            attended = hold(attended, hops, 1)
-        saved.append(kept[:4] + (attended,))
-        branch.append(scatter_rows(dot(attended, out_w, ((1,), (1,))), SEQUENCE_ROWS))
+            part = hold(part, hops, 1)
+        branch.append(scatter_rows(part, SEQUENCE_ROWS))
     middle, norm_two, inverse_two, norm_two_all = [], [], [], []
     for slot in each:
         summed_branch = branch[slot]
-        if slot == last:
+        if slot == 0:
             summed_branch = hold(summed_branch, hops, 2)
         middle.append(own_tokens[slot] + valid_rows[slot] * summed_branch)
         normed, inverse = normalize(middle[slot])
@@ -336,7 +342,7 @@
         gate_grad = (hidden_grad * upper * sigmoid * (1.0 + gate * (1.0 - sigmoid))).astype(low)
         upper_grad = (hidden_grad * silu).astype(low)
         gate_up_grad.append(jnp.concatenate([gate_grad, upper_grad], axis=1))
-        norm_two_grad.append(scatter_plane(dot(gate_up_grad[slot], gate_up_w, ((1,), (1,)))))
+        norm_two_grad.append(dot(gate_up_grad[slot], gate_up_w, ((1,), (1,))).astype(low))
 
     def over_slots(terms):
         total = terms[0]
@@ -346,6 +352,10 @@
 
     down_sum = over_slots([dot(ffn_grad_all[slot], hidden[slot], ((0,), (0,))) for slot in each])
     gate_up_sum = over_slots([dot(norm_two_all[slot], gate_up_grad[slot], ((0,), (0,))) for slot in each])
+    norm_two_grad[last], gate_up_sum, down_sum = lax.optimization_barrier(
+        (norm_two_grad[last], gate_up_sum, down_sum)
+    )
+    norm_two_grad = [scatter_plane(norm_two_grad[slot]) for slot in each]
     ffn_sum = Reduction([gate_up_sum, down_sum], groups, contexts)
 
     middle_grad, branch_grad_all = [], []
@@ -357,15 +367,12 @@
         branch_grad_all.append(
             gather_rows((valid_rows[slot] * middle_grad[slot]).astype(low), SEQUENCE_ROWS)
         )
-    branch_grad_all[0], *ffn_sum.parts = lax.optimization_barrier((branch_grad_all[0], *ffn_sum.parts))
     ffn_sum.hop()
 
     qkv_grad, norm_one_grad = [], []
     for slot in each:
-        query, key, value, probabilities, attended = saved[slot]
+        query, key, value, probabilities, _ = saved[slot]
         attended_grad = dot(branch_grad_all[slot], out_w, ((1,), (0,))).astype(low)
-        if slot == last:
-            attended_grad = ffn_sum.hold(attended_grad)
         attended_grad = split(attended_grad)
         prob_grad = einsum("qhd,khd->hqk", attended_grad, value)
         row_delta = jnp.sum(probabilities * prob_grad, axis=-1, keepdims=True)
@@ -384,6 +391,8 @@
             )
         )
         part = dot(qkv_grad[slot], qkv_w, ((1,), (1,))).astype(low)
+        if slot + 1 == last:
+            part = ffn_sum.hold(part)
         if slot + 1 < slots:
             part, branch_grad_all[slot + 1] = lax.optimization_barrier((part, branch_grad_all[slot + 1]))
         if slot + 1 == last:
@@ -391,7 +400,7 @@
                 (branch_grad_all[last], *hidden)
             )
         norm_one_grad.append(scatter_rows(part, SEQUENCE_ROWS))
-    out_sum = over_slots([dot(branch_grad_all[slot], saved[slot][4], ((0,), (0,))) for slot in each])
+    out_sum = over_slots([dot(branch_grad_all[slot], attended[slot], ((0,), (0,))) for slot in each])
     qkv_sum = over_slots([dot(norm_one_all[slot], qkv_grad[slot], ((0,), (0,))) for slot in each])
 
     ffn_sum.hop()

time: 1090 us -> 1060 us (0.972)
  starting transfers between devices: 105 us -> 83.3 us
  waiting for transfers between devices: 460 us -> 446 us
    ppermute x3, waiting for transfers between devices: 127 us -> 68.6 us  [relay_hops(): lax.ppermute(moving_down, 'context', [(i, i - 1) for i in range(1, n - st...]
    ppermute x3, waiting for transfers between devices: 1.19 us -> 41.8 us  [relay_hops(): lax.ppermute(moving_up, 'context', [(i, i + 1) for i in range(step - 1, n...]
    reduce_scatter x4, waiting for transfers between devices: 82.3 us -> 110 us  [scatter_rows(): lax.psum_scatter(values.astype(jnp.bfloat16), axes, scatter_dimension=0,...]
    ppermute x12, waiting for transfers between devices: 51.1 us -> 27.4 us  [swap(): arrived.append(lax.ppermute(take(pieces, here ^ step), axis, route))]
    ppermute x3, waiting for transfers between devices: 55.5 us -> 69.3 us  [hop(): lax.ppermute(above.astype(jnp.bfloat16), 'context', [(i, i + 1) for i in...]
    ppermute x3, starting transfers between devices: 24.1 us -> 12.1 us  [relay_hops(): lax.ppermute(moving_up, 'context', [(i, i + 1) for i in range(step - 1, n...]
    unnamed x250 -> x252, local copies, waits for them, and re-layouts: 22.1 us -> 24.9 us
  transfers between devices with their start and end apart: 64 -> 64, of which waited for: 28 -> 21; matrix products, arithmetic and copies ran while one was open for 38% -> 44% of each run, Pallas kernels for 0% -> 0%
where the time goes in v5:
time: 1060 us; the launch traced here: 1050 us
  waiting for transfers between devices  446 us (42%)
  matrix products  251 us (24%)
  local copies, waits for them, and re-layouts  128 us (12%)
  other arithmetic  127 us (12%)
  starting transfers between devices  83.3 us (8%)
  between operations  17 us (2%)
    dot_general x24, matrix products, dot(): lax.dot_general(left, right, (dims, ((), ())), preferred_element_type=jnp...  209 us
    reduce_scatter x4, waiting for transfers between devices, scatter_rows(): lax.psum_scatter(values.astype(jnp.bfloat16), axes, scatter_dimension=0,...  110 us
    ppermute x3, waiting for transfers between devices, hop(): lax.ppermute(above.astype(jnp.bfloat16), 'context', [(i, i + 1) for i in...  69.3 us
    ppermute x3, waiting for transfers between devices, relay_hops(): lax.ppermute(moving_down, 'context', [(i, i - 1) for i in range(1, n - st...  68.6 us
    ppermute x3, waiting for transfers between devices, reduce_groups(): lax.ppermute(term(group ^ step), 'dp', route).astype(jnp.float32)  42.6 us
    ppermute x3, waiting for transfers between devices, relay_hops(): lax.ppermute(moving_up, 'context', [(i, i + 1) for i in range(step - 1, n...  41.8 us
    ppermute x16, waiting for transfers between devices, scatter_plane(): other = lax.ppermute(send, 'dp', route)  34 us
    ppermute x3, waiting for transfers between devices, gather_groups(): whole = put(whole, lax.ppermute(mine, 'dp', route), group ^ step)  29.5 us
  transfers between devices with their start and end apart: 64, of which 21 were waited for; matrix products, arithmetic and copies ran while one was open for 44% of the time, Pallas kernels for 0%

profile of v5, /device:TPU:0, one launch (start us, length us, event | category | flops | bytes accessed | tf_op | source)
XLA Modules:
  0.0 1053.4 jit_solution(2544323285758181592)
XLA Ops:
  61.3 10.2 collective-permute-done.4
  74.6 7.4 collective-permute-start.9
  97.5 14.7 %collective-permute-done.6 = bf16[4,128,1024]{2,1,0:T(8,128)(2,1)} collective-permute-done((bf16[4,128,1024]{2,1,0:T(8,128)(2,1)S(1)}, bf16[4,128,1024]{2,1,0:T(8,128)(2,1)}, u32[]{:S(2)}, u32[]{:S(2)}) %collective-permute-start.6) | collective-permute-done | bytes 1048608 | tf_op jit(solution)/shard_map/ppermute | solution.py:91
  114.5 14.9 %collective-permute-done.7 = bf16[4,128,1024]{2,1,0:T(8,128)(2,1)} collective-permute-done((bf16[4,128,1024]{2,1,0:T(8,128)(2,1)S(1)}, bf16[4,128,1024]{2,1,0:T(8,128)(2,1)}, u32[]{:S(2)}, u32[]{:S(2)}) %collective-permute-start.7) | collective-permute-done | bytes 1048608 | tf_op jit(solution)/shard_map/ppermute | solution.py:91
  133.9 41.8 %collective-permute-done.9 = bf16[4,128,3072]{2,1,0:T(8,128)(2,1)} collective-permute-done((bf16[4,128,3072]{2,1,0:T(8,128)(2,1)}, bf16[4,128,3072]{2,1,0:T(8,128)(2,1)}, u32[]{:S(2)}, u32[]{:S(2)}) %collective-permute-start.9) | collective-permute-done | bytes 3145760 | tf_op jit(solution)/shard_map/ppermute | solution.py:131
  182.9 8.3 fusion.52
  209.6 9.6 fusion.175
  229.5 7.9 fusion.176
  241.8 9.8 collective-permute-done.12
  259.9 70.7 %reduce-scatter.5.cloned.1.call-done = bf16[128,2048]{1,0:T(8,128)(2,1)} async-done(((bf16[1024,2048]{1,0:T(8,128)(2,1)}), bf16[128,2048]{1,0:T(8,128)(2,1)}) %reduce-scatter.5.cloned.1.call-update) | async-done | bytes 524304 | tf_op jit(solution)/shard_map/reduce_scatter | solution.py:57
  331.8 55.5 %collective-permute-done.14 = bf16[4,128,3072]{2,1,0:T(8,128)(2,1)} collective-permute-done((bf16[4,128,3072]{2,1,0:T(8,128)(2,1)}, bf16[4,128,3072]{2,1,0:T(8,128)(2,1)}, u32[]{:S(2)}, u32[]{:S(2)}) %collective-permute-start.14) | collective-permute-done | bytes 3145760 | tf_op jit(solution)/shard_map/ppermute | solution.py:132
  419.7 23.1 %all-gather.17.cloned.1.call-done = bf16[1024,2048]{1,0:T(8,128)(2,1)} async-done(((bf16[128,2048]{1,0:T(8,128)(2,1)}), bf16[1024,2048]{1,0:T(8,128)(2,1)}) %all-gather.17.cloned.1.call-update) | async-done | bytes 4194320 | tf_op jit(solution)/shard_map/all_gather | solution.py:53
  442.8 15.3 %fusion.10 = f32[1024,2048]{0,1:T(8,128)} fusion(bf16[1024,2048]{1,0:T(8,128)(2,1)} %all-gather.17.cloned.1.call-done, bf16[2048,3072]{1,0:T(8,128)(2,1)} %bitcast.492), kind=kOutput, calls=%fused_computation.26 | convolution fusion | flops 8589934592 | bytes 20971520 | tf_op jit(solution)/shard_map/dot_general | solution.py:49
  458.1 11.8 %multiply_convert_fusion.7 = (bf16[1024,1024]{0,1:T(8,128)(2,1)}, bf16[1024,1024]{0,1:T(8,128)(2,1)}, bf16[1024,1024]{0,1:T(8,128)(2,1)}) fusion(f32[1024,2048]{0,1:T(8,128)} %fusion.10, bf16[1024,2048]{1,0:T(8,128)(2,1)S(1)} %copy-done.103, bf16[2048,3072]{1,0:T(8,128)(2,1)} %bitcast.493), kind=kOutput, calls=%fused_computation.46 | convolution fusion | flops 4310695936 | bytes 23068672 | tf_op jit(solution)/shard_map/dot_general | solution.py:49
  469.9 12.2 %fusion.26 = bf16[1024,2048]{1,0:T(8,128)(2,1)} fusion(bf16[2048,3072]{1,0:T(8,128)(2,1)S(1)} %bitcast.501, bf16[1024,1024]{0,1:T(8,128)(2,1)} %get-tuple-element.114, bf16[1024,1024]{0,1:T(8,128)(2,1)} %get-tuple-element.113), kind=kOutput, calls=%fused_computation.60 | convolution fusion | flops 8600420352 | bytes 16777216 | tf_op jit(solution)/shard_map/dot_general | solution.py:49
  485.7 8.6 fusion.177
  494.3 13.8 %fusion.32 = f32[2048,2048]{1,0:T(8,128)} fusion(bf16[1024,2048]{1,0:T(8,128)(2,1)S(1)} %copy-done.106, bf16[1024,1024]{0,1:T(8,128)(2,1)S(1)} %copy-done.115, bf16[1024,1024]{0,1:T(8,128)(2,1)S(1)} %copy-done.114), kind=kOutput, calls=%fused_computation.75 | convolution fusion | flops 8598323200 | bytes 25165824 | tf_op jit(solution)/shard_map/dot_general | solution.py:49
  508.1 14.9 %fusion.6 = f32[1024,2048]{0,1:T(8,128)} fusion(bf16[1024,2048]{1,0:T(8,128)(2,1)} %all-gather.21.cloned.1.call-done, bf16[2048,3072]{1,0:T(8,128)(2,1)} %bitcast.494), kind=kOutput, calls=%fused_computation.22 | convolution fusion | flops 8589934592 | bytes 20971520 | tf_op jit(solution)/shard_map/dot_general | solution.py:49
  523.0 11.8 %multiply_convert_fusion.5 = (bf16[1024,1024]{0,1:T(8,128)(2,1)}, bf16[1024,1024]{0,1:T(8,128)(2,1)}, bf16[1024,1024]{0,1:T(8,128)(2,1)}) fusion(f32[1024,2048]{0,1:T(8,128)} %fusion.6, bf16[1024,2048]{1,0:T(8,128)(2,1)S(1)} %copy-done.102, bf16[2048,3072]{1,0:T(8,128)(2,1)} %bitcast.495), kind=kOutput, calls=%fused_computation.42 | convolution fusion | flops 4310695936 | bytes 23068672 | tf_op jit(solution)/shard_map/dot_general | solution.py:49
  539.6 16.8 %add_convert_fusion = bf16[2048,2048]{1,0:T(8,128)(2,1)} fusion(f32[2048,2048]{1,0:T(8,128)} %fusion.32, bf16[1024,2048]{1,0:T(8,128)(2,1)} %all-gather.21.cloned.1.call-done, bf16[1024,1024]{0,1:T(8,128)(2,1)} %get-tuple-element.112, bf16[1024,1024]{0,1:T(8,128)(2,1)} %get-tuple-element.111), kind=kOutput, calls=%fused_computation.2 | convolution fusion | flops 8606711808 | bytes 33554432 | tf_op jit(solution)/shard_map/dot_general | solution.py:49
  559.1 12.8 %fusion.29 = bf16[1024,2048]{1,0:T(8,128)(2,1)} fusion(bf16[2048,3072]{1,0:T(8,128)(2,1)} %bitcast.496, bf16[1024,1024]{0,1:T(8,128)(2,1)S(1)} %copy-done.117, bf16[1024,1024]{0,1:T(8,128)(2,1)S(1)} %copy-done.116), kind=kOutput, calls=%fused_computation.61 | convolution fusion | flops 8600420352 | bytes 16777216 | tf_op jit(solution)/shard_map/dot_general | solution.py:49
  575.0 10.0 add_convert_fusion.1
  592.6 10.0 dynamic-slice_bitcast_fusion
  610.1 8.0 collective-permute-done.23
  657.6 69.3 %collective-permute-done.20 = bf16[4,128,3072]{2,1,0:T(8,128)(2,1)} collective-permute-done((bf16[4,128,3072]{2,1,0:T(8,128)(2,1)}, bf16[4,128,3072]{2,1,0:T(8,128)(2,1)}, u32[]{:S(2)}, u32[]{:S(2)}) %collective-permute-start.20) | collective-permute-done | bytes 3145760 | tf_op jit(solution)/shard_map/ppermute | solution.py:213
  753.8 7.4 convolution_convert_fusion.4
  777.5 8.7 convolution_convert_fusion.5
  804.0 7.2 add_convert_fusion.7
  818.9 9.7 collective-permute-done.33
  878.7 38.8 %reduce-scatter.11.cloned.1.call-done = bf16[128,2048]{1,0:T(8,128)(2,1)} async-done(((bf16[1024,2048]{1,0:T(8,128)(2,1)}), bf16[128,2048]{1,0:T(8,128)(2,1)}) %reduce-scatter.11.cloned.1.call-update) | async-done | bytes 524304 | tf_op jit(solution)/shard_map/reduce_scatter | solution.py:57
  932.3 42.6 %collective-permute-done.42 = bf16[512,1024]{1,0:T(8,128)(2,1)} collective-permute-done((bf16[512,1024]{1,0:T(8,128)(2,1)}, bf16[512,1024]{1,0:T(8,128)(2,1)}, u32[]{:S(2)}, u32[]{:S(2)}) %collective-permute-start.42) | collective-permute-done | bytes 1048608 | tf_op jit(solution)/shard_map/ppermute | solution.py:105
  1007.4 11.5 %collective-permute-done.47 = bf16[128,1024]{1,0:T(8,128)(2,1)} collective-permute-done((bf16[128,1024]{1,0:T(8,128)(2,1)}, bf16[128,1024]{1,0:T(8,128)(2,1)}, u32[]{:S(2)}, u32[]{:S(2)}) %collective-permute-start.47) | collective-permute-done | bytes 262176 | tf_op jit(solution)/shard_map/ppermute | solution.py:114
  (610 shorter events, 421.2 us)
Async XLA Ops:
  7.2 175.7 %all-gather.9.cloned.1.call-start = ((), (), s32[]{:S(2)}) async-start(), calls=%async_computation.4 | async-start | bytes 4718592 | tf_op jit(solution)/shard_map/all_gather | solution.py:53
  11.5 179.7 %all-gather.11.cloned.1.call-start = ((), (), s32[]{:S(2)}) async-start(), calls=%async_computation.5 | async-start | bytes 4718592 | tf_op jit(solution)/shard_map/all_gather | solution.py:53
  13.9 237.8 %all-gather.13.cloned.1.call-start = ((), (), s32[]{:S(2)}) async-start(), calls=%async_computation.7 | async-start | bytes 4718592 | tf_op jit(solution)/shard_map/all_gather | solution.py:53
  74.6 177.1 %all-gather.15.cloned.1.call-start = ((), (), s32[]{:S(2)}) async-start(), calls=%async_computation.8 | async-start | bytes 4718592 | tf_op jit(solution)/shard_map/all_gather | solution.py:53
  74.6 101.1 %collective-permute-start.9 = (bf16[4,128,3072]{2,1,0:T(8,128)(2,1)}, bf16[4,128,3072]{2,1,0:T(8,128)(2,1)}, u32[]{:S(2)}, u32[]{:S(2)}) collective-permute-start(bf16[4,128,3072]{2,1,0:T(8,128)(2,1)} %bitcast_dynamic-update-slice_fusion.8), channel_id=1, source_target_pairs={{0,2},{2,4},{4,6},{1,3},{3,5},{5,7},{8,10},{10,12},{12,14},{9,11},... | collective-permute-start | bytes 9437192 | tf_op jit(solution)/shard_map/ppermute | solution.py:131
  82.0 99.4 %collective-permute-start.10 = (bf16[4,128,3072]{2,1,0:T(8,128)(2,1)}, bf16[4,128,3072]{2,1,0:T(8,128)(2,1)}, u32[]{:S(2)}, u32[]{:S(2)}) collective-permute-start(bf16[4,128,3072]{2,1,0:T(8,128)(2,1)} %bitcast_dynamic-update-slice_fusion.8), channel_id=1, source_target_pairs={{2,0},{4,2},{6,4},{3,1},{5,3},{7,5},{10,8},{12,10},{14,12},{11,9},... | collective-permute-start | bytes 9437192 | tf_op jit(solution)/shard_map/ppermute | solution.py:132
  93.9 236.7 %reduce-scatter.5.cloned.1.call-start = ((), (), s32[]{:S(2)}) async-start(), calls=%async_computation.6 | async-start | bytes 4718592 | tf_op jit(solution)/shard_map/reduce_scatter | solution.py:57
  175.7 66.1 %collective-permute-start.11 = (bf16[4,128,3072]{2,1,0:T(8,128)(2,1)}, bf16[4,128,3072]{2,1,0:T(8,128)(2,1)}, u32[]{:S(2)}, u32[]{:S(2)}) collective-permute-start(bf16[4,128,3072]{2,1,0:T(8,128)(2,1)} %collective-permute-done.9), channel_id=1, source_target_pairs={{2,4},{4,6},{3,5},{5,7},{10,12},{12,14},{11,13},{13,15},{18,20},{2... | collective-permute-start | bytes 9437192 | tf_op jit(solution)/shard_map/ppermute | solution.py:131
  181.4 70.1 %collective-permute-start.12 = (bf16[4,128,3072]{2,1,0:T(8,128)(2,1)}, bf16[4,128,3072]{2,1,0:T(8,128)(2,1)}, u32[]{:S(2)}, u32[]{:S(2)}) collective-permute-start(bf16[4,128,3072]{2,1,0:T(8,128)(2,1)} %collective-permute-done.10), channel_id=1, source_target_pairs={{2,0},{4,2},{3,1},{5,3},{10,8},{12,10},{11,9},{13,11},{18,16},{20,... | collective-permute-start | bytes 9437192 | tf_op jit(solution)/shard_map/ppermute | solution.py:132
  251.6 162.9 %reduce-scatter.7.cloned.1.call-start = ((), (), s32[]{:S(2)}) async-start(), calls=%async_computation.11 | async-start | bytes 4718592 | tf_op jit(solution)/shard_map/reduce_scatter | solution.py:57
  256.2 186.5 %all-gather.17.cloned.1.call-start = ((), (), s32[]{:S(2)}) async-start(), calls=%async_computation.9 | async-start | bytes 4718592 | tf_op jit(solution)/shard_map/all_gather | solution.py:53
  256.3 75.5 %collective-permute-start.13 = (bf16[4,128,3072]{2,1,0:T(8,128)(2,1)}, bf16[4,128,3072]{2,1,0:T(8,128)(2,1)}, u32[]{:S(2)}, u32[]{:S(2)}) collective-permute-start(bf16[4,128,3072]{2,1,0:T(8,128)(2,1)} %collective-permute-done.11), channel_id=1, source_target_pairs={{4,6},{5,7},{12,14},{13,15},{20,22},{21,23},{28,30},{29,31}} | collective-permute-start | bytes 9437192 | tf_op jit(solution)/shard_map/ppermute | solution.py:131
  258.6 128.7 %collective-permute-start.14 = (bf16[4,128,3072]{2,1,0:T(8,128)(2,1)}, bf16[4,128,3072]{2,1,0:T(8,128)(2,1)}, u32[]{:S(2)}, u32[]{:S(2)}) collective-permute-start(bf16[4,128,3072]{2,1,0:T(8,128)(2,1)} %collective-permute-done.12), channel_id=1, source_target_pairs={{2,0},{3,1},{10,8},{11,9},{18,16},{19,17},{26,24},{27,25}} | collective-permute-start | bytes 9437192 | tf_op jit(solution)/shard_map/ppermute | solution.py:132
  390.1 118.0 %all-gather.21.cloned.1.call-start = ((), (), s32[]{:S(2)}) async-start(), calls=%async_computation.12 | async-start | bytes 4718592 | tf_op jit(solution)/shard_map/all_gather | solution.py:53
  419.6 211.1 %all-gather.19.cloned.1.call-start = ((), (), s32[]{:S(2)}) async-start(), calls=%async_computation.10 | async-start | bytes 4718592 | tf_op jit(solution)/shard_map/all_gather | solution.py:53
  485.4 49.4 %collective-permute-start.15 = (bf16[4,128,2048]{2,1,0:T(8,128)(2,1)}, bf16[4,128,2048]{2,1,0:T(8,128)(2,1)S(1)}, u32[]{:S(2)}, u32[]{:S(2)}) collective-permute-start(bf16[4,128,2048]{2,1,0:T(8,128)(2,1)} %dynamic-slice_bitcast_fusion.10), channel_id=1, source_target_pairs={{0,1},{1,0},{2,3},{3,2},{4,5},{5,4},{6,7},{7,6},{8,9},{9,8},{10,11... | collective-permute-start | bytes 6291464 | tf_op jit(solution)/shard_map/ppermute | solution.py:170
  575.0 178.8 %all-gather.23.cloned.1.call-start = ((), (), s32[]{:S(2)}) async-start(), calls=%async_computation.13 | async-start | bytes 4718592 | tf_op jit(solution)/shard_map/all_gather | solution.py:53
  607.8 49.8 %collective-permute-start.21 = (bf16[4,128,3072]{2,1,0:T(8,128)(2,1)}, bf16[4,128,3072]{2,1,0:T(8,128)(2,1)}, u32[]{:S(2)}, u32[]{:S(2)}) collective-permute-start(bf16[4,128,3072]{2,1,0:T(8,128)(2,1)} %pad_maximum_fusion.4), channel_id=1, source_target_pairs={{6,4},{7,5},{14,12},{15,13},{22,20},{23,21},{30,28},{31,29}} | collective-permute-start | bytes 9437192 | tf_op jit(solution)/shard_map/ppermute | solution.py:216
  622.8 104.0 %collective-permute-start.20 = (bf16[4,128,3072]{2,1,0:T(8,128)(2,1)}, bf16[4,128,3072]{2,1,0:T(8,128)(2,1)}, u32[]{:S(2)}, u32[]{:S(2)}) collective-permute-start(bf16[4,128,3072]{2,1,0:T(8,128)(2,1)} %pad_maximum_fusion.3), channel_id=1, source_target_pairs={{0,2},{1,3},{8,10},{9,11},{16,18},{17,19},{24,26},{25,27}} | collective-permute-start | bytes 9437192 | tf_op jit(solution)/shard_map/ppermute | solution.py:213
  630.6 223.7 %reduce-scatter.9.cloned.1.call-start = ((), (), s32[]{:S(2)}) async-start(), calls=%async_computation.14 | async-start | bytes 4718592 | tf_op jit(solution)/shard_map/reduce_scatter | solution.py:57
  732.8 123.7 %collective-permute-start.40 = (bf16[4,128,3072]{2,1,0:T(8,128)(2,1)}, bf16[4,128,3072]{2,1,0:T(8,128)(2,1)}, u32[]{:S(2)}, u32[]{:S(2)}) collective-permute-start(bf16[4,128,3072]{2,1,0:T(8,128)(2,1)} %add_convert_fusion.5), channel_id=1, source_target_pairs={{4,2},{6,4},{5,3},{7,5},{12,10},{14,12},{13,11},{15,13},{20,18},{2... | collective-permute-start | bytes 9437192 | tf_op jit(solution)/shard_map/ppermute | solution.py:216
  740.0 116.4 %collective-permute-start.39 = (bf16[4,128,3072]{2,1,0:T(8,128)(2,1)}, bf16[4,128,3072]{2,1,0:T(8,128)(2,1)}, u32[]{:S(2)}, u32[]{:S(2)}) collective-permute-start(bf16[4,128,3072]{2,1,0:T(8,128)(2,1)} %add_convert_fusion.6), channel_id=1, source_target_pairs={{0,2},{2,4},{1,3},{3,5},{8,10},{10,12},{9,11},{11,13},{16,18},{18,... | collective-permute-start | bytes 9437192 | tf_op jit(solution)/shard_map/ppermute | solution.py:213
  753.8 163.7 %reduce-scatter.11.cloned.1.call-start = ((), (), s32[]{:S(2)}) async-start(), calls=%async_computation.15 | async-start | bytes 4718592 | tf_op jit(solution)/shard_map/reduce_scatter | solution.py:57
  764.8 46.3 %collective-permute-start.32 = (bf16[4,128,2048]{2,1,0:T(8,128)(2,1)}, bf16[4,128,2048]{2,1,0:T(8,128)(2,1)}, u32[]{:S(2)}, u32[]{:S(2)}) collective-permute-start(bf16[4,128,2048]{2,1,0:T(8,128)(2,1)} %dynamic-slice_bitcast_fusion.5), channel_id=1, source_target_pairs={{0,1},{1,0},{2,3},{3,2},{4,5},{5,4},{6,7},{7,6},{8,9},{9,8},{10,11... | collective-permute-start | bytes 6291464 | tf_op jit(solution)/shard_map/ppermute | solution.py:170
  862.4 117.1 %collective-permute-start.45 = (bf16[4,128,3072]{2,1,0:T(8,128)(2,1)}, bf16[4,128,3072]{2,1,0:T(8,128)(2,1)}, u32[]{:S(2)}, u32[]{:S(2)}) collective-permute-start(bf16[4,128,3072]{2,1,0:T(8,128)(2,1)} %add_convert_fusion.3), channel_id=1, source_target_pairs={{2,0},{4,2},{6,4},{3,1},{5,3},{7,5},{10,8},{12,10},{14,12},{11,9},... | collective-permute-start | bytes 9437192 | tf_op jit(solution)/shard_map/ppermute | solution.py:216
  868.6 110.9 %collective-permute-start.44 = (bf16[4,128,3072]{2,1,0:T(8,128)(2,1)}, bf16[4,128,3072]{2,1,0:T(8,128)(2,1)}, u32[]{:S(2)}, u32[]{:S(2)}) collective-permute-start(bf16[4,128,3072]{2,1,0:T(8,128)(2,1)} %add_convert_fusion.4), channel_id=1, source_target_pairs={{0,2},{2,4},{4,6},{1,3},{3,5},{5,7},{8,10},{10,12},{12,14},{9,11},... | collective-permute-start | bytes 9437192 | tf_op jit(solution)/shard_map/ppermute | solution.py:213
  877.8 49.2 %collective-permute-start.41 = (bf16[512,1024]{1,0:T(8,128)(2,1)}, bf16[512,1024]{1,0:T(8,128)(2,1)}, u32[]{:S(2)}, u32[]{:S(2)}) collective-permute-start(bf16[512,1024]{1,0:T(8,128)(2,1)} %pad_maximum_fusion.16), channel_id=1, source_target_pairs={{0,8},{8,0},{16,24},{24,16},{1,9},{9,1},{17,25},{25,17},{2,10},{10... | collective-permute-start | bytes 3145736 | tf_op jit(solution)/shard_map/ppermute | solution.py:105
  924.3 53.4 %collective-permute-start.38 = (f32[2,128,2048]{2,1,0:T(8,128)}, f32[2,128,2048]{2,1,0:T(8,128)}, u32[]{:S(2)}, u32[]{:S(2)}) collective-permute-start(f32[2,128,2048]{2,1,0:T(8,128)} %pad_maximum_fusion.9), channel_id=1, source_target_pairs={{0,1},{1,0},{2,3},{3,2},{4,5},{5,4},{6,7},{7,6},{8,9},{9,8},{10,11... | collective-permute-start | bytes 6291464 | tf_op jit(solution)/shard_map/ppermute | solution.py:68
  927.0 47.9 %collective-permute-start.42 = (bf16[512,1024]{1,0:T(8,128)(2,1)}, bf16[512,1024]{1,0:T(8,128)(2,1)}, u32[]{:S(2)}, u32[]{:S(2)}) collective-permute-start(bf16[512,1024]{1,0:T(8,128)(2,1)} %pad_maximum_fusion.17), channel_id=1, source_target_pairs={{0,16},{8,24},{16,0},{24,8},{1,17},{9,25},{17,1},{25,9},{2,18},{10... | collective-permute-start | bytes 3145736 | tf_op jit(solution)/shard_map/ppermute | solution.py:105
  927.7 47.2 %collective-permute-start.43 = (bf16[512,1024]{1,0:T(8,128)(2,1)}, bf16[512,1024]{1,0:T(8,128)(2,1)}, u32[]{:S(2)}, u32[]{:S(2)}) collective-permute-start(bf16[512,1024]{1,0:T(8,128)(2,1)} %pad_maximum_fusion.18), channel_id=1, source_target_pairs={{0,24},{8,16},{16,8},{24,0},{1,25},{9,17},{17,9},{25,1},{2,26},{10... | collective-permute-start | bytes 3145736 | tf_op jit(solution)/shard_map/ppermute | solution.py:105
  986.3 43.7 %collective-permute-start.49 = (bf16[128,3072]{1,0:T(8,128)(2,1)S(1)}, bf16[128,3072]{1,0:T(8,128)(2,1)}, u32[]{:S(2)}, u32[]{:S(2)}) collective-permute-start(bf16[128,3072]{1,0:T(8,128)(2,1)S(1)} %get-tuple-element.133), channel_id=1, source_target_pairs={{0,8},{8,0},{16,24},{24,16},{1,9},{9,1},{17,25},{25,17},{2,10},{10... | collective-permute-start | bytes 2359304 | tf_op jit(solution)/shard_map/ppermute | solution.py:114
  990.0 44.3 %collective-permute-start.51 = (bf16[128,3072]{1,0:T(8,128)(2,1)}, bf16[128,3072]{1,0:T(8,128)(2,1)}, u32[]{:S(2)}, u32[]{:S(2)}) collective-permute-start(bf16[128,3072]{1,0:T(8,128)(2,1)} %get-tuple-element.131), channel_id=1, source_target_pairs={{0,24},{8,16},{16,8},{24,0},{1,25},{9,17},{17,9},{25,1},{2,26},{10... | collective-permute-start | bytes 2359304 | tf_op jit(solution)/shard_map/ppermute | solution.py:114
  (157 other events, 3182.4 us)
Sparse Core Ops, SparseCore 0:
  11.6 69.2 all-gather.8
  83.1 76.9 all-gather.10
  162.0 40.2 all-gather.12
  204.0 36.5 all-gather.14
  251.7 78.8 reduce-scatter.4
  332.7 69.6 reduce-scatter.6
  404.9 37.7 all-gather.16
  445.2 36.5 all-gather.20
  575.1 45.6 all-gather.18
  630.7 75.6 all-gather.22
  753.9 86.4 reduce-scatter.8
  842.5 74.9 reduce-scatter.10

commit v6 on v5

--- a/solution.py
+++ b/solution.py
@@ -391,38 +391,34 @@
             )
         )
         part = dot(qkv_grad[slot], qkv_w, ((1,), (1,))).astype(low)
-        if slot + 1 == last:
+        if slot == last:
+            ffn_sum.hop()
+        if slot + 1 >= last:
             part = ffn_sum.hold(part)
         if slot + 1 < slots:
             part, branch_grad_all[slot + 1] = lax.optimization_barrier((part, branch_grad_all[slot + 1]))
-        if slot + 1 == last:
-            branch_grad_all[last], *hidden_late = lax.optimization_barrier(
-                (branch_grad_all[last], *hidden)
-            )
         norm_one_grad.append(scatter_rows(part, SEQUENCE_ROWS))
     out_sum = over_slots([dot(branch_grad_all[slot], attended[slot], ((0,), (0,))) for slot in each])
     qkv_sum = over_slots([dot(norm_one_all[slot], qkv_grad[slot], ((0,), (0,))) for slot in each])
 
-    ffn_sum.hop()
-    qkv_sum, norm_one_grad[0] = lax.optimization_barrier((qkv_sum, norm_one_grad[0]))
-    qkv_sum = ffn_sum.hold(qkv_sum)
+    attention_total = reduce_groups([qkv_sum, out_sum])
+    attention_total, *hidden_late = lax.optimization_barrier((attention_total, *hidden))
 
     layer_out, input_grad = [], []
     for slot in each:
         feedforward = scatter_plane(dot(hidden_late[slot], down_w, ((1,), (1,))))
         layer_out.append((middle[slot] + valid_rows[slot] * feedforward).astype(low))
     ffn_sum.hop()
-    norm_one_grad[0], *layer_out = lax.optimization_barrier((norm_one_grad[0], *layer_out))
-    attention_total = ffn_sum.hold(reduce_groups([qkv_sum, out_sum]))
+    attention_pieces = swap(attention_total.reshape(contexts, -1, 4 * head_cols), "context")
     for slot in each:
         upstream = norm_one_grad[slot]
         input_grad.append(
             middle_grad[slot] + normalize_back(norm_one[slot], inverse_one[slot], upstream)
         )
     layer_out, input_grad = join_cores(jnp.stack(layer_out)), join_cores(jnp.stack(input_grad))
+    layer_out, input_grad, *attention_pieces = ffn_sum.hold((layer_out, input_grad, *attention_pieces))
 
     ffn_pieces = ffn_sum.finish()
-    attention_pieces = swap(attention_total.reshape(contexts, -1, 4 * head_cols), "context")
 
     def column_output(pieces, axis, start, size):
         members, here = lax.axis_size(axis), lax.axis_index(axis)

time: 1060 us -> 1070 us (level)
    ppermute x12, waiting for transfers between devices: 27.4 us -> 68.7 us  [swap(): arrived.append(lax.ppermute(take(pieces, here ^ step), axis, route))]
    reduce_scatter x4, waiting for transfers between devices: 110 us -> 68.3 us  [scatter_rows(): lax.psum_scatter(values.astype(jnp.bfloat16), axes, scatter_dimension=0,...]
    unnamed x252 -> x246, local copies, waits for them, and re-layouts: 24.9 us -> 29.5 us
  transfers between devices with their start and end apart: 64 -> 64, of which waited for: 21 -> 24; matrix products, arithmetic and copies ran while one was open for 44% -> 44% of each run, Pallas kernels for 0% -> 0%
where the time goes in v6:
time: 1070 us; the launch traced here: 1060 us
  waiting for transfers between devices  446 us (42%)
  matrix products  250 us (23%)
  local copies, waits for them, and re-layouts  137 us (13%)
  other arithmetic  129 us (12%)
  starting transfers between devices  76.7 us (7%)
  between operations  16.6 us (2%)
    dot_general x24, matrix products, dot(): lax.dot_general(left, right, (dims, ((), ())), preferred_element_type=jnp...  202 us
    ppermute x3, waiting for transfers between devices, relay_hops(): lax.ppermute(moving_down, 'context', [(i, i - 1) for i in range(1, n - st...  72.3 us
    ppermute x3, waiting for transfers between devices, hop(): lax.ppermute(above.astype(jnp.bfloat16), 'context', [(i, i + 1) for i in...  69.4 us
    ppermute x12, waiting for transfers between devices, swap(): arrived.append(lax.ppermute(take(pieces, here ^ step), axis, route))  68.7 us
    reduce_scatter x4, waiting for transfers between devices, scatter_rows(): lax.psum_scatter(values.astype(jnp.bfloat16), axes, scatter_dimension=0,...  68.3 us
    ppermute x3, waiting for transfers between devices, relay_hops(): lax.ppermute(moving_up, 'context', [(i, i + 1) for i in range(step - 1, n...  42.5 us
    ppermute x3, waiting for transfers between devices, reduce_groups(): lax.ppermute(term(group ^ step), 'dp', route).astype(jnp.float32)  35.3 us
    ppermute x16, waiting for transfers between devices, scatter_plane(): other = lax.ppermute(send, 'dp', route)  34.8 us
  transfers between devices with their start and end apart: 64, of which 24 were waited for; matrix products, arithmetic and copies ran while one was open for 44% of the time, Pallas kernels for 0%

profile of v6, /device:TPU:0, one launch (start us, length us, event | category | flops | bytes accessed | tf_op | source)
XLA Modules:
  0.0 1055.5 jit_solution(9451380475665489076)
XLA Ops:
  66.9 9.5 collective-permute-done.5
  97.6 14.7 %collective-permute-done.6 = bf16[4,128,1024]{2,1,0:T(8,128)(2,1)} collective-permute-done((bf16[4,128,1024]{2,1,0:T(8,128)(2,1)S(1)}, bf16[4,128,1024]{2,1,0:T(8,128)(2,1)}, u32[]{:S(2)}, u32[]{:S(2)}) %collective-permute-start.6) | collective-permute-done | bytes 1048608 | tf_op jit(solution)/shard_map/ppermute | solution.py:91
  114.6 17.5 %collective-permute-done.7 = bf16[4,128,1024]{2,1,0:T(8,128)(2,1)} collective-permute-done((bf16[4,128,1024]{2,1,0:T(8,128)(2,1)S(1)}, bf16[4,128,1024]{2,1,0:T(8,128)(2,1)}, u32[]{:S(2)}, u32[]{:S(2)}) %collective-permute-start.7) | collective-permute-done | bytes 1048608 | tf_op jit(solution)/shard_map/ppermute | solution.py:91
  136.6 42.5 %collective-permute-done.9 = bf16[4,128,3072]{2,1,0:T(8,128)(2,1)} collective-permute-done((bf16[4,128,3072]{2,1,0:T(8,128)(2,1)}, bf16[4,128,3072]{2,1,0:T(8,128)(2,1)}, u32[]{:S(2)}, u32[]{:S(2)}) %collective-permute-start.9) | collective-permute-done | bytes 3145760 | tf_op jit(solution)/shard_map/ppermute | solution.py:131
  186.5 8.9 fusion.52
  213.8 9.4 fusion.175
  234.0 8.1 fusion.176
  246.5 7.4 collective-permute-done.12
  262.2 66.0 %reduce-scatter.5.cloned.1.call-done = bf16[128,2048]{1,0:T(8,128)(2,1)} async-done(((bf16[1024,2048]{1,0:T(8,128)(2,1)}), bf16[128,2048]{1,0:T(8,128)(2,1)}) %reduce-scatter.5.cloned.1.call-update) | async-done | bytes 524304 | tf_op jit(solution)/shard_map/reduce_scatter | solution.py:57
  329.4 61.5 %collective-permute-done.14 = bf16[4,128,3072]{2,1,0:T(8,128)(2,1)} collective-permute-done((bf16[4,128,3072]{2,1,0:T(8,128)(2,1)}, bf16[4,128,3072]{2,1,0:T(8,128)(2,1)}, u32[]{:S(2)}, u32[]{:S(2)}) %collective-permute-start.14) | collective-permute-done | bytes 3145760 | tf_op jit(solution)/shard_map/ppermute | solution.py:132
  423.4 21.3 %all-gather.17.cloned.1.call-done = bf16[1024,2048]{1,0:T(8,128)(2,1)} async-done(((bf16[128,2048]{1,0:T(8,128)(2,1)}), bf16[1024,2048]{1,0:T(8,128)(2,1)}) %all-gather.17.cloned.1.call-update) | async-done | bytes 4194320 | tf_op jit(solution)/shard_map/all_gather | solution.py:53
  444.8 15.0 %fusion.10 = f32[1024,2048]{0,1:T(8,128)} fusion(bf16[1024,2048]{1,0:T(8,128)(2,1)} %all-gather.17.cloned.1.call-done, bf16[2048,3072]{1,0:T(8,128)(2,1)} %bitcast.494), kind=kOutput, calls=%fused_computation.26 | convolution fusion | flops 8589934592 | bytes 20971520 | tf_op jit(solution)/shard_map/dot_general | solution.py:49
  459.8 11.8 %multiply_convert_fusion.7 = (bf16[1024,1024]{0,1:T(8,128)(2,1)}, bf16[1024,1024]{0,1:T(8,128)(2,1)}, bf16[1024,1024]{0,1:T(8,128)(2,1)}) fusion(f32[1024,2048]{0,1:T(8,128)} %fusion.10, bf16[1024,2048]{1,0:T(8,128)(2,1)S(1)} %copy-done.97, bf16[2048,3072]{1,0:T(8,128)(2,1)} %bitcast.495), kind=kOutput, calls=%fused_computation.46 | convolution fusion | flops 4310695936 | bytes 23068672 | tf_op jit(solution)/shard_map/dot_general | solution.py:49
  471.6 12.2 %fusion.26 = bf16[1024,2048]{1,0:T(8,128)(2,1)} fusion(bf16[2048,3072]{1,0:T(8,128)(2,1)S(1)} %bitcast.503, bf16[1024,1024]{0,1:T(8,128)(2,1)} %get-tuple-element.114, bf16[1024,1024]{0,1:T(8,128)(2,1)} %get-tuple-element.113), kind=kOutput, calls=%fused_computation.60 | convolution fusion | flops 8600420352 | bytes 16777216 | tf_op jit(solution)/shard_map/dot_general | solution.py:49
  487.4 8.6 fusion.177
  496.0 13.8 %fusion.32 = f32[2048,2048]{1,0:T(8,128)} fusion(bf16[1024,2048]{1,0:T(8,128)(2,1)S(1)} %copy-done.100, bf16[1024,1024]{0,1:T(8,128)(2,1)S(1)} %copy-done.110, bf16[1024,1024]{0,1:T(8,128)(2,1)S(1)} %copy-done.109), kind=kOutput, calls=%fused_computation.75 | convolution fusion | flops 8598323200 | bytes 25165824 | tf_op jit(solution)/shard_map/dot_general | solution.py:49
  509.8 15.2 %fusion.6 = f32[1024,2048]{0,1:T(8,128)} fusion(bf16[1024,2048]{1,0:T(8,128)(2,1)} %all-gather.21.cloned.1.call-done, bf16[2048,3072]{1,0:T(8,128)(2,1)} %bitcast.496), kind=kOutput, calls=%fused_computation.22 | convolution fusion | flops 8589934592 | bytes 20971520 | tf_op jit(solution)/shard_map/dot_general | solution.py:49
  525.0 11.8 %multiply_convert_fusion.5 = (bf16[1024,1024]{0,1:T(8,128)(2,1)}, bf16[1024,1024]{0,1:T(8,128)(2,1)}, bf16[1024,1024]{0,1:T(8,128)(2,1)}) fusion(f32[1024,2048]{0,1:T(8,128)} %fusion.6, bf16[1024,2048]{1,0:T(8,128)(2,1)S(1)} %copy-done.96, bf16[2048,3072]{1,0:T(8,128)(2,1)} %bitcast.497), kind=kOutput, calls=%fused_computation.42 | convolution fusion | flops 4310695936 | bytes 23068672 | tf_op jit(solution)/shard_map/dot_general | solution.py:49
  541.5 16.8 %add_convert_fusion = bf16[2048,2048]{1,0:T(8,128)(2,1)} fusion(f32[2048,2048]{1,0:T(8,128)} %fusion.32, bf16[1024,2048]{1,0:T(8,128)(2,1)} %all-gather.21.cloned.1.call-done, bf16[1024,1024]{0,1:T(8,128)(2,1)} %get-tuple-element.112, bf16[1024,1024]{0,1:T(8,128)(2,1)} %get-tuple-element.111), kind=kOutput, calls=%fused_computation.2 | convolution fusion | flops 8606711808 | bytes 33554432 | tf_op jit(solution)/shard_map/dot_general | solution.py:49
  561.0 12.8 %fusion.29 = bf16[1024,2048]{1,0:T(8,128)(2,1)} fusion(bf16[2048,3072]{1,0:T(8,128)(2,1)} %bitcast.498, bf16[1024,1024]{0,1:T(8,128)(2,1)S(1)} %copy-done.112, bf16[1024,1024]{0,1:T(8,128)(2,1)S(1)} %copy-done.111), kind=kOutput, calls=%fused_computation.61 | convolution fusion | flops 8600420352 | bytes 16777216 | tf_op jit(solution)/shard_map/dot_general | solution.py:49
  576.9 10.3 add_convert_fusion.1
  594.7 10.0 dynamic-slice_bitcast_fusion
  612.3 8.0 collective-permute-done.23
  659.8 69.4 %collective-permute-done.20 = bf16[4,128,3072]{2,1,0:T(8,128)(2,1)} collective-permute-done((bf16[4,128,3072]{2,1,0:T(8,128)(2,1)}, bf16[4,128,3072]{2,1,0:T(8,128)(2,1)}, u32[]{:S(2)}, u32[]{:S(2)}) %collective-permute-start.20) | collective-permute-done | bytes 3145760 | tf_op jit(solution)/shard_map/ppermute | solution.py:213
  760.2 8.1 multiply_reduce_fusion
  768.4 7.8 multiply_convert_fusion
  806.9 13.6 %collective-permute-done.27 = bf16[512,1024]{1,0:T(8,128)(2,1)S(1)} collective-permute-done((bf16[512,1024]{1,0:T(8,128)(2,1)}, bf16[512,1024]{1,0:T(8,128)(2,1)S(1)}, u32[]{:S(2)}, u32[]{:S(2)}) %collective-permute-start.27) | collective-permute-done | bytes 1048608 | tf_op jit(solution)/shard_map/ppermute | solution.py:105
  820.5 21.7 %collective-permute-done.28 = bf16[512,1024]{1,0:T(8,128)(2,1)} collective-permute-done((bf16[512,1024]{1,0:T(8,128)(2,1)}, bf16[512,1024]{1,0:T(8,128)(2,1)}, u32[]{:S(2)}, u32[]{:S(2)}) %collective-permute-start.28) | collective-permute-done | bytes 1048608 | tf_op jit(solution)/shard_map/ppermute | solution.py:105
  890.0 10.9 %collective-permute-done.36 = bf16[2,128,1024]{2,1,0:T(8,128)(2,1)S(1)} collective-permute-done((bf16[2,128,1024]{2,1,0:T(8,128)(2,1)S(1)}, bf16[2,128,1024]{2,1,0:T(8,128)(2,1)S(1)}, u32[]{:S(2)}, u32[]{:S(2)}) %collective-permute-start.36) | collective-permute-done | bytes 524320 | tf_op jit(solution)/shard_map/ppermute | solution.py:185
  903.5 7.6 collective-permute-done.31
  950.2 30.3 %collective-permute-done.44 = bf16[128,1024]{1,0:T(8,128)(2,1)S(1)} collective-permute-done((bf16[128,1024]{1,0:T(8,128)(2,1)S(1)}, bf16[128,1024]{1,0:T(8,128)(2,1)S(1)}, u32[]{:S(2)}, u32[]{:S(2)}) %collective-permute-start.44) | collective-permute-done | bytes 262176 | tf_op jit(solution)/shard_map/ppermute | solution.py:114
  1015.1 15.7 %collective-permute-done.50 = bf16[128,3072]{1,0:T(8,128)(2,1)} collective-permute-done((bf16[128,3072]{1,0:T(8,128)(2,1)}, bf16[128,3072]{1,0:T(8,128)(2,1)}, u32[]{:S(2)}, u32[]{:S(2)}) %collective-permute-start.50) | collective-permute-done | bytes 786464 | tf_op jit(solution)/shard_map/ppermute | solution.py:114
  (604 shorter events, 440.4 us)
Async XLA Ops:
  7.2 179.3 %all-gather.9.cloned.1.call-start = ((), (), s32[]{:S(2)}) async-start(), calls=%async_computation.4 | async-start | bytes 4718592 | tf_op jit(solution)/shard_map/all_gather | solution.py:53
  11.5 183.8 %all-gather.11.cloned.1.call-start = ((), (), s32[]{:S(2)}) async-start(), calls=%async_computation.5 | async-start | bytes 4718592 | tf_op jit(solution)/shard_map/all_gather | solution.py:53
  14.0 239.9 %all-gather.13.cloned.1.call-start = ((), (), s32[]{:S(2)}) async-start(), calls=%async_computation.7 | async-start | bytes 4718592 | tf_op jit(solution)/shard_map/all_gather | solution.py:53
  17.0 40.3 %collective-permute-start = (bf16[128,1024]{1,0:T(8,128)(2,1)}, bf16[128,1024]{1,0:T(8,128)(2,1)}, u32[]{:S(2)}, u32[]{:S(2)}) collective-permute-start(bf16[128,1024]{1,0:T(8,128)(2,1)} %get-tuple-element.191), channel_id=1, source_target_pairs={{0,2},{2,0},{4,6},{6,4},{1,3},{3,1},{5,7},{7,5},{8,10},{10,8},{12,... | collective-permute-start | bytes 786440 | tf_op jit(solution)/shard_map/ppermute | solution.py:114
  20.0 39.2 %collective-permute-start.1 = (bf16[128,1024]{1,0:T(8,128)(2,1)}, bf16[128,1024]{1,0:T(8,128)(2,1)}, u32[]{:S(2)}, u32[]{:S(2)}) collective-permute-start(bf16[128,1024]{1,0:T(8,128)(2,1)} %get-tuple-element.190), channel_id=1, source_target_pairs={{0,4},{2,6},{4,0},{6,2},{1,5},{3,7},{5,1},{7,3},{8,12},{10,14},{12... | collective-permute-start | bytes 786440 | tf_op jit(solution)/shard_map/ppermute | solution.py:114
  77.4 176.6 %all-gather.15.cloned.1.call-start = ((), (), s32[]{:S(2)}) async-start(), calls=%async_computation.8 | async-start | bytes 4718592 | tf_op jit(solution)/shard_map/all_gather | solution.py:53
  77.5 101.7 %collective-permute-start.9 = (bf16[4,128,3072]{2,1,0:T(8,128)(2,1)}, bf16[4,128,3072]{2,1,0:T(8,128)(2,1)}, u32[]{:S(2)}, u32[]{:S(2)}) collective-permute-start(bf16[4,128,3072]{2,1,0:T(8,128)(2,1)} %bitcast_dynamic-update-slice_fusion.8), channel_id=1, source_target_pairs={{0,2},{2,4},{4,6},{1,3},{3,5},{5,7},{8,10},{10,12},{12,14},{9,11},... | collective-permute-start | bytes 9437192 | tf_op jit(solution)/shard_map/ppermute | solution.py:131
  82.2 102.7 %collective-permute-start.10 = (bf16[4,128,3072]{2,1,0:T(8,128)(2,1)}, bf16[4,128,3072]{2,1,0:T(8,128)(2,1)}, u32[]{:S(2)}, u32[]{:S(2)}) collective-permute-start(bf16[4,128,3072]{2,1,0:T(8,128)(2,1)} %bitcast_dynamic-update-slice_fusion.8), channel_id=1, source_target_pairs={{2,0},{4,2},{6,4},{3,1},{5,3},{7,5},{10,8},{12,10},{14,12},{11,9},... | collective-permute-start | bytes 9437192 | tf_op jit(solution)/shard_map/ppermute | solution.py:132
  88.9 43.2 %collective-permute-start.7 = (bf16[4,128,1024]{2,1,0:T(8,128)(2,1)S(1)}, bf16[4,128,1024]{2,1,0:T(8,128)(2,1)}, u32[]{:S(2)}, u32[]{:S(2)}) collective-permute-start(bf16[4,128,1024]{2,1,0:T(8,128)(2,1)S(1)} %copy-done.29), channel_id=1, source_target_pairs={{0,16},{8,24},{16,0},{24,8},{1,17},{9,25},{17,1},{25,9},{2,18},{10... | collective-permute-start | bytes 3145736 | tf_op jit(solution)/shard_map/ppermute | solution.py:91
  90.4 44.0 %collective-permute-start.8 = (bf16[4,128,1024]{2,1,0:T(8,128)(2,1)S(1)}, bf16[4,128,1024]{2,1,0:T(8,128)(2,1)}, u32[]{:S(2)}, u32[]{:S(2)}) collective-permute-start(bf16[4,128,1024]{2,1,0:T(8,128)(2,1)S(1)} %copy-done.29), channel_id=1, source_target_pairs={{0,24},{8,16},{16,8},{24,0},{1,25},{9,17},{17,9},{25,1},{2,26},{10... | collective-permute-start | bytes 3145736 | tf_op jit(solution)/shard_map/ppermute | solution.py:91
  94.0 234.2 %reduce-scatter.5.cloned.1.call-start = ((), (), s32[]{:S(2)}) async-start(), calls=%async_computation.6 | async-start | bytes 4718592 | tf_op jit(solution)/shard_map/reduce_scatter | solution.py:57
  179.2 67.3 %collective-permute-start.11 = (bf16[4,128,3072]{2,1,0:T(8,128)(2,1)}, bf16[4,128,3072]{2,1,0:T(8,128)(2,1)}, u32[]{:S(2)}, u32[]{:S(2)}) collective-permute-start(bf16[4,128,3072]{2,1,0:T(8,128)(2,1)} %collective-permute-done.9), channel_id=1, source_target_pairs={{2,4},{4,6},{3,5},{5,7},{10,12},{12,14},{11,13},{13,15},{18,20},{2... | collective-permute-start | bytes 9437192 | tf_op jit(solution)/shard_map/ppermute | solution.py:131
  184.9 69.0 %collective-permute-start.12 = (bf16[4,128,3072]{2,1,0:T(8,128)(2,1)}, bf16[4,128,3072]{2,1,0:T(8,128)(2,1)}, u32[]{:S(2)}, u32[]{:S(2)}) collective-permute-start(bf16[4,128,3072]{2,1,0:T(8,128)(2,1)} %collective-permute-done.10), channel_id=1, source_target_pairs={{2,0},{4,2},{3,1},{5,3},{10,8},{12,10},{11,9},{13,11},{18,16},{20,... | collective-permute-start | bytes 9437192 | tf_op jit(solution)/shard_map/ppermute | solution.py:132
  253.9 164.4 %reduce-scatter.7.cloned.1.call-start = ((), (), s32[]{:S(2)}) async-start(), calls=%async_computation.11 | async-start | bytes 4718592 | tf_op jit(solution)/shard_map/reduce_scatter | solution.py:57
  258.6 186.2 %all-gather.17.cloned.1.call-start = ((), (), s32[]{:S(2)}) async-start(), calls=%async_computation.9 | async-start | bytes 4718592 | tf_op jit(solution)/shard_map/all_gather | solution.py:53
  258.6 70.7 %collective-permute-start.13 = (bf16[4,128,3072]{2,1,0:T(8,128)(2,1)}, bf16[4,128,3072]{2,1,0:T(8,128)(2,1)}, u32[]{:S(2)}, u32[]{:S(2)}) collective-permute-start(bf16[4,128,3072]{2,1,0:T(8,128)(2,1)} %collective-permute-done.11), channel_id=1, source_target_pairs={{4,6},{5,7},{12,14},{13,15},{20,22},{21,23},{28,30},{29,31}} | collective-permute-start | bytes 9437192 | tf_op jit(solution)/shard_map/ppermute | solution.py:131
  260.9 129.9 %collective-permute-start.14 = (bf16[4,128,3072]{2,1,0:T(8,128)(2,1)}, bf16[4,128,3072]{2,1,0:T(8,128)(2,1)}, u32[]{:S(2)}, u32[]{:S(2)}) collective-permute-start(bf16[4,128,3072]{2,1,0:T(8,128)(2,1)} %collective-permute-done.12), channel_id=1, source_target_pairs={{2,0},{3,1},{10,8},{11,9},{18,16},{19,17},{26,24},{27,25}} | collective-permute-start | bytes 9437192 | tf_op jit(solution)/shard_map/ppermute | solution.py:132
  393.7 116.2 %all-gather.21.cloned.1.call-start = ((), (), s32[]{:S(2)}) async-start(), calls=%async_computation.12 | async-start | bytes 4718592 | tf_op jit(solution)/shard_map/all_gather | solution.py:53
  423.4 209.7 %all-gather.19.cloned.1.call-start = ((), (), s32[]{:S(2)}) async-start(), calls=%async_computation.10 | async-start | bytes 4718592 | tf_op jit(solution)/shard_map/all_gather | solution.py:53
  487.1 49.7 %collective-permute-start.15 = (bf16[4,128,2048]{2,1,0:T(8,128)(2,1)}, bf16[4,128,2048]{2,1,0:T(8,128)(2,1)S(1)}, u32[]{:S(2)}, u32[]{:S(2)}) collective-permute-start(bf16[4,128,2048]{2,1,0:T(8,128)(2,1)} %dynamic-slice_bitcast_fusion.10), channel_id=1, source_target_pairs={{0,1},{1,0},{2,3},{3,2},{4,5},{5,4},{6,7},{7,6},{8,9},{9,8},{10,11... | collective-permute-start | bytes 6291464 | tf_op jit(solution)/shard_map/ppermute | solution.py:170
  576.8 178.8 %all-gather.23.cloned.1.call-start = ((), (), s32[]{:S(2)}) async-start(), calls=%async_computation.13 | async-start | bytes 4718592 | tf_op jit(solution)/shard_map/all_gather | solution.py:53
  610.1 49.8 %collective-permute-start.21 = (bf16[4,128,3072]{2,1,0:T(8,128)(2,1)}, bf16[4,128,3072]{2,1,0:T(8,128)(2,1)}, u32[]{:S(2)}, u32[]{:S(2)}) collective-permute-start(bf16[4,128,3072]{2,1,0:T(8,128)(2,1)} %pad_maximum_fusion.4), channel_id=1, source_target_pairs={{6,4},{7,5},{14,12},{15,13},{22,20},{23,21},{30,28},{31,29}} | collective-permute-start | bytes 9437192 | tf_op jit(solution)/shard_map/ppermute | solution.py:216
  624.9 104.4 %collective-permute-start.20 = (bf16[4,128,3072]{2,1,0:T(8,128)(2,1)}, bf16[4,128,3072]{2,1,0:T(8,128)(2,1)}, u32[]{:S(2)}, u32[]{:S(2)}) collective-permute-start(bf16[4,128,3072]{2,1,0:T(8,128)(2,1)} %pad_maximum_fusion.3), channel_id=1, source_target_pairs={{0,2},{1,3},{8,10},{9,11},{16,18},{17,19},{24,26},{25,27}} | collective-permute-start | bytes 9437192 | tf_op jit(solution)/shard_map/ppermute | solution.py:213
  633.0 292.1 %reduce-scatter.9.cloned.1.call-start = ((), (), s32[]{:S(2)}) async-start(), calls=%async_computation.14 | async-start | bytes 4718592 | tf_op jit(solution)/shard_map/reduce_scatter | solution.py:57
  735.1 121.2 %collective-permute-start.42 = (bf16[4,128,3072]{2,1,0:T(8,128)(2,1)}, bf16[4,128,3072]{2,1,0:T(8,128)(2,1)}, u32[]{:S(2)}, u32[]{:S(2)}) collective-permute-start(bf16[4,128,3072]{2,1,0:T(8,128)(2,1)} %add_convert_fusion.5), channel_id=1, source_target_pairs={{4,2},{6,4},{5,3},{7,5},{12,10},{14,12},{13,11},{15,13},{20,18},{2... | collective-permute-start | bytes 9437192 | tf_op jit(solution)/shard_map/ppermute | solution.py:216
  742.4 114.0 %collective-permute-start.41 = (bf16[4,128,3072]{2,1,0:T(8,128)(2,1)}, bf16[4,128,3072]{2,1,0:T(8,128)(2,1)}, u32[]{:S(2)}, u32[]{:S(2)}) collective-permute-start(bf16[4,128,3072]{2,1,0:T(8,128)(2,1)} %add_convert_fusion.6), channel_id=1, source_target_pairs={{0,2},{2,4},{1,3},{3,5},{8,10},{10,12},{9,11},{11,13},{16,18},{18,... | collective-permute-start | bytes 9437192 | tf_op jit(solution)/shard_map/ppermute | solution.py:213
  768.4 163.3 %reduce-scatter.11.cloned.1.call-start = ((), (), s32[]{:S(2)}) async-start(), calls=%async_computation.15 | async-start | bytes 4718592 | tf_op jit(solution)/shard_map/reduce_scatter | solution.py:57
  796.7 45.5 %collective-permute-start.28 = (bf16[512,1024]{1,0:T(8,128)(2,1)}, bf16[512,1024]{1,0:T(8,128)(2,1)}, u32[]{:S(2)}, u32[]{:S(2)}) collective-permute-start(bf16[512,1024]{1,0:T(8,128)(2,1)} %pad_maximum_fusion.16), channel_id=1, source_target_pairs={{0,16},{8,24},{16,0},{24,8},{1,17},{9,25},{17,1},{25,9},{2,18},{10... | collective-permute-start | bytes 3145736 | tf_op jit(solution)/shard_map/ppermute | solution.py:105
  798.6 43.6 %collective-permute-start.29 = (bf16[512,1024]{1,0:T(8,128)(2,1)}, bf16[512,1024]{1,0:T(8,128)(2,1)}, u32[]{:S(2)}, u32[]{:S(2)}) collective-permute-start(bf16[512,1024]{1,0:T(8,128)(2,1)} %pad_maximum_fusion.17), channel_id=1, source_target_pairs={{0,24},{8,16},{16,8},{24,0},{1,25},{9,17},{17,9},{25,1},{2,26},{10... | collective-permute-start | bytes 3145736 | tf_op jit(solution)/shard_map/ppermute | solution.py:105
  870.5 117.1 %collective-permute-start.48 = (bf16[4,128,3072]{2,1,0:T(8,128)(2,1)}, bf16[4,128,3072]{2,1,0:T(8,128)(2,1)}, u32[]{:S(2)}, u32[]{:S(2)}) collective-permute-start(bf16[4,128,3072]{2,1,0:T(8,128)(2,1)} %add_convert_fusion.3), channel_id=1, source_target_pairs={{2,0},{4,2},{6,4},{3,1},{5,3},{7,5},{10,8},{12,10},{14,12},{11,9},... | collective-permute-start | bytes 9437192 | tf_op jit(solution)/shard_map/ppermute | solution.py:216
  876.8 110.8 %collective-permute-start.47 = (bf16[4,128,3072]{2,1,0:T(8,128)(2,1)}, bf16[4,128,3072]{2,1,0:T(8,128)(2,1)}, u32[]{:S(2)}, u32[]{:S(2)}) collective-permute-start(bf16[4,128,3072]{2,1,0:T(8,128)(2,1)} %add_convert_fusion.4), channel_id=1, source_target_pairs={{0,2},{2,4},{4,6},{1,3},{3,5},{5,7},{8,10},{10,12},{12,14},{9,11},... | collective-permute-start | bytes 9437192 | tf_op jit(solution)/shard_map/ppermute | solution.py:213
  946.1 41.5 %collective-permute-start.46 = (bf16[128,1024]{1,0:T(8,128)(2,1)S(1)}, bf16[128,1024]{1,0:T(8,128)(2,1)S(1)}, u32[]{:S(2)}, u32[]{:S(2)}) collective-permute-start(bf16[128,1024]{1,0:T(8,128)(2,1)S(1)} %get-tuple-element.159), channel_id=1, source_target_pairs={{0,6},{2,4},{4,2},{6,0},{1,7},{3,5},{5,3},{7,1},{8,14},{10,12},{12... | collective-permute-start | bytes 786440 | tf_op jit(solution)/shard_map/ppermute | solution.py:114
  (154 other events, 3153.9 us)
Sparse Core Ops, SparseCore 0:
  11.7 69.3 all-gather.8
  83.2 76.6 all-gather.10
  161.8 40.2 all-gather.12
  203.9 36.5 all-gather.14
  254.0 74.1 reduce-scatter.4
  330.4 75.7 reduce-scatter.6
  408.6 36.1 all-gather.16
  447.2 36.5 all-gather.20
  576.9 45.6 all-gather.18
  633.1 75.6 all-gather.22
  768.5 82.3 reduce-scatter.8
  856.5 75.1 reduce-scatter.10

commit v7 on v5

--- a/solution.py
+++ b/solution.py
@@ -317,7 +317,7 @@
             part, attended[slot + 1] = lax.optimization_barrier((part, attended[slot + 1]))
         if slot == 0:
             part = hold(part, hops, 1)
-        branch.append(scatter_rows(part, SEQUENCE_ROWS))
+        branch.append(scatter_rows(part, SEQUENCE_ROWS) if slot == 0 else part)
     middle, norm_two, inverse_two, norm_two_all = [], [], [], []
     for slot in each:
         summed_branch = branch[slot]
@@ -327,7 +327,12 @@
         normed, inverse = normalize(middle[slot])
         norm_two.append(normed)
         inverse_two.append(inverse)
-        norm_two_all.append(gather_rows(normed.astype(low), PLANE_ROWS))
+        normed = normed.astype(low)
+        if slot + 1 < slots:
+            normed, part = lax.optimization_barrier((normed, branch[slot + 1]))
+        norm_two_all.append(gather_rows(normed, PLANE_ROWS))
+        if slot + 1 < slots:
+            branch[slot + 1] = scatter_rows(part, SEQUENCE_ROWS)
     ffn_w = assemble(ffn_block, hops)
     gate_up_w, down_w = ffn_w[:, : 2 * units], ffn_w[:, 2 * units :]
 

time: 1060 us -> 1050 us (level)
  local copies, waits for them, and re-layouts: 128 us -> 107 us
  waiting for transfers between devices: 446 us -> 460 us
    reduce_scatter x4, waiting for transfers between devices: 110 us -> 134 us  [scatter_rows(): lax.psum_scatter(values.astype(jnp.bfloat16), axes, scatter_dimension=0,...]
    ppermute x3, waiting for transfers between devices: 68.6 us -> 45 us  [relay_hops(): lax.ppermute(moving_down, 'context', [(i, i - 1) for i in range(1, n - st...]
    ppermute x3, waiting for transfers between devices: 42.6 us -> 26.2 us  [reduce_groups(): lax.ppermute(term(group ^ step), 'dp', route).astype(jnp.float32)]
    ppermute x3, waiting for transfers between devices: 0.01 us -> 10.8 us  [hop(): lax.ppermute(below.astype(jnp.bfloat16), 'context', [(i, i - 1) for i in...]
    unnamed x252 -> x230, local copies, waits for them, and re-layouts: 24.9 us -> 19.5 us
  transfers between devices with their start and end apart: 64 -> 64, of which waited for: 21 -> 33; matrix products, arithmetic and copies ran while one was open for 44% -> 43% of each run, Pallas kernels for 0% -> 0%
where the time goes in v7:
time: 1050 us; the launch traced here: 1040 us
  waiting for transfers between devices  460 us (44%)
  matrix products  246 us (23%)
  other arithmetic  127 us (12%)
  local copies, waits for them, and re-layouts  107 us (10%)
  starting transfers between devices  82.4 us (8%)
  between operations  16.8 us (2%)
    dot_general x24, matrix products, dot(): lax.dot_general(left, right, (dims, ((), ())), preferred_element_type=jnp...  206 us
    reduce_scatter x4, waiting for transfers between devices, scatter_rows(): lax.psum_scatter(values.astype(jnp.bfloat16), axes, scatter_dimension=0,...  134 us
    ppermute x3, waiting for transfers between devices, hop(): lax.ppermute(above.astype(jnp.bfloat16), 'context', [(i, i + 1) for i in...  74.5 us
    ppermute x3, waiting for transfers between devices, relay_hops(): lax.ppermute(moving_down, 'context', [(i, i - 1) for i in range(1, n - st...  45 us
    ppermute x3, waiting for transfers between devices, relay_hops(): lax.ppermute(moving_up, 'context', [(i, i + 1) for i in range(step - 1, n...  43.7 us
    ppermute x16, waiting for transfers between devices, scatter_plane(): other = lax.ppermute(send, 'dp', route)  41.5 us
    ppermute x12, waiting for transfers between devices, swap(): arrived.append(lax.ppermute(take(pieces, here ^ step), axis, route))  33.8 us
    ppermute x3, waiting for transfers between devices, gather_groups(): whole = put(whole, lax.ppermute(mine, 'dp', route), group ^ step)  30.3 us
  transfers between devices with their start and end apart: 64, of which 33 were waited for; matrix products, arithmetic and copies ran while one was open for 43% of the time, Pallas kernels for 0%

profile of v7, /device:TPU:0, one launch (start us, length us, event | category | flops | bytes accessed | tf_op | source)
XLA Modules:
  0.0 1039.3 jit_solution(4112027430464728911)
XLA Ops:
  57.3 13.9 %collective-permute-done.4 = bf16[128,3072]{1,0:T(8,128)(2,1)} collective-permute-done((bf16[128,3072]{1,0:T(8,128)(2,1)}, bf16[128,3072]{1,0:T(8,128)(2,1)}, u32[]{:S(2)}, u32[]{:S(2)}) %collective-permute-start.4) | collective-permute-done | bytes 786464 | tf_op jit(solution)/shard_map/ppermute | solution.py:114
  96.9 14.7 %collective-permute-done.6 = bf16[4,128,1024]{2,1,0:T(8,128)(2,1)} collective-permute-done((bf16[4,128,1024]{2,1,0:T(8,128)(2,1)S(1)}, bf16[4,128,1024]{2,1,0:T(8,128)(2,1)}, u32[]{:S(2)}, u32[]{:S(2)}) %collective-permute-start.6) | collective-permute-done | bytes 1048608 | tf_op jit(solution)/shard_map/ppermute | solution.py:91
  113.8 15.6 %collective-permute-done.7 = bf16[4,128,1024]{2,1,0:T(8,128)(2,1)} collective-permute-done((bf16[4,128,1024]{2,1,0:T(8,128)(2,1)S(1)}, bf16[4,128,1024]{2,1,0:T(8,128)(2,1)}, u32[]{:S(2)}, u32[]{:S(2)}) %collective-permute-start.7) | collective-permute-done | bytes 1048608 | tf_op jit(solution)/shard_map/ppermute | solution.py:91
  132.7 43.7 %collective-permute-done.9 = bf16[4,128,3072]{2,1,0:T(8,128)(2,1)} collective-permute-done((bf16[4,128,3072]{2,1,0:T(8,128)(2,1)}, bf16[4,128,3072]{2,1,0:T(8,128)(2,1)}, u32[]{:S(2)}, u32[]{:S(2)}) %collective-permute-start.9) | collective-permute-done | bytes 3145760 | tf_op jit(solution)/shard_map/ppermute | solution.py:131
  184.0 8.3 fusion.52
  207.7 9.4 fusion.175
  238.6 13.8 %collective-permute-done.12 = bf16[4,128,3072]{2,1,0:T(8,128)(2,1)} collective-permute-done((bf16[4,128,3072]{2,1,0:T(8,128)(2,1)}, bf16[4,128,3072]{2,1,0:T(8,128)(2,1)}, u32[]{:S(2)}, u32[]{:S(2)}) %collective-permute-start.12) | collective-permute-done | bytes 3145760 | tf_op jit(solution)/shard_map/ppermute | solution.py:132
  260.8 72.2 %reduce-scatter.5.cloned.1.call-done = bf16[128,2048]{1,0:T(8,128)(2,1)} async-done(((bf16[1024,2048]{1,0:T(8,128)(2,1)}), bf16[128,2048]{1,0:T(8,128)(2,1)}) %reduce-scatter.5.cloned.1.call-update) | async-done | bytes 524304 | tf_op jit(solution)/shard_map/reduce_scatter | solution.py:57
  334.2 27.5 %collective-permute-done.14 = bf16[4,128,3072]{2,1,0:T(8,128)(2,1)} collective-permute-done((bf16[4,128,3072]{2,1,0:T(8,128)(2,1)}, bf16[4,128,3072]{2,1,0:T(8,128)(2,1)}, u32[]{:S(2)}, u32[]{:S(2)}) %collective-permute-start.14) | collective-permute-done | bytes 3145760 | tf_op jit(solution)/shard_map/ppermute | solution.py:132
  388.0 10.3 all-gather.17.cloned.1.call-done
  398.3 13.4 %fusion.10 = f32[1024,2048]{0,1:T(8,128)S(1)} fusion(bf16[1024,2048]{1,0:T(8,128)(2,1)} %all-gather.17.cloned.1.call-done, bf16[2048,3072]{1,0:T(8,128)(2,1)} %bitcast.492), kind=kOutput, calls=%fused_computation.26 | convolution fusion | flops 8589934592 | bytes 20971520 | tf_op jit(solution)/shard_map/dot_general | solution.py:49
  411.7 9.2 multiply_convert_fusion.7
  422.3 11.6 %fusion.26 = bf16[1024,2048]{1,0:T(8,128)(2,1)S(1)} fusion(bf16[2048,3072]{1,0:T(8,128)(2,1)} %bitcast.494, bf16[1024,1024]{0,1:T(8,128)(2,1)S(1)} %get-tuple-element.118, bf16[1024,1024]{0,1:T(8,128)(2,1)S(1)} %get-tuple-element.117), kind=kOutput, calls=%fused_computation.60 | convolution fusion | flops 8600420352 | bytes 16777216 | tf_op jit(solution)/shard_map/dot_general | solution.py:49
  437.7 12.9 %reduce-scatter.7.cloned.1.call-done = bf16[128,2048]{1,0:T(8,128)(2,1)} async-done(((bf16[1024,2048]{1,0:T(8,128)(2,1)}), bf16[128,2048]{1,0:T(8,128)(2,1)}) %reduce-scatter.7.cloned.1.call-update) | async-done | bytes 524304 | tf_op jit(solution)/shard_map/reduce_scatter | solution.py:57
  462.3 14.1 %fusion.32 = f32[2048,2048]{1,0:T(8,128)} fusion(bf16[1024,2048]{1,0:T(8,128)(2,1)S(1)} %copy-done.94, bf16[1024,1024]{0,1:T(8,128)(2,1)S(1)} %copy-done.106, bf16[1024,1024]{0,1:T(8,128)(2,1)S(1)} %copy-done.104), kind=kOutput, calls=%fused_computation.75 | convolution fusion | flops 8598323200 | bytes 25165824 | tf_op jit(solution)/shard_map/dot_general | solution.py:49
  498.7 15.4 %fusion.6 = f32[1024,2048]{0,1:T(8,128)} fusion(bf16[1024,2048]{1,0:T(8,128)(2,1)} %all-gather.21.cloned.1.call-done, bf16[2048,3072]{1,0:T(8,128)(2,1)} %bitcast.495), kind=kOutput, calls=%fused_computation.22 | convolution fusion | flops 8589934592 | bytes 20971520 | tf_op jit(solution)/shard_map/dot_general | solution.py:49
  514.2 11.8 %multiply_convert_fusion.5 = (bf16[1024,1024]{0,1:T(8,128)(2,1)}, bf16[1024,1024]{0,1:T(8,128)(2,1)}, bf16[1024,1024]{0,1:T(8,128)(2,1)}) fusion(f32[1024,2048]{0,1:T(8,128)} %fusion.6, bf16[1024,2048]{1,0:T(8,128)(2,1)S(1)} %copy-done.91, bf16[2048,3072]{1,0:T(8,128)(2,1)} %bitcast.496), kind=kOutput, calls=%fused_computation.42 | convolution fusion | flops 4310695936 | bytes 23068672 | tf_op jit(solution)/shard_map/dot_general | solution.py:49
  526.0 12.2 %fusion.29 = bf16[1024,2048]{1,0:T(8,128)(2,1)} fusion(bf16[2048,3072]{1,0:T(8,128)(2,1)S(1)} %bitcast.501, bf16[1024,1024]{0,1:T(8,128)(2,1)} %get-tuple-element.116, bf16[1024,1024]{0,1:T(8,128)(2,1)} %get-tuple-element.115), kind=kOutput, calls=%fused_computation.61 | convolution fusion | flops 8600420352 | bytes 16777216 | tf_op jit(solution)/shard_map/dot_general | solution.py:49
  538.2 16.7 %add_convert_fusion = bf16[2048,2048]{1,0:T(8,128)(2,1)} fusion(f32[2048,2048]{1,0:T(8,128)} %fusion.32, bf16[1024,2048]{1,0:T(8,128)(2,1)} %all-gather.21.cloned.1.call-done, bf16[1024,1024]{0,1:T(8,128)(2,1)} %get-tuple-element.116, bf16[1024,1024]{0,1:T(8,128)(2,1)} %get-tuple-element.115), kind=kOutput, calls=%fused_computation.2 | convolution fusion | flops 8606711808 | bytes 33554432 | tf_op jit(solution)/shard_map/dot_general | solution.py:49
  554.9 10.1 add_convert_fusion.1
  574.5 10.5 %dynamic-slice_bitcast_fusion = (bf16[4,128,2048]{2,1,0:T(8,128)(2,1)}, bf16[4,128,2048]{2,1,0:T(8,128)(2,1)}, bf16[4,128,2048]{2,1,0:T(8,128)(2,1)}, bf16[4,128...) fusion(bf16[4,4,128,2048]{3,2,1,0:T(8,128)(2,1)} %bitcast.490, ...), kind=kLoop, calls=%fused_computation.86 | loop fusion | bytes 29360156 | tf_op jit(solution)/shard_map/jit(dynamic_index_in_dim)/squeeze | solution.py:202
  590.1 9.8 collective-permute-done.23
  644.6 8.7 fusion.131
  653.3 53.8 %collective-permute-done.20 = bf16[4,128,3072]{2,1,0:T(8,128)(2,1)} collective-permute-done((bf16[4,128,3072]{2,1,0:T(8,128)(2,1)}, bf16[4,128,3072]{2,1,0:T(8,128)(2,1)}, u32[]{:S(2)}, u32[]{:S(2)}) %collective-permute-start.20) | collective-permute-done | bytes 3145760 | tf_op jit(solution)/shard_map/ppermute | solution.py:213
  742.4 7.3 convolution_convert_fusion.2
  749.8 7.4 convolution_convert_fusion.5
  785.8 10.3 collective-permute-done.30
  824.8 48.7 %reduce-scatter.11.cloned.1.call-done = bf16[128,2048]{1,0:T(8,128)(2,1)} async-done(((bf16[1024,2048]{1,0:T(8,128)(2,1)}), bf16[128,2048]{1,0:T(8,128)(2,1)}) %reduce-scatter.11.cloned.1.call-update) | async-done | bytes 524304 | tf_op jit(solution)/shard_map/reduce_scatter | solution.py:57
  909.9 18.8 %collective-permute-done.42 = bf16[512,1024]{1,0:T(8,128)(2,1)} collective-permute-done((bf16[512,1024]{1,0:T(8,128)(2,1)}, bf16[512,1024]{1,0:T(8,128)(2,1)}, u32[]{:S(2)}, u32[]{:S(2)}) %collective-permute-start.42) | collective-permute-done | bytes 1048608 | tf_op jit(solution)/shard_map/ppermute | solution.py:105
  935.7 20.7 %collective-permute-done.44 = bf16[4,128,3072]{2,1,0:T(8,128)(2,1)} collective-permute-done((bf16[4,128,3072]{2,1,0:T(8,128)(2,1)}, bf16[4,128,3072]{2,1,0:T(8,128)(2,1)}, u32[]{:S(2)}, u32[]{:S(2)}) %collective-permute-start.44) | collective-permute-done | bytes 3145760 | tf_op jit(solution)/shard_map/ppermute | solution.py:213
  956.4 10.8 %collective-permute-done.45 = bf16[4,128,3072]{2,1,0:T(8,128)(2,1)} collective-permute-done((bf16[4,128,3072]{2,1,0:T(8,128)(2,1)}, bf16[4,128,3072]{2,1,0:T(8,128)(2,1)}, u32[]{:S(2)}, u32[]{:S(2)}) %collective-permute-start.45) | collective-permute-done | bytes 3145760 | tf_op jit(solution)/shard_map/ppermute | solution.py:216
  1001.3 16.1 %collective-permute-done.50 = bf16[128,3072]{1,0:T(8,128)(2,1)} collective-permute-done((bf16[128,3072]{1,0:T(8,128)(2,1)}, bf16[128,3072]{1,0:T(8,128)(2,1)}, u32[]{:S(2)}, u32[]{:S(2)}) %collective-permute-start.50) | collective-permute-done | bytes 786464 | tf_op jit(solution)/shard_map/ppermute | solution.py:114
  (588 shorter events, 442.8 us)
Async XLA Ops:
  7.2 176.8 %all-gather.9.cloned.1.call-start = ((), (), s32[]{:S(2)}) async-start(), calls=%async_computation.4 | async-start | bytes 4718592 | tf_op jit(solution)/shard_map/all_gather | solution.py:53
  11.5 180.8 %all-gather.11.cloned.1.call-start = ((), (), s32[]{:S(2)}) async-start(), calls=%async_computation.5 | async-start | bytes 4718592 | tf_op jit(solution)/shard_map/all_gather | solution.py:53
  13.9 242.3 %all-gather.13.cloned.1.call-start = ((), (), s32[]{:S(2)}) async-start(), calls=%async_computation.7 | async-start | bytes 4718592 | tf_op jit(solution)/shard_map/all_gather | solution.py:53
  16.8 32.3 %collective-permute-start = (bf16[128,1024]{1,0:T(8,128)(2,1)}, bf16[128,1024]{1,0:T(8,128)(2,1)}, u32[]{:S(2)}, u32[]{:S(2)}) collective-permute-start(bf16[128,1024]{1,0:T(8,128)(2,1)} %get-tuple-element.195), channel_id=1, source_target_pairs={{0,2},{2,0},{4,6},{6,4},{1,3},{3,1},{5,7},{7,5},{8,10},{10,8},{12,... | collective-permute-start | bytes 786440 | tf_op jit(solution)/shard_map/ppermute | solution.py:114
  19.9 32.0 %collective-permute-start.1 = (bf16[128,1024]{1,0:T(8,128)(2,1)}, bf16[128,1024]{1,0:T(8,128)(2,1)}, u32[]{:S(2)}, u32[]{:S(2)}) collective-permute-start(bf16[128,1024]{1,0:T(8,128)(2,1)} %get-tuple-element.194), channel_id=1, source_target_pairs={{0,4},{2,6},{4,0},{6,2},{1,5},{3,7},{5,1},{7,3},{8,12},{10,14},{12... | collective-permute-start | bytes 786440 | tf_op jit(solution)/shard_map/ppermute | solution.py:114
  35.9 35.3 %collective-permute-start.4 = (bf16[128,3072]{1,0:T(8,128)(2,1)}, bf16[128,3072]{1,0:T(8,128)(2,1)}, u32[]{:S(2)}, u32[]{:S(2)}) collective-permute-start(bf16[128,3072]{1,0:T(8,128)(2,1)} %bitcast.553), channel_id=1, source_target_pairs={{0,16},{8,24},{16,0},{24,8},{1,17},{9,25},{17,1},{25,9},{2,18},{10... | collective-permute-start | bytes 2359304 | tf_op jit(solution)/shard_map/ppermute | solution.py:114
  74.3 181.9 %all-gather.15.cloned.1.call-start = ((), (), s32[]{:S(2)}) async-start(), calls=%async_computation.8 | async-start | bytes 4718592 | tf_op jit(solution)/shard_map/all_gather | solution.py:53
  74.4 102.1 %collective-permute-start.9 = (bf16[4,128,3072]{2,1,0:T(8,128)(2,1)}, bf16[4,128,3072]{2,1,0:T(8,128)(2,1)}, u32[]{:S(2)}, u32[]{:S(2)}) collective-permute-start(bf16[4,128,3072]{2,1,0:T(8,128)(2,1)} %bitcast_dynamic-update-slice_fusion.8), channel_id=1, source_target_pairs={{0,2},{2,4},{4,6},{1,3},{3,5},{5,7},{8,10},{10,12},{12,14},{9,11},... | collective-permute-start | bytes 9437192 | tf_op jit(solution)/shard_map/ppermute | solution.py:131
  81.5 100.9 %collective-permute-start.10 = (bf16[4,128,3072]{2,1,0:T(8,128)(2,1)}, bf16[4,128,3072]{2,1,0:T(8,128)(2,1)}, u32[]{:S(2)}, u32[]{:S(2)}) collective-permute-start(bf16[4,128,3072]{2,1,0:T(8,128)(2,1)} %bitcast_dynamic-update-slice_fusion.8), channel_id=1, source_target_pairs={{2,0},{4,2},{6,4},{3,1},{5,3},{7,5},{10,8},{12,10},{14,12},{11,9},... | collective-permute-start | bytes 9437192 | tf_op jit(solution)/shard_map/ppermute | solution.py:132
  88.2 41.2 %collective-permute-start.7 = (bf16[4,128,1024]{2,1,0:T(8,128)(2,1)S(1)}, bf16[4,128,1024]{2,1,0:T(8,128)(2,1)}, u32[]{:S(2)}, u32[]{:S(2)}) collective-permute-start(bf16[4,128,1024]{2,1,0:T(8,128)(2,1)S(1)} %bitcast_dynamic-update-slice_fusion.11), channel_id=1, source_target_pairs={{0,16},{8,24},{16,0},{24,8},{1,17},{9,25},{17,1},{25,9},{2,18},{10... | collective-permute-start | bytes 3145736 | tf_op jit(solution)/shard_map/ppermute | solution.py:91
  89.7 42.0 %collective-permute-start.8 = (bf16[4,128,1024]{2,1,0:T(8,128)(2,1)S(1)}, bf16[4,128,1024]{2,1,0:T(8,128)(2,1)S(1)}, u32[]{:S(2)}, u32[]{:S(2)}) collective-permute-start(bf16[4,128,1024]{2,1,0:T(8,128)(2,1)S(1)} %bitcast_dynamic-update-slice_fusion.11), channel_id=1, source_target_pairs={{0,24},{8,16},{16,8},{24,0},{1,25},{9,17},{17,9},{25,1},{2,26},{10... | collective-permute-start | bytes 3145736 | tf_op jit(solution)/shard_map/ppermute | solution.py:91
  93.3 239.7 %reduce-scatter.5.cloned.1.call-start = ((), (), s32[]{:S(2)}) async-start(), calls=%async_computation.6 | async-start | bytes 4718592 | tf_op jit(solution)/shard_map/reduce_scatter | solution.py:57
  176.4 62.2 %collective-permute-start.11 = (bf16[4,128,3072]{2,1,0:T(8,128)(2,1)}, bf16[4,128,3072]{2,1,0:T(8,128)(2,1)}, u32[]{:S(2)}, u32[]{:S(2)}) collective-permute-start(bf16[4,128,3072]{2,1,0:T(8,128)(2,1)} %collective-permute-done.9), channel_id=1, source_target_pairs={{2,4},{4,6},{3,5},{5,7},{10,12},{12,14},{11,13},{13,15},{18,20},{2... | collective-permute-start | bytes 9437192 | tf_op jit(solution)/shard_map/ppermute | solution.py:131
  182.4 70.1 %collective-permute-start.12 = (bf16[4,128,3072]{2,1,0:T(8,128)(2,1)}, bf16[4,128,3072]{2,1,0:T(8,128)(2,1)}, u32[]{:S(2)}, u32[]{:S(2)}) collective-permute-start(bf16[4,128,3072]{2,1,0:T(8,128)(2,1)} %collective-permute-done.10), channel_id=1, source_target_pairs={{2,0},{4,2},{3,1},{5,3},{10,8},{12,10},{11,9},{13,11},{18,16},{20,... | collective-permute-start | bytes 9437192 | tf_op jit(solution)/shard_map/ppermute | solution.py:132
  252.5 145.8 %all-gather.17.cloned.1.call-start = ((), (), s32[]{:S(2)}) async-start(), calls=%async_computation.9 | async-start | bytes 4718592 | tf_op jit(solution)/shard_map/all_gather | solution.py:53
  252.6 81.6 %collective-permute-start.13 = (bf16[4,128,3072]{2,1,0:T(8,128)(2,1)}, bf16[4,128,3072]{2,1,0:T(8,128)(2,1)}, u32[]{:S(2)}, u32[]{:S(2)}) collective-permute-start(bf16[4,128,3072]{2,1,0:T(8,128)(2,1)} %collective-permute-done.11), channel_id=1, source_target_pairs={{4,6},{5,7},{12,14},{13,15},{20,22},{21,23},{28,30},{29,31}} | collective-permute-start | bytes 9437192 | tf_op jit(solution)/shard_map/ppermute | solution.py:131
  254.9 106.7 %collective-permute-start.14 = (bf16[4,128,3072]{2,1,0:T(8,128)(2,1)}, bf16[4,128,3072]{2,1,0:T(8,128)(2,1)}, u32[]{:S(2)}, u32[]{:S(2)}) collective-permute-start(bf16[4,128,3072]{2,1,0:T(8,128)(2,1)} %collective-permute-done.12), channel_id=1, source_target_pairs={{2,0},{3,1},{10,8},{11,9},{18,16},{19,17},{26,24},{27,25}} | collective-permute-start | bytes 9437192 | tf_op jit(solution)/shard_map/ppermute | solution.py:132
  363.2 87.3 %reduce-scatter.7.cloned.1.call-start = ((), (), s32[]{:S(2)}) async-start(), calls=%async_computation.11 | async-start | bytes 4718592 | tf_op jit(solution)/shard_map/reduce_scatter | solution.py:57
  373.5 125.2 %all-gather.21.cloned.1.call-start = ((), (), s32[]{:S(2)}) async-start(), calls=%async_computation.12 | async-start | bytes 4718592 | tf_op jit(solution)/shard_map/all_gather | solution.py:53
  455.6 162.4 %all-gather.19.cloned.1.call-start = ((), (), s32[]{:S(2)}) async-start(), calls=%async_computation.10 | async-start | bytes 4718592 | tf_op jit(solution)/shard_map/all_gather | solution.py:53
  492.6 214.5 %all-gather.23.cloned.1.call-start = ((), (), s32[]{:S(2)}) async-start(), calls=%async_computation.13 | async-start | bytes 4718592 | tf_op jit(solution)/shard_map/all_gather | solution.py:53
  603.4 103.7 %collective-permute-start.20 = (bf16[4,128,3072]{2,1,0:T(8,128)(2,1)}, bf16[4,128,3072]{2,1,0:T(8,128)(2,1)}, u32[]{:S(2)}, u32[]{:S(2)}) collective-permute-start(bf16[4,128,3072]{2,1,0:T(8,128)(2,1)} %pad_maximum_fusion.3), channel_id=1, source_target_pairs={{0,2},{1,3},{8,10},{9,11},{16,18},{17,19},{24,26},{25,27}} | collective-permute-start | bytes 9437192 | tf_op jit(solution)/shard_map/ppermute | solution.py:213
  612.0 210.7 %reduce-scatter.9.cloned.1.call-start = ((), (), s32[]{:S(2)}) async-start(), calls=%async_computation.14 | async-start | bytes 4718592 | tf_op jit(solution)/shard_map/reduce_scatter | solution.py:57
  615.6 91.6 %collective-permute-start.21 = (bf16[4,128,3072]{2,1,0:T(8,128)(2,1)}, bf16[4,128,3072]{2,1,0:T(8,128)(2,1)}, u32[]{:S(2)}, u32[]{:S(2)}) collective-permute-start(bf16[4,128,3072]{2,1,0:T(8,128)(2,1)} %pad_maximum_fusion.4), channel_id=1, source_target_pairs={{6,4},{7,5},{14,12},{15,13},{22,20},{23,21},{30,28},{31,29}} | collective-permute-start | bytes 9437192 | tf_op jit(solution)/shard_map/ppermute | solution.py:216
  707.2 166.3 %reduce-scatter.11.cloned.1.call-start = ((), (), s32[]{:S(2)}) async-start(), calls=%async_computation.15 | async-start | bytes 4718592 | tf_op jit(solution)/shard_map/reduce_scatter | solution.py:57
  717.3 160.9 %collective-permute-start.39 = (bf16[4,128,3072]{2,1,0:T(8,128)(2,1)}, bf16[4,128,3072]{2,1,0:T(8,128)(2,1)}, u32[]{:S(2)}, u32[]{:S(2)}) collective-permute-start(bf16[4,128,3072]{2,1,0:T(8,128)(2,1)} %add_convert_fusion.6), channel_id=1, source_target_pairs={{0,2},{2,4},{1,3},{3,5},{8,10},{10,12},{9,11},{11,13},{16,18},{18,... | collective-permute-start | bytes 9437192 | tf_op jit(solution)/shard_map/ppermute | solution.py:213
  728.2 150.0 %collective-permute-start.40 = (bf16[4,128,3072]{2,1,0:T(8,128)(2,1)}, bf16[4,128,3072]{2,1,0:T(8,128)(2,1)}, u32[]{:S(2)}, u32[]{:S(2)}) collective-permute-start(bf16[4,128,3072]{2,1,0:T(8,128)(2,1)} %add_convert_fusion.5), channel_id=1, source_target_pairs={{4,2},{6,4},{5,3},{7,5},{12,10},{14,12},{13,11},{15,13},{20,18},{2... | collective-permute-start | bytes 9437192 | tf_op jit(solution)/shard_map/ppermute | solution.py:216
  887.0 69.5 %collective-permute-start.44 = (bf16[4,128,3072]{2,1,0:T(8,128)(2,1)}, bf16[4,128,3072]{2,1,0:T(8,128)(2,1)}, u32[]{:S(2)}, u32[]{:S(2)}) collective-permute-start(bf16[4,128,3072]{2,1,0:T(8,128)(2,1)} %add_convert_fusion.4), channel_id=1, source_target_pairs={{0,2},{2,4},{4,6},{1,3},{3,5},{5,7},{8,10},{10,12},{12,14},{9,11},... | collective-permute-start | bytes 9437192 | tf_op jit(solution)/shard_map/ppermute | solution.py:213
  894.8 72.4 %collective-permute-start.45 = (bf16[4,128,3072]{2,1,0:T(8,128)(2,1)}, bf16[4,128,3072]{2,1,0:T(8,128)(2,1)}, u32[]{:S(2)}, u32[]{:S(2)}) collective-permute-start(bf16[4,128,3072]{2,1,0:T(8,128)(2,1)} %add_convert_fusion.3), channel_id=1, source_target_pairs={{2,0},{4,2},{6,4},{3,1},{5,3},{7,5},{10,8},{12,10},{14,12},{11,9},... | collective-permute-start | bytes 9437192 | tf_op jit(solution)/shard_map/ppermute | solution.py:216
  898.2 35.4 %collective-permute-start.38 = (f32[2,128,2048]{2,1,0:T(8,128)}, f32[2,128,2048]{2,1,0:T(8,128)}, u32[]{:S(2)}, u32[]{:S(2)}) collective-permute-start(f32[2,128,2048]{2,1,0:T(8,128)} %pad_maximum_fusion.9), channel_id=1, source_target_pairs={{0,1},{1,0},{2,3},{3,2},{4,5},{5,4},{6,7},{7,6},{8,9},{9,8},{10,11... | collective-permute-start | bytes 6291464 | tf_op jit(solution)/shard_map/ppermute | solution.py:68
  982.8 34.5 %collective-permute-start.50 = (bf16[128,3072]{1,0:T(8,128)(2,1)}, bf16[128,3072]{1,0:T(8,128)(2,1)}, u32[]{:S(2)}, u32[]{:S(2)}) collective-permute-start(bf16[128,3072]{1,0:T(8,128)(2,1)} %get-tuple-element.136), channel_id=1, source_target_pairs={{0,16},{8,24},{16,0},{24,8},{1,17},{9,25},{17,1},{25,9},{2,18},{10... | collective-permute-start | bytes 2359304 | tf_op jit(solution)/shard_map/ppermute | solution.py:114
  984.5 36.0 %collective-permute-start.51 = (bf16[128,3072]{1,0:T(8,128)(2,1)}, bf16[128,3072]{1,0:T(8,128)(2,1)}, u32[]{:S(2)}, u32[]{:S(2)}) collective-permute-start(bf16[128,3072]{1,0:T(8,128)(2,1)} %get-tuple-element.135), channel_id=1, source_target_pairs={{0,24},{8,16},{16,8},{24,0},{1,25},{9,17},{17,9},{25,1},{2,26},{10... | collective-permute-start | bytes 2359304 | tf_op jit(solution)/shard_map/ppermute | solution.py:114
  (146 other events, 2654.9 us)
Sparse Core Ops, SparseCore 0:
  11.6 69.2 all-gather.8
  83.1 77.3 all-gather.10
  162.3 40.2 all-gather.12
  204.3 36.5 all-gather.14
  252.6 80.3 reduce-scatter.4
  363.3 34.9 all-gather.16
  400.6 49.8 reduce-scatter.6
  455.8 42.9 all-gather.20
  500.3 47.0 all-gather.18
  612.1 73.2 all-gather.22
  707.3 94.7 reduce-scatter.8
  804.2 69.2 reduce-scatter.10
